TPU v7x, 128 devices: a whole 4x4x4 slice. The times are simulated.
128 devices in a mesh: ty: 8 (over z, core), tx: 16 (over x, y).
Axes of the slice: x: 4, y: 4, z: 4, core: 2. Of those that a mesh axis runs over, the one named last changes fastest.
Arguments:
- spectra: float32 [36, 36, 32, 2048], P(None, None, 'ty', 'tx'), may hold values from 0.05 to 2
- sea_mask: int32 [32, 2048], P('ty', 'tx'), may hold values from 0 to 1, as said below
- currents: float32 [2, 131072], P(None, ('ty', 'tx')), may hold values from -3.6 to 3.6
- sea_depth: float32 [131072], P(('ty', 'tx')), may hold values from 10 to 4000
- slopes: float32 [2, 131072], P(None, ('ty', 'tx')), may hold values from -0.018 to 0.018
- piece_offset: int32 [128, 128], replicated, may hold values from 0 to 1020, as said below
- piece_count: int32 [128, 128], replicated, may hold values from 0 to 4, as said below
Outputs:
- advanced: float32 [36, 36, 32, 2048], P(None, None, 'ty', 'tx')
Inputs may be any that keep to these rules, and one draw needn't show every extreme that they name: piece_count[o, w] is the number of sea points that ocean device o sends to wave tile w (both numbered latitude band major); in every draw some wave tile receives exactly 4 from every ocean device; the sea cells of tile w number the sum of column w. `piece_offset`: the pieces of one ocean device lie in order of w, do not intersect, and end within its 1024 rows. `sea_mask`: tile w has as many sea cells as the column sum of piece_count for w.
All inputs are finite; a program needn't handle non-finite values.
Results may differ from a plain program's by a relative error of at most 0.0003.
Values sent between devices are 32-bit elements; how exact they have to be, the bound alone decides.
No kernel may reach another device: no remote copies, remote signals or barrier semaphores. Data moves between devices by JAX's collectives and lax.ppermute only.
A program may use at most 192 MiB of HBM per device.

v0:
```python
import math

import jax
import jax.numpy as jnp
from jax import lax
from jax.sharding import PartitionSpec as P

SUBSTEPS = 2


gravity = 9.81
first_frequency = 0.0418
frequency_ratio = 1.1
time_step = 600.0
cell_metres = 13900.0
refraction_limit = 0.8
land_depth = 1000.0
product_limit = 20.0
group_width = 4


def with_halo(shard, sides, width, wrap):
    for axis, dim in sides:
        devices, length = (lax.axis_size(axis), shard.shape[dim])
        up = [(i, (i + 1) % devices) for i in range(devices if wrap else devices - 1)]
        down = [(j, i) for i, j in up]
        last = lax.slice_in_dim(shard, length - width, length, axis=dim)
        initial = lax.slice_in_dim(shard, 0, width, axis=dim)
        before = lax.ppermute(last, axis, up)
        after = lax.ppermute(initial, axis, down)
        shard = jnp.concatenate([before, shard, after], axis=dim)
    return shard


def frequencies(number):
    ordinal = jnp.arange(number, dtype=jnp.float32)
    return first_frequency * jnp.exp(ordinal * math.log(frequency_ratio))


def angles(number):
    heading = jnp.arange(number, dtype=jnp.float32) * (2.0 * math.pi / number)
    return (jnp.cos(heading)[:, None, None], jnp.sin(heading)[:, None, None])


def kinematics(fields, frequency):
    water_depth = jnp.where(fields[5] > 0.5, fields[2], land_depth)
    radian_freq = (2.0 * math.pi * frequency)[:, None, None]
    squared = radian_freq * radian_freq
    initial = squared / (gravity * jnp.sqrt(jnp.tanh(squared * water_depth / gravity)))
    hyperbolic = jnp.tanh(initial * water_depth)
    residue = gravity * initial * hyperbolic - squared
    derivative = gravity * hyperbolic + gravity * initial * water_depth * (
        1.0 - hyperbolic * hyperbolic
    )
    wavenumber = initial - residue / derivative
    product = jnp.minimum(wavenumber * water_depth, product_limit)
    double = jnp.sinh(2.0 * product)
    return (radian_freq / wavenumber * (0.5 + product / double), radian_freq / double)


def window(values, offset, length, along):
    return lax.slice_in_dim(values, offset, offset + length, axis=along)


def face_flux(action, courant, sea_layer, along):
    interior = action.shape[along] - 4
    faces = interior + 1
    action_back, action_here, action_next, action_ahead = [
        window(action, offset, faces, along) for offset in range(4)
    ]
    speed_back, speed_here, speed_next, speed_ahead = [
        window(courant, offset, faces, along) for offset in range(4)
    ]
    sea_here = window(sea_layer, 1, faces, along - 2)
    sea_next = window(sea_layer, 2, faces, along - 2)
    face_speed = (
        (9.0 * (speed_here + speed_next) - speed_back - speed_ahead) / 16.0 * sea_here * sea_next
    )
    upwind_left = 1.5 * action_here - 0.5 * action_back
    upwind_right = 1.5 * action_next - 0.5 * action_ahead
    through = (
        jnp.maximum(face_speed, 0.0) * upwind_left + jnp.minimum(face_speed, 0.0) * upwind_right
    )
    return window(through, 1, interior, along) - window(through, 0, interior, along)


def advance(row_action, column_action, row_fields, column_fields, frequency):
    dir_count = row_action.shape[1]
    cosine_dir, sine_dir = angles(dir_count)
    row_group, row_turning = kinematics(row_fields, frequency)
    column_group, column_turning = kinematics(column_fields, frequency)
    courant_scale = time_step / cell_metres
    speed_x = (
        (column_group[:, None] * cosine_dir + column_fields[0]) * column_fields[5] * courant_scale
    )
    speed_y = (row_group[:, None] * sine_dir + row_fields[1]) * row_fields[5] * courant_scale
    centre = row_action[:, :, 2:-2]
    shifted = (
        centre
        - face_flux(column_action, speed_x, column_fields[5], 3)
        - face_flux(row_action, speed_y, row_fields[5], 2)
    )
    inner_fields = row_fields[:, 2:-2]
    turning = row_turning[:, 2:-2]
    rotation = (
        jnp.clip(
            turning[:, None]
            * (sine_dir * inner_fields[3] - cosine_dir * inner_fields[4])
            * (time_step * dir_count / (2.0 * math.pi)),
            -refraction_limit,
            refraction_limit,
        )
        * inner_fields[5]
    )
    across = 0.5 * (rotation + jnp.roll(rotation, -1, 1))
    angular_flux = jnp.maximum(across, 0.0) * shifted + jnp.minimum(across, 0.0) * jnp.roll(
        shifted, -1, 1
    )
    return (shifted - angular_flux + jnp.roll(angular_flux, 1, 1)) * inner_fields[5]


def propagate(row_action, column_action, row_fields, column_fields):
    total_freqs = row_action.shape[0]
    groups = total_freqs // group_width
    frequency = frequencies(total_freqs).reshape(groups, group_width)
    row_blocks = row_action.reshape((groups, group_width) + row_action.shape[1:])
    column_blocks = column_action.reshape((groups, group_width) + column_action.shape[1:])

    def advance_block(members):
        return advance(members[0], members[1], row_fields, column_fields, members[2])

    result = lax.map(advance_block, (row_blocks, column_blocks, frequency))
    return result.reshape((total_freqs,) + result.shape[2:])


def extend(payload, margin):
    column_side = with_halo(payload, (("tx", 2),), margin, True)
    row_side = with_halo(payload, (("ty", 1),), margin, False)
    return (row_side, column_side)


def on_device(spectra, sea_mask, currents, sea_depth, slopes, piece_offset, piece_count):
    tile_rows, tile_columns = sea_mask.shape
    freq_count, dir_count = (spectra.shape[0], spectra.shape[1])
    bin_count = freq_count * dir_count
    across_y = lax.axis_size("ty")
    across_x = lax.axis_size("tx")
    devices = across_y * across_x
    capacity = tile_rows * tile_columns // devices
    myself = lax.axis_index("ty") * across_x + lax.axis_index("tx")
    ocean_count = sea_depth.shape[0]
    sending_offset = lax.dynamic_index_in_dim(piece_offset, myself, 0, keepdims=False)
    sending_count = lax.dynamic_index_in_dim(piece_count, myself, 0, keepdims=False)
    receiving_count = lax.dynamic_index_in_dim(piece_count, myself, 1, keepdims=False)
    slot_index = jnp.arange(capacity, dtype=jnp.int32)
    source_rows = jnp.clip(sending_offset[:, None] + slot_index[None, :], 0, ocean_count - 1)
    filled = slot_index[None, :] < sending_count[:, None]
    ocean_table = jnp.concatenate([currents, sea_depth[None], slopes], 0)
    packed = jnp.where(filled[None], jnp.take(ocean_table, source_rows, axis=1), 0.0)
    arrived = lax.all_to_all(packed, ("ty", "tx"), split_axis=1, concat_axis=1, tiled=True).reshape(
        5, devices * capacity
    )
    flat_mask = sea_mask.reshape(-1)
    sea_rank = jnp.cumsum(flat_mask) - 1
    ending = jnp.cumsum(receiving_count)
    passed = ending[None, :] <= sea_rank[:, None]
    source = jnp.minimum(jnp.sum(passed.astype(jnp.int32), 1), devices - 1)
    before = jnp.sum(jnp.where(passed, receiving_count[None, :], 0), 1)
    position = jnp.clip(source * capacity + sea_rank - before, 0, devices * capacity - 1)
    mask_layer = sea_mask.astype(jnp.float32)
    landed = jnp.take(arrived, position, axis=1) * flat_mask.astype(jnp.float32)[None]
    fields = jnp.concatenate([landed.reshape(5, tile_rows, tile_columns), mask_layer[None]], 0)
    action = spectra * mask_layer
    row_fields = fields
    column_fields = fields
    for substep in range(SUBSTEPS):
        flattened = action.reshape(bin_count, tile_rows, tile_columns)
        payload = jnp.concatenate([flattened, fields], 0) if substep == 0 else flattened
        row_side, column_side = extend(payload, 2)
        if substep == 0:
            row_fields = row_side[bin_count:]
            column_fields = column_side[bin_count:]
        action = propagate(
            row_side[:bin_count].reshape(freq_count, dir_count, tile_rows + 4, tile_columns),
            column_side[:bin_count].reshape(freq_count, dir_count, tile_rows, tile_columns + 4),
            row_fields,
            column_fields,
        )
    return action


def solution(mesh):
    return jax.shard_map(
        on_device,
        mesh=mesh,
        in_specs=(
            P(None, None, "ty", "tx"),
            P("ty", "tx"),
            P(None, ("ty", "tx")),
            P(("ty", "tx")),
            P(None, ("ty", "tx")),
            P(),
            P(),
        ),
        out_specs=P(None, None, "ty", "tx"),
        check_vma=False,
    )
```

profile of v0, /device:TPU:1, one launch (start us, length us, event | category | flops | bytes accessed | tf_op | source)
XLA Modules:
  0.0 247.4 jit_solution(17654790264013485907)
XLA Ops:
  4.3 11.5 %all-to-all-start = ((f32[5,128,4]{0,2,1:T(4,128)}), f32[5,128,4]{0,2,1:T(4,128)S(1)}, u32[]{:S(2)}, u32[]{:S(2)}) async-start(f32[5,128,4]{0,2,1:T(4,128)} %select_bitcast_fusion.4), calls=%async_computation | async-start | bytes 524288 | tf_op jit(solution)/shard_map/all_to_all | solution.py:160
  19.3 7.6 %all-to-all-done = f32[5,128,4]{0,2,1:T(4,128)S(1)} async-done(((f32[5,128,4]{0,2,1:T(4,128)}), f32[5,128,4]{0,2,1:T(4,128)S(1)}, u32[]{:S(2)}, u32[]{:S(2)}) %all-to-all-start) | async-done | bytes 10272 | tf_op jit(solution)/shard_map/all_to_all | solution.py:160
  28.0 3.2 %pad_maximum_fusion.7 = f32[1302,4,128]{2,1,0:T(4,128)S(1)} fusion(f32[1,4,128]{2,1,0:T(4,128)S(1)} %get-tuple-element.178, f32[5,4,128]{2,1,0:T(4,128)S(1)} %select_multiply_fusion, f32[1296,4,128]{2,1,0:T(4,128)S(1)} %bitcast.148), kind=kLoop, calls=%fused_computation.173 | loop fusion | flops 1333248 | bytes 5332992 | tf_op jit(solution)/shard_map/concatenate | solution.py:178
  33.3 3.1 %collective-permute-start = (f32[1302,2,128]{2,1,0:T(2,128)}, f32[1302,2,128]{2,1,0:T(2,128)}, u32[]{:S(2)}, u32[]{:S(2)}) collective-permute-start(f32[1302,2,128]{2,1,0:T(2,128)} %get-tuple-element.171), channel_id=1, source_target_pairs={{0,16},{16,32},{32,48},{48,64},{64,80},{80,96},{96,112},{1,17},{17... | collective-permute-start | bytes 3999752 | tf_op jit(solution)/shard_map/ppermute | solution.py:29
  38.8 3.1 %fusion.77 = (f32[1302,4,2]{2,1,0:T(4,128)}, f32[1302,4,2]{2,1,0:T(4,128)}) fusion(f32[1302,4,128]{2,1,0:T(4,128)S(1)} %pad_maximum_fusion.7), kind=kLoop, calls=%fused_computation.211 | loop fusion | bytes 166656 | tf_op jit(solution)/shard_map/slice | solution.py:27
  41.9 2.9 %copy.44 = f32[1302,4,2]{0,1,2:T(4,128)S(1)} copy(f32[1302,4,2]{2,1,0:T(4,128)} %get-tuple-element.169) | data formatting | bytes 83328 | tf_op jit(solution)/shard_map/slice | solution.py:27
  45.3 2.9 %copy.45 = f32[1302,4,2]{0,1,2:T(4,128)S(1)} copy(f32[1302,4,2]{2,1,0:T(4,128)} %get-tuple-element.170) | data formatting | bytes 83328 | tf_op jit(solution)/shard_map/slice | solution.py:28
  48.3 4.7 %collective-permute-start.3 = (f32[1302,4,2]{0,1,2:T(4,128)S(1)}, f32[1302,4,2]{0,1,2:T(4,128)S(1)}, u32[]{:S(2)}, u32[]{:S(2)}) collective-permute-start(f32[1302,4,2]{0,1,2:T(4,128)S(1)} %copy.45), channel_id=1, source_target_pairs={{1,0},{2,1},{3,2},{4,3},{5,4},{6,5},{7,6},{8,7},{9,8},{10,9},{11,1... | collective-permute-start | bytes 125000 | tf_op jit(solution)/shard_map/ppermute | solution.py:30
  53.0 2.6 %copy.46 = f32[1302,4,2]{2,1,0:T(4,128)} copy(f32[1302,4,2]{0,1,2:T(4,128)S(1)} %collective-permute-done.2) | data formatting | bytes 83328 | tf_op jit(solution)/shard_map/ppermute | solution.py:29
  55.6 2.6 %copy.47 = f32[1302,4,2]{2,1,0:T(4,128)} copy(f32[1302,4,2]{0,1,2:T(4,128)S(1)} %collective-permute-done.3) | data formatting | bytes 83328 | tf_op jit(solution)/shard_map/ppermute | solution.py:30
  60.8 11.0 %pad_maximum_fusion.1 = f32[1296,4,132]{2,1,0:T(4,128)} fusion(f32[1302,4,2]{2,1,0:T(4,128)S(1)} %copy-done.1, f32[1302,4,2]{2,1,0:T(4,128)S(1)} %copy-done, f32[1,4,128]{2,1,0:T(4,128)S(1)} %get-tuple-element.178, f32[5,4,128]{2,1,0:T(4,128)S(1)} %select_multiply_fusion, f32[1296,4,128]{2,1,0:T(4,128)S(1)} %bitcast.150), kind=kLoop, calls=%fused_computation.167 | loop fusion | flops 2737152 | bytes 5486976 | tf_op jit(solution)/shard_map/concatenate | solution.py:31
  71.8 5.3 %pad_maximum_fusion = f32[1302,8,128]{2,1,0:T(8,128)S(1)} fusion(f32[1302,2,128]{2,1,0:T(2,128)} %collective-permute-done.1, f32[1,4,128]{2,1,0:T(4,128)S(1)} %get-tuple-element.178, f32[5,4,128]{2,1,0:T(4,128)S(1)} %select_multiply_fusion, f32[1296,4,128]{2,1,0:T(4,128)S(1)} %bitcast.151, f32[1302,2,128]{2,1,0:T(2,128)} %collective-permute-done), kind=kLoop, calls=%fused_computation.166 | loop fusion | flops 5332992 | bytes 10665984 | tf_op jit(solution)/shard_map/concatenate | solution.py:31
  77.1 2.6 %slice.399 = f32[1296,8,128]{2,1,0:T(8,128)} slice(f32[1302,8,128]{2,1,0:T(8,128)S(1)} %pad_maximum_fusion), slice={[0:1296], [0:8], [0:128]} | slice | bytes 10616832 | tf_op jit(solution)/shard_map/slice | solution.py:184
  80.8 61.2 %while.20 = (s32[]{:T(128)}, f32[9,4,36,4,128]{4,3,2,1,0:T(4,128)S(1)}, f32[9,4,36,8,128]{4,3,2,1,0:T(8,128)}, f32[9,4]{1,0:T(8,128)S(1)}, f32[6,4,132]{2,1,0:T(...) while((s32[]{:T(128)}, f32[9,4,36,4,128]{4,3,2,1,0:T(4,128)S(1)}, ...), condition=%wide.region_6.7_spmd, body=%wide.region_5.6_spmd.sunk | while | flops 5835106 | bytes 15313573 | solution.py:132
  144.2 3.8 %collective-permute-start.4 = (f32[1296,2,128]{2,1,0:T(2,128)}, f32[1296,2,128]{2,1,0:T(2,128)}, u32[]{:S(2)}, u32[]{:S(2)}) collective-permute-start(f32[1296,2,128]{2,1,0:T(2,128)} %get-tuple-element.175), channel_id=1, source_target_pairs={{0,16},{16,32},{32,48},{48,64},{64,80},{80,96},{96,112},{1,17},{17... | collective-permute-start | bytes 3981320 | tf_op jit(solution)/shard_map/ppermute | solution.py:29
  150.2 3.2 %fusion.79 = (f32[1296,4,2]{2,1,0:T(4,128)}, f32[1296,4,2]{2,1,0:T(4,128)}) fusion(f32[1296,4,128]{2,1,0:T(4,128)S(1)} %bitcast.147), kind=kLoop, calls=%fused_computation.213 | loop fusion | bytes 165888 | tf_op jit(solution)/shard_map/slice | solution.py:27
  153.4 2.9 %copy.48 = f32[1296,4,2]{0,1,2:T(4,128)S(1)} copy(f32[1296,4,2]{2,1,0:T(4,128)} %get-tuple-element.173) | data formatting | bytes 82944 | tf_op jit(solution)/shard_map/slice | solution.py:27
  156.4 3.0 %copy.49 = f32[1296,4,2]{0,1,2:T(4,128)S(1)} copy(f32[1296,4,2]{2,1,0:T(4,128)} %get-tuple-element.174) | data formatting | bytes 82944 | tf_op jit(solution)/shard_map/slice | solution.py:28
  159.3 4.8 %collective-permute-start.7 = (f32[1296,4,2]{0,1,2:T(4,128)S(1)}, f32[1296,4,2]{0,1,2:T(4,128)S(1)}, u32[]{:S(2)}, u32[]{:S(2)}) collective-permute-start(f32[1296,4,2]{0,1,2:T(4,128)S(1)} %copy.49), channel_id=1, source_target_pairs={{1,0},{2,1},{3,2},{4,3},{5,4},{6,5},{7,6},{8,7},{9,8},{10,9},{11,1... | collective-permute-start | bytes 124424 | tf_op jit(solution)/shard_map/ppermute | solution.py:30
  164.2 2.5 %copy.52 = f32[1296,4,2]{2,1,0:T(4,128)} copy(f32[1296,4,2]{0,1,2:T(4,128)S(1)} %collective-permute-done.6) | data formatting | bytes 82944 | tf_op jit(solution)/shard_map/concatenate | solution.py:31
  166.7 2.5 %copy.53 = f32[1296,4,2]{2,1,0:T(4,128)} copy(f32[1296,4,2]{0,1,2:T(4,128)S(1)} %collective-permute-done.7) | data formatting | bytes 82944 | tf_op jit(solution)/shard_map/concatenate | solution.py:31
  169.3 9.1 %pad_maximum_fusion.6 = f32[9,4,36,4,132]{4,3,2,1,0:T(4,128)} fusion(f32[9,4,36,4,2]{4,3,2,1,0:T(4,128)} %bitcast.156, f32[9,4,36,4,128]{4,3,2,1,0:T(4,128)S(1)} %get-tuple-element.79, f32[9,4,36,4,2]{4,3,2,1,0:T(4,128)} %bitcast.155), kind=kLoop, calls=%fused_computation.172 | loop fusion | flops 1368576 | bytes 5474304 | tf_op jit(solution)/shard_map/concatenate | solution.py:31
  178.4 5.8 %pad_maximum_fusion.5 = f32[9,4,36,8,128]{4,3,2,1,0:T(8,128)} fusion(f32[9,4,36,2,128]{4,3,2,1,0:T(2,128)} %bitcast.51, f32[9,4,36,4,128]{4,3,2,1,0:T(4,128)S(1)} %get-tuple-element.79, f32[9,4,36,2,128]{4,3,2,1,0:T(2,128)} %bitcast.50), kind=kLoop, calls=%fused_computation.171 | loop fusion | flops 2654208 | bytes 10616832 | tf_op jit(solution)/shard_map/concatenate | solution.py:31
  184.6 61.2 %while.21 = (s32[]{:T(128)}, f32[9,4,36,4,128]{4,3,2,1,0:T(4,128)S(1)}, f32[9,4,36,8,128]{4,3,2,1,0:T(8,128)}, f32[9,4]{1,0:T(8,128)S(1)}, f32[6,4,132]{2,1,0:T(...) while((s32[]{:T(128)}, f32[9,4,36,4,128]{4,3,2,1,0:T(4,128)S(1)}, ...), condition=%wide.region_8.9_spmd, body=%wide.region_7.8_spmd.sunk | while | flops 5835106 | bytes 15313573 | solution.py:132
  (581 shorter events, 143.1 us)
Async XLA Ops:
  0.0 15.7 %copy-start.3 = (s32[128,128]{1,0:T(8,128)S(1)}, s32[128,128]{1,0:T(8,128)}, u32[]{:S(2)}) copy-start(s32[128,128]{1,0:T(8,128)} %param.17) | copy-start | bytes 196612
  0.0 15.9 %copy-start.4 = (s32[4,128]{1,0:T(4,128)S(1)}, s32[4,128]{1,0:T(4,128)}, u32[]{:S(2)}) copy-start(s32[4,128]{1,0:T(4,128)} %param.12) | copy-start | bytes 6148
  4.3 22.6 %all-to-all-start = ((f32[5,128,4]{0,2,1:T(4,128)}), f32[5,128,4]{0,2,1:T(4,128)S(1)}, u32[]{:S(2)}, u32[]{:S(2)}) async-start(f32[5,128,4]{0,2,1:T(4,128)} %select_bitcast_fusion.4), calls=%async_computation | async-start | bytes 524288 | tf_op jit(solution)/shard_map/all_to_all | solution.py:160
  33.3 38.4 %collective-permute-start = (f32[1302,2,128]{2,1,0:T(2,128)}, f32[1302,2,128]{2,1,0:T(2,128)}, u32[]{:S(2)}, u32[]{:S(2)}) collective-permute-start(f32[1302,2,128]{2,1,0:T(2,128)} %get-tuple-element.171), channel_id=1, source_target_pairs={{0,16},{16,32},{32,48},{48,64},{64,80},{80,96},{96,112},{1,17},{17... | collective-permute-start | bytes 3999752 | tf_op jit(solution)/shard_map/ppermute | solution.py:29
  36.5 35.3 %collective-permute-start.1 = (f32[1302,2,128]{2,1,0:T(2,128)}, f32[1302,2,128]{2,1,0:T(2,128)}, u32[]{:S(2)}, u32[]{:S(2)}) collective-permute-start(f32[1302,2,128]{2,1,0:T(2,128)} %get-tuple-element.172), channel_id=1, source_target_pairs={{16,0},{32,16},{48,32},{64,48},{80,64},{96,80},{112,96},{17,1},{33... | collective-permute-start | bytes 3999752 | tf_op jit(solution)/shard_map/ppermute | solution.py:30
  44.9 8.1 %collective-permute-start.2 = (f32[1302,4,2]{0,1,2:T(4,128)S(1)}, f32[1302,4,2]{0,1,2:T(4,128)S(1)}, u32[]{:S(2)}, u32[]{:S(2)}) collective-permute-start(f32[1302,4,2]{0,1,2:T(4,128)S(1)} %copy.44), channel_id=1, source_target_pairs={{0,1},{1,2},{2,3},{3,4},{4,5},{5,6},{6,7},{7,8},{8,9},{9,10},{10,1... | collective-permute-start | bytes 125000 | tf_op jit(solution)/shard_map/ppermute | solution.py:29
  48.3 7.3 %collective-permute-start.3 = (f32[1302,4,2]{0,1,2:T(4,128)S(1)}, f32[1302,4,2]{0,1,2:T(4,128)S(1)}, u32[]{:S(2)}, u32[]{:S(2)}) collective-permute-start(f32[1302,4,2]{0,1,2:T(4,128)S(1)} %copy.45), channel_id=1, source_target_pairs={{1,0},{2,1},{3,2},{4,3},{5,4},{6,5},{7,6},{8,7},{9,8},{10,9},{11,1... | collective-permute-start | bytes 125000 | tf_op jit(solution)/shard_map/ppermute | solution.py:30
  58.2 1.8 copy-start
  58.2 2.6 %copy-start.1 = (f32[1302,4,2]{2,1,0:T(4,128)S(1)}, f32[1302,4,2]{2,1,0:T(4,128)}, u32[]{:S(2)}) copy-start(f32[1302,4,2]{2,1,0:T(4,128)} %copy.47) | copy-start | bytes 124996
  144.2 34.1 %collective-permute-start.4 = (f32[1296,2,128]{2,1,0:T(2,128)}, f32[1296,2,128]{2,1,0:T(2,128)}, u32[]{:S(2)}, u32[]{:S(2)}) collective-permute-start(f32[1296,2,128]{2,1,0:T(2,128)} %get-tuple-element.175), channel_id=1, source_target_pairs={{0,16},{16,32},{32,48},{48,64},{64,80},{80,96},{96,112},{1,17},{17... | collective-permute-start | bytes 3981320 | tf_op jit(solution)/shard_map/ppermute | solution.py:29
  148.0 30.3 %collective-permute-start.5 = (f32[1296,2,128]{2,1,0:T(2,128)}, f32[1296,2,128]{2,1,0:T(2,128)}, u32[]{:S(2)}, u32[]{:S(2)}) collective-permute-start(f32[1296,2,128]{2,1,0:T(2,128)} %get-tuple-element.176), channel_id=1, source_target_pairs={{16,0},{32,16},{48,32},{64,48},{80,64},{96,80},{112,96},{17,1},{33... | collective-permute-start | bytes 3981320 | tf_op jit(solution)/shard_map/ppermute | solution.py:30
  156.3 7.9 %collective-permute-start.6 = (f32[1296,4,2]{0,1,2:T(4,128)S(1)}, f32[1296,4,2]{0,1,2:T(4,128)S(1)}, u32[]{:S(2)}, u32[]{:S(2)}) collective-permute-start(f32[1296,4,2]{0,1,2:T(4,128)S(1)} %copy.48), channel_id=1, source_target_pairs={{0,1},{1,2},{2,3},{3,4},{4,5},{5,6},{6,7},{7,8},{8,9},{9,10},{10,1... | collective-permute-start | bytes 124424 | tf_op jit(solution)/shard_map/ppermute | solution.py:29
  159.3 7.4 %collective-permute-start.7 = (f32[1296,4,2]{0,1,2:T(4,128)S(1)}, f32[1296,4,2]{0,1,2:T(4,128)S(1)}, u32[]{:S(2)}, u32[]{:S(2)}) collective-permute-start(f32[1296,4,2]{0,1,2:T(4,128)S(1)} %copy.49), channel_id=1, source_target_pairs={{1,0},{2,1},{3,2},{4,3},{5,4},{6,5},{7,6},{8,7},{9,8},{10,9},{11,1... | collective-permute-start | bytes 124424 | tf_op jit(solution)/shard_map/ppermute | solution.py:30
  245.9 1.5 copy-start.2
where the time goes:
time: 250 us; the launch traced here: 247 us
  other arithmetic  118 us (47%)
  local copies, waits for them, and re-layouts  85.5 us (34%)
  starting transfers between devices  32.9 us (13%)
  waiting for transfers between devices  7.62 us (3%)
  loops' own time  3.26 us (1%)
    add x36, other arithmetic, face_flux(): jnp.maximum(face_speed, 0.0) * upwind_left  44.1 us
    squeeze x36, local copies, waits for them, and re-layouts, propagate(): result = lax.map(advance_block, (row_blocks, column_blocks, frequency))  41.1 us
    concatenate x4, other arithmetic, with_halo(): shard = jnp.concatenate([before, shard, after], axis=dim)  31.2 us
    slice x6, local copies, waits for them, and re-layouts, with_halo(): last = lax.slice_in_dim(shard, length - width, length, axis=dim)  16.5 us
    ppermute x4, starting transfers between devices, with_halo(): after = lax.ppermute(initial, axis, down)  13.9 us
    all_to_all x1, starting transfers between devices, on_device(): lax.all_to_all(packed, ('ty', 'tx'), split_axis=1, concat_axis=1, tiled=T...  11.5 us
    all_to_all x1, waiting for transfers between devices, on_device(): lax.all_to_all(packed, ('ty', 'tx'), split_axis=1, concat_axis=1, tiled=T...  7.6 us
    ppermute x4, starting transfers between devices, with_halo(): before = lax.ppermute(last, axis, up)  7.45 us
  transfers between devices with their start and end apart: 9, of which 1 were waited for; matrix products, arithmetic and copies ran while one was open for 21% of the time, Pallas kernels for 0%

commit v1 on v0

v1 whole, which is shorter than its diff:
```python
import functools
import math

import jax
import jax.numpy as jnp
import numpy as np
from jax import lax
from jax.experimental import pallas as pl
from jax.experimental.pallas import tpu as pltpu
from jax.sharding import PartitionSpec as P

NF, ND = 36, 36
BINS = NF * ND
ROWS = BINS + 8
GROUPS = NF // 4
STARTS = (0, 8, 16, 24, 28)

gravity = 9.81
first_frequency = 0.0418
frequency_ratio = 1.1
time_step = 600.0
cell_metres = 13900.0
refraction_limit = 0.8
land_depth = 1000.0
product_limit = 20.0
courant_scale = time_step / cell_metres
turn_scale = time_step * ND / (2.0 * math.pi)

f32, bf16, i32 = jnp.float32, jnp.bfloat16, jnp.int32
HEADING = np.arange(48) % ND * (2.0 * math.pi / ND)
COSINE = np.broadcast_to(np.cos(HEADING)[:, None], (48, 128)).astype(np.float32)
SINE = np.broadcast_to(np.sin(HEADING)[:, None], (48, 128)).astype(np.float32)
SIGMA = (2.0 * math.pi * first_frequency * frequency_ratio ** np.arange(64)).astype(np.float32)
SIGMA_ROWS = np.broadcast_to(SIGMA[:NF, None], (NF, 128)).astype(np.float32)
SIGMA_PACKED = np.where(
    np.arange(16)[:, None] < GROUPS, SIGMA[np.minimum(4 * np.arange(16)[:, None] + np.arange(128)[None, :] // 32, 35)], 1.0
).astype(np.float32)


def roll(x, shift, axis=1):
    size = x.shape[axis]
    if isinstance(shift, int):
        shift %= size
        return x if shift == 0 else pltpu.roll(x, shift, axis)
    return pltpu.roll(x, shift, axis)


def lanes(shape=(8, 128)):
    return lax.broadcasted_iota(i32, shape, len(shape) - 1)


def split3(x):
    high = x.astype(bf16)
    rest = x - high.astype(f32)
    middle = rest.astype(bf16)
    low = (rest - middle.astype(f32)).astype(bf16)
    return jnp.concatenate([high, middle, low], 0)


def dot(a, b):
    return jnp.dot(a, b, preferred_element_type=f32)


def parity():
    return lax.rem(lax.axis_index("ty"), 2)


def planes_kernel(spectra, sea, na, nb, edges):
    flip = parity()
    lane = lanes()
    mask = sea[...].astype(f32)
    for ref in (na, nb):
        for part in range(2):
            ref[part, pl.ds(BINS, 8), :] = jnp.concatenate([mask, jnp.zeros((4, 128), f32)], 0)
    edges[GROUPS, pl.ds(0, 8), :] = jnp.concatenate([mask, jnp.zeros((4, 128), f32)], 0)
    for r in range(8, 40, 8):
        edges[GROUPS, pl.ds(r, 8), :] = jnp.zeros((8, 128), f32)
    row_mask = [jnp.broadcast_to(jnp.where(flip == 1, mask[3 - j : 4 - j], mask[j : j + 1]), (8, 128)) for j in range(4)]
    source = [jnp.where(flip == 1, 3 - j, j) for j in range(4)]

    def group(g, carry):
        for b, start in enumerate(STARTS):
            packed = jnp.zeros((8, 128), f32)
            for q in range(4):
                base = (4 * g + q) * ND + start
                for j in range(4):
                    value = spectra[pl.ds(4 * base + source[j], 8, stride=4), :] * row_mask[j]
                    (na if j < 2 else nb)[j % 2, pl.ds(base, 8), :] = value
                    at = 32 * q + 8 * j
                    packed = jnp.where((lane >= at) & (lane < at + 8), roll(value, at + 4), packed)
            edges[g, pl.ds(8 * b, 8), :] = packed
        return carry

    lax.fori_loop(0, GROUPS, group, 0)


def pieces_kernel(currents, depth, slopes, offset, count, out, rows):
    me = lax.axis_index("ty") * 16 + lax.axis_index("tx")
    table = jnp.concatenate([currents[...], depth[...], slopes[...], jnp.zeros((3, 1024), f32)], 0)
    shifted = jnp.concatenate([roll(table, -s) for s in range(4)], 0)
    wanted = offset[pl.ds(me, 1), :]
    number = count[pl.ds(me, 1), :]
    chosen = (lax.broadcasted_iota(i32, (1024, 128), 0) == wanted).astype(f32).astype(bf16)
    picked = dot(split3(shifted), chosen)
    picked = picked[:32] + picked[32:64] + picked[64:]
    lane = lanes()
    for s in range(4):
        own = jnp.where(number > s, picked[8 * s : 8 * s + 8], 0.0)
        up, down = roll(own, -16), roll(own, 16)
        left = jnp.where(lane % 16 == 0, roll(own, -15), roll(own, 1))
        right = jnp.where(lane % 16 == 15, roll(own, 15), roll(own, -1))
        rows[pl.ds(16 * s, 16), :] = jnp.concatenate(
            [own[:5], up[1:3], down[1:3], left[0:1], left[2:3], right[0:1], right[2:3], jnp.zeros((3, 128), f32)], 0
        )
    rows[pl.ds(64, 64), :] = jnp.zeros((64, 128), f32)
    out[...] = jnp.transpose(rows[...])


def kinematics(water_depth, sigma):
    squared = sigma * sigma
    initial = squared / (gravity * jnp.sqrt(jnp.tanh(squared * water_depth / gravity)))
    hyperbolic = jnp.tanh(initial * water_depth)
    residue = gravity * initial * hyperbolic - squared
    derivative = gravity * hyperbolic + gravity * initial * water_depth * (1.0 - hyperbolic * hyperbolic)
    wavenumber = initial - residue / derivative
    product = jnp.minimum(wavenumber * water_depth, product_limit)
    growth = jnp.exp(2.0 * product)
    double = 0.5 * (growth - 1.0 / growth)
    return sigma / wavenumber * (0.5 + product / double), sigma / double


def pack_edges(rows):
    lane = lanes()
    total = jnp.zeros((8, 128), f32)
    for j, row in enumerate(rows):
        moved = roll(jnp.broadcast_to(row, (8, 128)), 8 * j + 4)
        total = jnp.where((lane >= 8 * j) & (lane < 8 * j + 8), moved, total)
    total = total + roll(total, 32)
    return total + roll(total, 64)


def faces(x, mask, axis):
    ahead = roll(x, -1, axis)
    value = (9.0 * (x + ahead) - roll(x, 1, axis) - roll(x, -2, axis)) * (1.5 / 16.0)
    return value * (mask * roll(mask, -1, axis))


def fields_kernel(
    arrived, count, sea, chip_in, z_in, left_in, right_in, sigma_rows, sigma_packed,
    cgx, cgy, tx, ty, ux, vy, water, edge_cg, edge_u,
):
    flip = parity()
    row, column = lax.axis_index("ty"), lax.axis_index("tx")
    up, down = row * 16 + column + 16, row * 16 + column - 16
    chip = jnp.where(flip == 1, down, up)
    beyond = jnp.where(flip == 1, up, down)
    left = row * 16 + lax.rem(column + 15, 16)
    right = row * 16 + lax.rem(column + 1, 16)
    tile = (row * 16 + column, chip, beyond, left, right)
    lane128 = lanes((128, 128))
    sub128 = lax.broadcasted_iota(i32, (128, 128), 0)
    select = jnp.zeros((128, 128), f32)
    for t in range(5):
        select = jnp.where((lane128 == t) & (sub128 == tile[t]), 1.0, select)
    columns = dot(count[...].astype(f32).astype(bf16), select.astype(bf16))
    below = (lane128 < sub128).astype(f32).astype(bf16)
    first = dot(below, columns.astype(bf16))

    masks = [
        sea[...].astype(f32),
        chip_in[0, pl.ds(BINS, 4), :],
        z_in[0, pl.ds(BINS, 4), :],
        left_in[GROUPS, pl.ds(0, 4), :],
        right_in[GROUPS, pl.ds(0, 4), :],
    ]
    stacked = jnp.concatenate(masks + [jnp.zeros((4, 128), f32)], 0)
    upto = (sub128 <= lane128).astype(f32).astype(bf16)
    prefix = dot(stacked.astype(bf16), upto)
    ranks = []
    for t in range(5):
        before = jnp.zeros((1, 1), f32)
        for r in range(4):
            line = prefix[4 * t + r : 4 * t + r + 1]
            ranks.append(jnp.where(masks[t][r : r + 1] > 0.5, line - 1.0 + before, -2.0))
            before = before + line[:, 127:128]

    def flipped(t, j, table):
        return jnp.where(flip == 1, table[4 * t + 3 - j], table[4 * t + j])

    mask_rows = [masks[t][r : r + 1] for t in range(5) for r in range(4)]
    own_rank = [flipped(0, j, ranks) for j in range(4)]
    own_mask = [flipped(0, j, mask_rows) for j in range(4)]
    chip_rank = [flipped(1, j, ranks) for j in range(2)]
    chip_mask = [flipped(1, j, mask_rows) for j in range(2)]
    z_rank = [flipped(2, 3 - j, ranks) for j in range(2)]
    z_mask = [flipped(2, 3 - j, mask_rows) for j in range(2)]
    left_rank = pack_edges([flipped(3, j, ranks) for j in range(4)])[0:1]
    right_rank = pack_edges([flipped(4, j, ranks) for j in range(4)])[0:1]
    left_mask = pack_edges([flipped(3, j, mask_rows) for j in range(4)])
    right_mask = pack_edges([flipped(4, j, mask_rows) for j in range(4)])

    turned = jnp.transpose(arrived[...])
    values = split3(jnp.concatenate([turned[16 * s : 16 * s + 16] for s in range(4)], 1))

    keys = []
    for t in range(5):
        number, start = columns[:, t : t + 1], first[:, t : t + 1]
        keys.append(
            jnp.concatenate([jnp.where(number > s, start + s, -1.0) for s in range(4)], 0)
        )

    def place(t, rank):
        chosen = (keys[t] == rank).astype(f32).astype(bf16)
        found = dot(values, chosen)
        return found[:16] + found[16:32] + found[32:]

    own = [place(0, own_rank[j]) for j in range(4)]
    near_chip = [place(1, chip_rank[j]) for j in range(2)]
    near_z = [place(2, z_rank[j]) for j in range(2)]
    found_left, found_right = place(3, left_rank), place(4, right_rank)

    def pick(found, chip_side, k):
        use_up = (flip == 0) if chip_side else (flip == 1)
        return jnp.where(use_up, found[5 + k : 6 + k], found[7 + k : 8 + k])

    def stack(rows):
        return jnp.concatenate(rows, 0)

    v8 = stack([pick(near_z[1], False, 0), pick(near_z[0], False, 0)] + [o[1:2] for o in own] + [pick(near_chip[0], True, 0), pick(near_chip[1], True, 0)])
    h8 = stack([pick(near_z[1], False, 1), pick(near_z[0], False, 1)] + [o[2:3] for o in own] + [pick(near_chip[0], True, 1), pick(near_chip[1], True, 1)])
    m8 = stack([z_mask[1], z_mask[0]] + own_mask + [chip_mask[0], chip_mask[1]])
    zero4 = jnp.zeros((4, 128), f32)
    own_m = stack(own_mask + [zero4])
    own_u = stack([o[0:1] for o in own] + [zero4])
    own_sx = stack([o[3:4] for o in own] + [zero4])
    own_sy = stack([o[4:5] for o in own] + [zero4])
    sign = jnp.where(flip == 1, -1.0, 1.0).astype(f32)
    water[...] = own_m
    depth8 = jnp.where(m8 > 0.5, h8, land_depth)
    m8s = m8 * courant_scale
    own_ms = own_m * courant_scale
    ux[...] = faces(own_u * own_ms, own_m, 1)
    vy[...] = roll(faces(v8 * m8s, m8, 0), -1, 0) * sign
    turn_x = own_sx * own_m * (0.5 * turn_scale)
    turn_y = own_sy * own_m * (0.5 * turn_scale)

    def one(f, carry):
        speed, turning = kinematics(depth8, jnp.broadcast_to(sigma_rows[pl.ds(f, 1), :], (8, 128)))
        cgy[f] = roll(faces(speed * m8s, m8, 0), -1, 0) * sign
        cgx[f] = faces(roll(speed, -2, 0) * own_ms, own_m, 1)
        turning = roll(turning, -2, 0)
        tx[f] = turning * turn_x
        ty[f] = turning * turn_y
        return carry

    lax.fori_loop(0, NF, one, 0, unroll=4)

    low = lanes() % 8 < 4
    own_mask_edge = pack_edges(own_mask)
    own_u_edge = pack_edges([o[0:1] for o in own])
    own_h_edge = pack_edges([o[2:3] for o in own])
    for side in range(2):
        outside = low if side == 0 else jnp.logical_not(low)
        found = found_left[9:11] if side == 0 else found_right[11:13]
        mask = jnp.where(outside, left_mask if side == 0 else right_mask, own_mask_edge)
        u = jnp.where(outside, found[0:1], own_u_edge)
        h = jnp.where(outside, found[1:2], own_h_edge)
        depth = jnp.where(mask > 0.5, h, land_depth)
        edge_u[side] = faces(u * (mask * courant_scale), mask, 1)
        for part in range(2):
            speed, _ = kinematics(depth, sigma_packed[pl.ds(8 * part, 8), :])
            edge_cg[side, pl.ds(8 * part, 8), :] = faces(speed * (mask * courant_scale), mask, 1)


def flux(speed, behind, ahead):
    return speed * jnp.where(speed > 0.0, behind, ahead)


def along_x(value, speed):
    third = value * (1.0 / 3.0)
    behind = value - roll(third, 1)
    ahead = roll(value - roll(third, -1), -1)
    through = flux(speed, behind, ahead)
    return through - roll(through, 1)


def step_kernel(
    last, na, nb, z_in, chip_in, edges, left_in, right_in,
    cgx, cgy, tx, ty, ux, vy, water, edge_cg, edge_u, cosine, sine, *rest,
):
    if last:
        out, fix, moved, turn, swirl = rest
    else:
        out_a, out_b, out_edges, fix, moved, turn, swirl = rest
    flip = parity()
    lane = lanes()
    source = [jnp.where(flip == 1, 3 - j, j) for j in range(4)]
    low = lane % 8 < 4

    def edge_group(g, carry):
        for b, start in enumerate(STARTS):
            mine = edges[g, pl.ds(8 * b, 8), :]
            west = jnp.where(low, left_in[g, pl.ds(8 * b, 8), :], mine)
            east = jnp.where(low, mine, right_in[g, pl.ds(8 * b, 8), :])
            c = cosine[pl.ds(start, 8), :]
            change = [
                along_x(value, c * edge_cg[side, pl.ds(g, 1), :] + edge_u[side])
                for side, value in enumerate((west, east))
            ]
            fix[g, pl.ds(8 * b, 8), :] = jnp.where(low, change[1], change[0])
        return carry

    lax.fori_loop(0, GROUPS, edge_group, 0)
    at_edge = (lane < 2) | (lane >= 126)

    def one(g, q):
        f = 4 * g + q
        for b, start in enumerate(STARTS):
            base = f * ND + start
            c, s = cosine[pl.ds(start, 8), :], sine[pl.ds(start, 8), :]
            here = pl.ds(base, 8)
            value = [
                z_in[1, here, :], z_in[0, here, :], na[0, here, :], na[1, here, :],
                nb[0, here, :], nb[1, here, :], chip_in[1, here, :], chip_in[0, here, :],
            ]
            third = [v * (1.0 / 3.0) for v in value]
            across = []
            for k in range(5):
                speed = s * cgy[f, pl.ds(k, 1), :] + vy[pl.ds(k, 1), :]
                across.append(flux(speed, value[k + 1] - third[k], value[k + 2] - third[k + 3]))
            edge = fix[g, pl.ds(8 * b, 8), :]
            for j in range(4):
                speed = c * cgx[f, pl.ds(j, 1), :] + ux[pl.ds(j, 1), :]
                change = along_x(value[j + 2], speed)
                change = jnp.where(at_edge, roll(edge, -(32 * q + 8 * j + 4)), change)
                moved[q, j, pl.ds(8 + start, 8), :] = value[j + 2] - change - (across[j + 1] - across[j])
                half = s * tx[f, pl.ds(j, 1), :] - c * ty[f, pl.ds(j, 1), :]
                turn[q, j, pl.ds(8 + start, 8), :] = jnp.clip(half, -0.5 * refraction_limit, 0.5 * refraction_limit)
        for j in range(4):
            moved[q, j, pl.ds(8 + ND, 1), :] = moved[q, j, pl.ds(8, 1), :]
            turn[q, j, pl.ds(8 + ND, 1), :] = turn[q, j, pl.ds(8, 1), :]
            for start in STARTS:
                speed = turn[q, j, pl.ds(8 + start, 8), :] + turn[q, j, pl.ds(9 + start, 8), :]
                swirl[q, j, pl.ds(8 + start, 8), :] = flux(
                    speed, moved[q, j, pl.ds(8 + start, 8), :], moved[q, j, pl.ds(9 + start, 8), :]
                )
            swirl[q, j, pl.ds(7, 1), :] = swirl[q, j, pl.ds(7 + ND, 1), :]

    def finish(g, q, b):
        f = 4 * g + q
        start = STARTS[b]
        base = f * ND + start
        values = []
        for j in range(4):
            value = (
                moved[q, j, pl.ds(8 + start, 8), :]
                - swirl[q, j, pl.ds(8 + start, 8), :]
                + swirl[q, j, pl.ds(7 + start, 8), :]
            ) * water[pl.ds(j, 1), :]
            if last:
                out[pl.ds(4 * base + source[j], 8, stride=4), :] = value
            else:
                (out_a if j < 2 else out_b)[j % 2, pl.ds(base, 8), :] = value
            values.append(value)
        return values

    def group(g, carry):
        for q in range(4):
            one(g, q)
        for b in range(5):
            packed = jnp.zeros((8, 128), f32)
            for q in range(4):
                for j, value in enumerate(finish(g, q, b)):
                    if not last:
                        at = 32 * q + 8 * j
                        packed = jnp.where((lane >= at) & (lane < at + 8), roll(value, at + 4), packed)
            if not last:
                out_edges[g, pl.ds(8 * b, 8), :] = packed
        return carry

    lax.fori_loop(0, GROUPS, group, 0)


def shape(*dims, dtype=f32):
    return jax.ShapeDtypeStruct(dims, dtype)


def call(kernel, out, name, scratch=(), cost=2_000_000, moved=4_000_000):
    return pl.pallas_call(
        kernel,
        out_shape=out,
        scratch_shapes=list(scratch),
        name=name,
        cost_estimate=pl.CostEstimate(flops=cost, bytes_accessed=moved, transcendentals=0),
    )


PLANE = shape(2, ROWS, 128)
EDGES = shape(GROUPS + 1, 40, 128)
STEP_SCRATCH = [pltpu.VMEM((GROUPS, 40, 128), f32)] + [pltpu.VMEM((4, 4, 56, 128), f32)] * 3


def exchange(na, nb, edges):
    z_pairs = [p for z in range(3) for p in ((2 * z + 1, 2 * z + 2), (2 * z + 2, 2 * z + 1))]
    chip_pairs = [p for z in range(4) for p in ((2 * z, 2 * z + 1), (2 * z + 1, 2 * z))]
    east = [(i, (i + 1) % 16) for i in range(16)]
    west = [((i + 1) % 16, i) for i in range(16)]
    z_in = lax.ppermute(na, "ty", z_pairs)
    chip_in = lax.ppermute(nb, "ty", chip_pairs)
    left_in = lax.ppermute(edges, "tx", east)
    right_in = lax.ppermute(edges, "tx", west)
    return z_in, chip_in, left_in, right_in


def on_device(spectra, sea_mask, currents, sea_depth, slopes, piece_offset, piece_count):
    flat = spectra.reshape(4 * BINS, 128)
    pieces = call(pieces_kernel, shape(128, 128), "pieces", [pltpu.VMEM((128, 128), f32)])(
        currents, sea_depth.reshape(1, 1024), slopes, piece_offset, piece_count
    )
    na, nb, edges = call(planes_kernel, (PLANE, PLANE, EDGES), "planes")(flat, sea_mask)
    z_in, chip_in, left_in, right_in = exchange(na, nb, edges)
    arrived = lax.all_to_all(pieces, ("ty", "tx"), split_axis=0, concat_axis=0, tiled=True)
    per_frequency = shape(NF, 8, 128)
    speeds = call(
        fields_kernel,
        (per_frequency,) * 4 + (shape(8, 128),) * 3 + (shape(2, 16, 128), shape(2, 8, 128)),
        "fields",
    )(arrived, piece_count, sea_mask, chip_in, z_in, left_in, right_in, SIGMA_ROWS, SIGMA_PACKED)
    na, nb, own_edges = call(
        functools.partial(step_kernel, False), (PLANE, PLANE, EDGES), "step_one", STEP_SCRATCH
    )(na, nb, z_in, chip_in, edges, left_in, right_in, *speeds, COSINE, SINE)
    z_in, chip_in, left_in, right_in = exchange(na, nb, own_edges)
    out = call(functools.partial(step_kernel, True), shape(4 * BINS, 128), "step_two", STEP_SCRATCH)(
        na, nb, z_in, chip_in, own_edges, left_in, right_in, *speeds, COSINE, SINE
    )
    return out.reshape(spectra.shape)


def solution(mesh):
    return jax.shard_map(
        on_device,
        mesh=mesh,
        in_specs=(
            P(None, None, "ty", "tx"),
            P("ty", "tx"),
            P(None, ("ty", "tx")),
            P(("ty", "tx")),
            P(None, ("ty", "tx")),
            P(),
            P(),
        ),
        out_specs=P(None, None, "ty", "tx"),
        check_vma=False,
    )
```

time: 250 us -> 145 us (0.58); the launches traced: 247 us -> 145 us
  other arithmetic: 118 us -> 0 us
  Pallas kernels: 0 us -> 92 us
  local copies, waits for them, and re-layouts: 85.5 us -> 3.78 us
  blocking collectives: 0 us -> 19.9 us
  starting transfers between devices: 32.9 us -> 14.9 us
  waiting for transfers between devices: 7.62 us -> 14.5 us
  loops' own time: 3.26 us -> 0 us
    pallas_call x0 -> x5, Pallas kernels: none -> 92 us  [the longest x1 47.1 us: on_device(): call(functools.partial(step_kernel, False), (PLANE, PLANE, EDGES), 'step_...]
    add x54 -> x0, other arithmetic: 48.7 us -> none  [the longest x36 44.1 us: face_flux(): jnp.maximum(face_speed, 0.0) * upwind_left]
    squeeze x36 -> x0, local copies, waits for them, and re-layouts: 41.1 us -> none  [propagate(): result = lax.map(advance_block, (row_blocks, column_blocks, frequency))]
    concatenate x6 -> x0, other arithmetic: 35.1 us -> none  [the longest x4 31.2 us: with_halo(): shard = jnp.concatenate([before, shard, after], axis=dim)]
    slice x117 -> x0, local copies, waits for them, and re-layouts: 26.3 us -> none  [the longest x6 16.5 us: with_halo(): last = lax.slice_in_dim(shard, length - width, length, axis=dim)]
    all_to_all x0 -> x1, blocking collectives: none -> 19.9 us  [on_device(): lax.all_to_all(pieces, ('ty', 'tx'), split_axis=0, concat_axis=0, tiled=T...]
    mul x166 -> x0, other arithmetic: 15.2 us -> none  [the longest x18 4.08 us: advance(): (column_group[:, None] * cosine_dir + column_fields[0]) * column_fields[5]]
    ppermute x8, waiting for transfers between devices: 0.02 us -> 14.5 us  [the longest x2 5.55 us: exchange(): z_in = lax.ppermute(na, 'ty', z_pairs)]
  transfers between devices with their start and end apart: 9 -> 8, of which waited for: 1 -> 3; matrix products, arithmetic and copies ran while one was open for 21% -> 0% of each run, Pallas kernels for 0% -> 1%
where the time goes in v1:
time: 145 us
  Pallas kernels  92 us (63%)
  blocking collectives  19.9 us (14%)
  starting transfers between devices  14.9 us (10%)
  waiting for transfers between devices  14.5 us (10%)
  local copies, waits for them, and re-layouts  3.78 us (3%)
    pallas_call x1, Pallas kernels, on_device(): call(functools.partial(step_kernel, False), (PLANE, PLANE, EDGES), 'step_...  47.1 us
    pallas_call x1, Pallas kernels, on_device(): call(functools.partial(step_kernel, True), shape(4 * BINS, 128), 'step_tw...  33 us
    all_to_all x1, blocking collectives, on_device(): lax.all_to_all(pieces, ('ty', 'tx'), split_axis=0, concat_axis=0, tiled=T...  19.9 us
    ppermute x2, starting transfers between devices, exchange(): z_in = lax.ppermute(na, 'ty', z_pairs)  8.21 us
    ppermute x2, starting transfers between devices, exchange(): right_in = lax.ppermute(edges, 'tx', west)  5.98 us
    ppermute x2, waiting for transfers between devices, exchange(): z_in = lax.ppermute(na, 'ty', z_pairs)  5.55 us
    pallas_call x1, Pallas kernels, on_device(): call(fields_kernel, (per_frequency,) * 4 + (shape(8, 128),) * 3 + (shape(...  5.11 us
    ppermute x2, waiting for transfers between devices, exchange(): right_in = lax.ppermute(edges, 'tx', west)  4.96 us
  transfers between devices with their start and end apart: 8, of which 3 were waited for; matrix products, arithmetic and copies ran while one was open for 0% of the time, Pallas kernels for 1%

profile of v1, /device:TPU:1, one launch (start us, length us, event | category | flops | bytes accessed | tf_op | source)
XLA Modules:
  0.0 145.2 jit_solution(13228310968058069545)
XLA Ops:
  0.0 4.8 %planes.1 = (f32[2,1304,128]{2,1,0:T(8,128)}, f32[2,1304,128]{2,1,0:T(8,128)}, f32[10,40,128]{2,1,0:T(8,128)}) custom-call(f32[5184,128]{1,0:T(8,128)} %bitcast.7, s32[4,128]{1,0:T(4,128)} %sea.3), custom_call_target="tpu_custom_call" | custom-call | flops 2000000 | bytes 4000000 | tf_op jit(solution)/shard_map/planes/pallas_call | solution.py:420
  4.8 4.9 %collective-permute-start = (f32[2,1304,128]{2,1,0:T(8,128)}, f32[2,1304,128]{2,1,0:T(8,128)S(1)}, u32[]{:S(2)}, u32[]{:S(2)}) collective-permute-start(f32[2,1304,128]{2,1,0:T(8,128)} %get-tuple-element.20.na), channel_id=1, source_target_pairs={{16,32},{32,16},{48,64},{64,48},{80,96},{96,80},{17,33},{33,17},{4... | collective-permute-start | bytes 4005896 | tf_op jit(solution)/shard_map/ppermute | solution.py:408
  9.7 0.1 collective-permute-start.1
  9.8 5.0 %collective-permute-start.3 = (f32[10,40,128]{2,1,0:T(8,128)}, f32[10,40,128]{2,1,0:T(8,128)S(1)}, u32[]{:S(2)}, u32[]{:S(2)}) collective-permute-start(f32[10,40,128]{2,1,0:T(8,128)} %get-tuple-element.22.edges), channel_id=1, source_target_pairs={{1,0},{2,1},{3,2},{4,3},{5,4},{6,5},{7,6},{8,7},{9,8},{10,9},{11,1... | collective-permute-start | bytes 614408 | tf_op jit(solution)/shard_map/ppermute | solution.py:411
  14.8 0.0 collective-permute-start.2
  14.8 2.0 %pieces.1 = f32[128,128]{1,0:T(8,128)} custom-call(f32[2,1024]{1,0:T(2,128)} %currents.1, f32[1,1024]{1,0:T(1,128)} %bitcast.10, f32[2,1024]{1,0:T(2,128)} %slopes.1, s32[128,128]{1,0:T(8,128)} %offset.1, s32[128,128]{1,0:T(8,128)} %count.3), custom_call_target="tpu_custom_call" | custom-call | flops 2000000 | bytes 4000000 | tf_op jit(solution)/shard_map/pieces/pallas_call | solution.py:417
  16.7 19.9 %all_to_all.11 = f32[128,1,128]{2,1,0:T(1,128)} all-to-all(f32[128,1,128]{2,1,0:T(1,128)} %bitcast.9), channel_id=1, replica_groups=mesh['ty'=8,'tx'=16] {'ty','tx'}, dimensions={0} | all-to-all | bytes 131072 | tf_op jit(solution)/shard_map/all_to_all | solution.py:422
  36.7 0.0 collective-permute-done.z_in
  36.8 0.6 copy-done.4
  37.4 0.1 copy-done.5
  37.4 0.5 copy-done
  37.9 0.4 copy-done.1
  38.4 5.1 %fields.1 = (f32[36,8,128]{2,1,0:T(8,128)}, f32[36,8,128]{2,1,0:T(8,128)}, f32[36,8,128]{2,1,0:T(8,128)}, f32[36,8,128]{2,1,0:T(8,128)}, f32[8,128]{1,0:T(8,128)...) custom-call(f32[128,128]{1,0:T(8,128)} %bitcast.8, s32[128,128]{1,0:T(8,128)} %count.3, ...), custom_call_target="tpu_custom_call" | custom-call | flops 2000000 | bytes 4000000 | tf_op jit(solution)/shard_map/fields/pallas_call | solution.py:424
  43.5 47.1 %step_one.1 = (f32[2,1304,128]{2,1,0:T(8,128)}, f32[2,1304,128]{2,1,0:T(8,128)}, f32[10,40,128]{2,1,0:T(8,128)}) custom-call(f32[2,1304,128]{2,1,0:T(8,128)} %get-tuple-element.20.na, f32[2,1304,128]{2,1,0:T(8,128)} %get-tuple-element.21.nb, f32[2,1304,128]{2,1,0:T(8,128)} %copy-done, f32[2,1304,128]{2,1,0:T(8,128)} %copy-done.1, ...), custom_call_target="tpu_custom_call" | custom-call | flops 2000000 | bytes 4000000 | tf_op jit(solution)/shard_map/step_one/pallas_call | solution.py:429
  90.6 3.3 %collective-permute-start.4 = (f32[2,1304,128]{2,1,0:T(8,128)}, f32[2,1304,128]{2,1,0:T(8,128)S(1)}, u32[]{:S(2)}, u32[]{:S(2)}) collective-permute-start(f32[2,1304,128]{2,1,0:T(8,128)} %get-tuple-element.32.na), channel_id=1, source_target_pairs={{16,32},{32,16},{48,64},{64,48},{80,96},{96,80},{17,33},{33,17},{4... | collective-permute-start | bytes 4005896 | tf_op jit(solution)/shard_map/ppermute | solution.py:408
  93.9 0.1 collective-permute-start.5
  94.0 1.0 collective-permute-start.7
  95.0 0.6 collective-permute-start.6
  95.5 5.0 %collective-permute-done.7.right_in = f32[10,40,128]{2,1,0:T(8,128)S(1)} collective-permute-done((f32[10,40,128]{2,1,0:T(8,128)}, f32[10,40,128]{2,1,0:T(8,128)S(1)}, u32[]{:S(2)}, u32[]{:S(2)}) %collective-permute-start.7) | collective-permute-done | bytes 204832 | tf_op jit(solution)/shard_map/ppermute | solution.py:411
  100.5 3.9 %collective-permute-done.6.left_in = f32[10,40,128]{2,1,0:T(8,128)S(1)} collective-permute-done((f32[10,40,128]{2,1,0:T(8,128)}, f32[10,40,128]{2,1,0:T(8,128)S(1)}, u32[]{:S(2)}, u32[]{:S(2)}) %collective-permute-start.6) | collective-permute-done | bytes 204832 | tf_op jit(solution)/shard_map/ppermute | solution.py:410
  104.4 5.6 %collective-permute-done.4.z_in = f32[2,1304,128]{2,1,0:T(8,128)S(1)} collective-permute-done((f32[2,1304,128]{2,1,0:T(8,128)}, f32[2,1304,128]{2,1,0:T(8,128)S(1)}, u32[]{:S(2)}, u32[]{:S(2)}) %collective-permute-start.4) | collective-permute-done | bytes 1335328 | tf_op jit(solution)/shard_map/ppermute | solution.py:408
  110.0 1.1 copy-done.2
  111.1 1.1 copy-done.3
  112.2 33.0 %step_two.1 = f32[5184,128]{1,0:T(8,128)} custom-call(f32[2,1304,128]{2,1,0:T(8,128)} %get-tuple-element.32.na, f32[2,1304,128]{2,1,0:T(8,128)} %get-tuple-element.33.nb, f32[2,1304,128]{2,1,0:T(8,128)} %copy-done.2, f32[2,1304,128]{2,1,0:T(8,128)} %copy-done.3, f32[10,40,128]{2,1,0:T(8,128)} %get-tuple-element.34.edges, f32[10,40,128]{2,1,0:T(8,128)} %copy-done.7, ...), custom_call_target="tpu_custom_call" | custom-call | flops 2000000 | bytes 4000000 | tf_op jit(solution)/shard_map/step_two/pallas_call | solution.py:433
  (14 shorter events, 0.0 us)
Async XLA Ops:
  4.8 32.0 %collective-permute-start = (f32[2,1304,128]{2,1,0:T(8,128)}, f32[2,1304,128]{2,1,0:T(8,128)S(1)}, u32[]{:S(2)}, u32[]{:S(2)}) collective-permute-start(f32[2,1304,128]{2,1,0:T(8,128)} %get-tuple-element.20.na), channel_id=1, source_target_pairs={{16,32},{32,16},{48,64},{64,48},{80,96},{96,80},{17,33},{33,17},{4... | collective-permute-start | bytes 4005896 | tf_op jit(solution)/shard_map/ppermute | solution.py:408
  9.7 27.1 %collective-permute-start.1 = (f32[2,1304,128]{2,1,0:T(8,128)}, f32[2,1304,128]{2,1,0:T(8,128)S(1)}, u32[]{:S(2)}, u32[]{:S(2)}) collective-permute-start(f32[2,1304,128]{2,1,0:T(8,128)} %get-tuple-element.21.nb), channel_id=1, source_target_pairs={{0,16},{16,0},{32,48},{48,32},{64,80},{80,64},{96,112},{112,96},{1... | collective-permute-start | bytes 4005896 | tf_op jit(solution)/shard_map/ppermute | solution.py:409
  9.8 26.9 %collective-permute-start.3 = (f32[10,40,128]{2,1,0:T(8,128)}, f32[10,40,128]{2,1,0:T(8,128)S(1)}, u32[]{:S(2)}, u32[]{:S(2)}) collective-permute-start(f32[10,40,128]{2,1,0:T(8,128)} %get-tuple-element.22.edges), channel_id=1, source_target_pairs={{1,0},{2,1},{3,2},{4,3},{5,4},{6,5},{7,6},{8,7},{9,8},{10,9},{11,1... | collective-permute-start | bytes 614408 | tf_op jit(solution)/shard_map/ppermute | solution.py:411
  14.8 21.9 %collective-permute-start.2 = (f32[10,40,128]{2,1,0:T(8,128)}, f32[10,40,128]{2,1,0:T(8,128)S(1)}, u32[]{:S(2)}, u32[]{:S(2)}) collective-permute-start(f32[10,40,128]{2,1,0:T(8,128)} %get-tuple-element.22.edges), channel_id=1, source_target_pairs={{0,1},{1,2},{2,3},{3,4},{4,5},{5,6},{6,7},{7,8},{8,9},{9,10},{10,1... | collective-permute-start | bytes 614408 | tf_op jit(solution)/shard_map/ppermute | solution.py:410
  36.7 0.7 copy-start.4
  36.7 0.7 copy-start.5
  36.7 1.2 copy-start
  36.7 1.6 %copy-start.1 = (f32[2,1304,128]{2,1,0:T(8,128)}, f32[2,1304,128]{2,1,0:T(8,128)S(1)}, u32[]{:S(2)}) copy-start(f32[2,1304,128]{2,1,0:T(8,128)S(1)} %collective-permute-done.1.chip_in) | copy-start | bytes 4005892
  90.6 19.4 %collective-permute-start.4 = (f32[2,1304,128]{2,1,0:T(8,128)}, f32[2,1304,128]{2,1,0:T(8,128)S(1)}, u32[]{:S(2)}, u32[]{:S(2)}) collective-permute-start(f32[2,1304,128]{2,1,0:T(8,128)} %get-tuple-element.32.na), channel_id=1, source_target_pairs={{16,32},{32,16},{48,64},{64,48},{80,96},{96,80},{17,33},{33,17},{4... | collective-permute-start | bytes 4005896 | tf_op jit(solution)/shard_map/ppermute | solution.py:408
  93.9 16.1 %collective-permute-start.5 = (f32[2,1304,128]{2,1,0:T(8,128)}, f32[2,1304,128]{2,1,0:T(8,128)S(1)}, u32[]{:S(2)}, u32[]{:S(2)}) collective-permute-start(f32[2,1304,128]{2,1,0:T(8,128)} %get-tuple-element.33.nb), channel_id=1, source_target_pairs={{0,16},{16,0},{32,48},{48,32},{64,80},{80,64},{96,112},{112,96},{1... | collective-permute-start | bytes 4005896 | tf_op jit(solution)/shard_map/ppermute | solution.py:409
  94.0 6.5 %collective-permute-start.7 = (f32[10,40,128]{2,1,0:T(8,128)}, f32[10,40,128]{2,1,0:T(8,128)S(1)}, u32[]{:S(2)}, u32[]{:S(2)}) collective-permute-start(f32[10,40,128]{2,1,0:T(8,128)} %get-tuple-element.34.edges), channel_id=1, source_target_pairs={{1,0},{2,1},{3,2},{4,3},{5,4},{6,5},{7,6},{8,7},{9,8},{10,9},{11,1... | collective-permute-start | bytes 614408 | tf_op jit(solution)/shard_map/ppermute | solution.py:411
  95.0 9.5 %collective-permute-start.6 = (f32[10,40,128]{2,1,0:T(8,128)}, f32[10,40,128]{2,1,0:T(8,128)S(1)}, u32[]{:S(2)}, u32[]{:S(2)}) collective-permute-start(f32[10,40,128]{2,1,0:T(8,128)} %get-tuple-element.34.edges), channel_id=1, source_target_pairs={{0,1},{1,2},{2,3},{3,4},{4,5},{5,6},{6,7},{7,8},{8,9},{9,10},{10,1... | collective-permute-start | bytes 614408 | tf_op jit(solution)/shard_map/ppermute | solution.py:410
  100.5 9.5 %copy-start.6 = (f32[10,40,128]{2,1,0:T(8,128)}, f32[10,40,128]{2,1,0:T(8,128)S(1)}, u32[]{:S(2)}) copy-start(f32[10,40,128]{2,1,0:T(8,128)S(1)} %collective-permute-done.7.right_in) | copy-start | bytes 614404
  104.4 5.6 %copy-start.7 = (f32[10,40,128]{2,1,0:T(8,128)}, f32[10,40,128]{2,1,0:T(8,128)S(1)}, u32[]{:S(2)}) copy-start(f32[10,40,128]{2,1,0:T(8,128)S(1)} %collective-permute-done.6.left_in) | copy-start | bytes 614404
  110.0 1.1 copy-start.2
  111.1 1.1 copy-start.3

commit v2 on v1

--- a/solution.py
+++ b/solution.py
@@ -67,7 +67,6 @@
 
 def planes_kernel(spectra, sea, na, nb, edges):
     flip = parity()
-    lane = lanes()
     mask = sea[...].astype(f32)
     for ref in (na, nb):
         for part in range(2):
@@ -79,13 +78,27 @@
     source = [jnp.where(flip == 1, 3 - j, j) for j in range(4)]
 
     def group(g, carry):
+        for k in range(18):
+            base = 144 * g + 8 * k
+            for j in range(4):
+                (na if j < 2 else nb)[j % 2, pl.ds(base, 8), :] = (
+                    spectra[pl.ds(4 * base + source[j], 8, stride=4), :] * row_mask[j]
+                )
+        return carry
+
+    lax.fori_loop(0, GROUPS, group, 0)
+    pack_planes(na, nb, edges)
+
+
+def pack_planes(na, nb, edges):
+    lane = lanes()
+
+    def group(g, carry):
         for b, start in enumerate(STARTS):
             packed = jnp.zeros((8, 128), f32)
             for q in range(4):
-                base = (4 * g + q) * ND + start
                 for j in range(4):
-                    value = spectra[pl.ds(4 * base + source[j], 8, stride=4), :] * row_mask[j]
-                    (na if j < 2 else nb)[j % 2, pl.ds(base, 8), :] = value
+                    value = (na if j < 2 else nb)[j % 2, pl.ds((4 * g + q) * ND + start, 8), :]
                     at = 32 * q + 8 * j
                     packed = jnp.where((lane >= at) & (lane < at + 8), roll(value, at + 4), packed)
             edges[g, pl.ds(8 * b, 8), :] = packed
@@ -276,12 +289,9 @@
     return speed * jnp.where(speed > 0.0, behind, ahead)
 
 
-def along_x(value, speed):
-    third = value * (1.0 / 3.0)
-    behind = value - roll(third, 1)
-    ahead = roll(value - roll(third, -1), -1)
-    through = flux(speed, behind, ahead)
-    return through - roll(through, 1)
+def through_east(value, speed):
+    third = 1.0 / 3.0
+    return flux(speed, value - roll(value, 1) * third, roll(value, -1) - roll(value, -2) * third)
 
 
 def step_kernel(
@@ -289,9 +299,9 @@
     cgx, cgy, tx, ty, ux, vy, water, edge_cg, edge_u, cosine, sine, *rest,
 ):
     if last:
-        out, fix, moved, turn, swirl = rest
+        out, edge_flux, fix, east, moved, turn, swirl = rest
     else:
-        out_a, out_b, out_edges, fix, moved, turn, swirl = rest
+        out_a, out_b, out_edges, edge_flux, fix, east, moved, turn, swirl = rest
     flip = parity()
     lane = lanes()
     source = [jnp.where(flip == 1, 3 - j, j) for j in range(4)]
@@ -300,17 +310,37 @@
     def edge_group(g, carry):
         for b, start in enumerate(STARTS):
             mine = edges[g, pl.ds(8 * b, 8), :]
-            west = jnp.where(low, left_in[g, pl.ds(8 * b, 8), :], mine)
-            east = jnp.where(low, mine, right_in[g, pl.ds(8 * b, 8), :])
+            left = jnp.where(low, left_in[g, pl.ds(8 * b, 8), :], mine)
+            right = jnp.where(low, mine, right_in[g, pl.ds(8 * b, 8), :])
             c = cosine[pl.ds(start, 8), :]
-            change = [
-                along_x(value, c * edge_cg[side, pl.ds(g, 1), :] + edge_u[side])
-                for side, value in enumerate((west, east))
-            ]
-            fix[g, pl.ds(8 * b, 8), :] = jnp.where(low, change[1], change[0])
+            for side, value in enumerate((left, right)):
+                speed = c * edge_cg[side, pl.ds(g, 1), :] + edge_u[side]
+                edge_flux[side, g, pl.ds(8 * b, 8), :] = through_east(value, speed)
         return carry
 
     lax.fori_loop(0, GROUPS, edge_group, 0)
+
+    def x_group(g, carry):
+        for q in range(4):
+            f = 4 * g + q
+            for start in STARTS:
+                here = pl.ds(f * ND + start, 8)
+                c = cosine[pl.ds(start, 8), :]
+                for j in range(4):
+                    value = (na if j < 2 else nb)[j % 2, here, :]
+                    east[j, here, :] = through_east(value, c * cgx[f, pl.ds(j, 1), :] + ux[pl.ds(j, 1), :])
+        return carry
+
+    lax.fori_loop(0, GROUPS, x_group, 0)
+
+    def fix_group(g, carry):
+        for b in range(5):
+            here = pl.ds(8 * b, 8)
+            left, right = edge_flux[0, g, here, :], edge_flux[1, g, here, :]
+            fix[g, here, :] = jnp.where(low, right - roll(right, 1), left - roll(left, 1))
+        return carry
+
+    lax.fori_loop(0, GROUPS, fix_group, 0)
     at_edge = (lane < 2) | (lane >= 126)
 
     def one(g, q):
@@ -330,9 +360,8 @@
                 across.append(flux(speed, value[k + 1] - third[k], value[k + 2] - third[k + 3]))
             edge = fix[g, pl.ds(8 * b, 8), :]
             for j in range(4):
-                speed = c * cgx[f, pl.ds(j, 1), :] + ux[pl.ds(j, 1), :]
-                change = along_x(value[j + 2], speed)
-                change = jnp.where(at_edge, roll(edge, -(32 * q + 8 * j + 4)), change)
+                through = east[j, here, :]
+                change = jnp.where(at_edge, roll(edge, -(32 * q + 8 * j + 4)), through - roll(through, 1))
                 moved[q, j, pl.ds(8 + start, 8), :] = value[j + 2] - change - (across[j + 1] - across[j])
                 half = s * tx[f, pl.ds(j, 1), :] - c * ty[f, pl.ds(j, 1), :]
                 turn[q, j, pl.ds(8 + start, 8), :] = jnp.clip(half, -0.5 * refraction_limit, 0.5 * refraction_limit)
@@ -347,10 +376,8 @@
             swirl[q, j, pl.ds(7, 1), :] = swirl[q, j, pl.ds(7 + ND, 1), :]
 
     def finish(g, q, b):
-        f = 4 * g + q
         start = STARTS[b]
-        base = f * ND + start
-        values = []
+        base = (4 * g + q) * ND + start
         for j in range(4):
             value = (
                 moved[q, j, pl.ds(8 + start, 8), :]
@@ -361,43 +388,38 @@
                 out[pl.ds(4 * base + source[j], 8, stride=4), :] = value
             else:
                 (out_a if j < 2 else out_b)[j % 2, pl.ds(base, 8), :] = value
-            values.append(value)
-        return values
 
     def group(g, carry):
         for q in range(4):
             one(g, q)
-        for b in range(5):
-            packed = jnp.zeros((8, 128), f32)
-            for q in range(4):
-                for j, value in enumerate(finish(g, q, b)):
-                    if not last:
-                        at = 32 * q + 8 * j
-                        packed = jnp.where((lane >= at) & (lane < at + 8), roll(value, at + 4), packed)
-            if not last:
-                out_edges[g, pl.ds(8 * b, 8), :] = packed
+        for q in range(4):
+            for b in range(5):
+                finish(g, q, b)
         return carry
 
     lax.fori_loop(0, GROUPS, group, 0)
+    if not last:
+        pack_planes(out_a, out_b, out_edges)
 
 
 def shape(*dims, dtype=f32):
     return jax.ShapeDtypeStruct(dims, dtype)
 
 
-def call(kernel, out, name, scratch=(), cost=2_000_000, moved=4_000_000):
+def call(kernel, out, name, scratch=(), limit=24, cost=2_000_000, moved=4_000_000):
     return pl.pallas_call(
         kernel,
         out_shape=out,
         scratch_shapes=list(scratch),
         name=name,
+        compiler_params=pltpu.CompilerParams(vmem_limit_bytes=limit << 20),
         cost_estimate=pl.CostEstimate(flops=cost, bytes_accessed=moved, transcendentals=0),
     )
 
 
 PLANE = shape(2, ROWS, 128)
 EDGES = shape(GROUPS + 1, 40, 128)
-STEP_SCRATCH = [pltpu.VMEM((GROUPS, 40, 128), f32)] + [pltpu.VMEM((4, 4, 56, 128), f32)] * 3
+STEP_SCRATCH = [pltpu.VMEM((2, GROUPS, 40, 128), f32), pltpu.VMEM((GROUPS, 40, 128), f32), pltpu.VMEM((4, BINS, 128), f32)] + [pltpu.VMEM((4, 4, 56, 128), f32)] * 3
 
 
 def exchange(na, nb, edges):

time: 145 us -> 76.6 us (0.53)
  Pallas kernels: 92 us -> 25.3 us
    pallas_call x1, Pallas kernels: 47.1 us -> 10.1 us  [on_device(): call(functools.partial(step_kernel, False), (PLANE, PLANE, EDGES), 'step_...]
    pallas_call x1, Pallas kernels: 33 us -> 10.2 us  [on_device(): call(functools.partial(step_kernel, True), shape(4 * BINS, 128), 'step_tw...]
    pallas_call x1, Pallas kernels: 4.75 us -> 1.82 us  [on_device(): call(planes_kernel, (PLANE, PLANE, EDGES), 'planes')(flat, sea_mask)]
    pallas_call x1, Pallas kernels: 5.11 us -> 2.65 us  [on_device(): call(fields_kernel, (per_frequency,) * 4 + (shape(8, 128),) * 3 + (shape(...]
    pallas_call x1, Pallas kernels: 1.98 us -> 0.44 us  [on_device(): call(pieces_kernel, shape(128, 128), 'pieces', [pltpu.VMEM((128, 128), f3...]
    unnamed x16 -> x22, local copies, waits for them, and re-layouts: 3.78 us -> 2.48 us
where the time goes in v2:
time: 76.6 us; the launch traced here: 76.4 us
  Pallas kernels  25.3 us (33%)
  blocking collectives  19.3 us (25%)
  starting transfers between devices  15 us (20%)
  waiting for transfers between devices  14.2 us (19%)
  local copies, waits for them, and re-layouts  2.48 us (3%)
    all_to_all x1, blocking collectives, on_device(): lax.all_to_all(pieces, ('ty', 'tx'), split_axis=0, concat_axis=0, tiled=T...  19.3 us
    pallas_call x1, Pallas kernels, on_device(): call(functools.partial(step_kernel, True), shape(4 * BINS, 128), 'step_tw...  10.2 us
    pallas_call x1, Pallas kernels, on_device(): call(functools.partial(step_kernel, False), (PLANE, PLANE, EDGES), 'step_...  10.1 us
    ppermute x2, starting transfers between devices, exchange(): z_in = lax.ppermute(na, 'ty', z_pairs)  8.25 us
    ppermute x2, starting transfers between devices, exchange(): right_in = lax.ppermute(edges, 'tx', west)  6.05 us
    ppermute x2, waiting for transfers between devices, exchange(): z_in = lax.ppermute(na, 'ty', z_pairs)  5.47 us
    ppermute x2, waiting for transfers between devices, exchange(): right_in = lax.ppermute(edges, 'tx', west)  4.74 us
    ppermute x2, waiting for transfers between devices, exchange(): left_in = lax.ppermute(edges, 'tx', east)  4.03 us
  transfers between devices with their start and end apart: 8, of which 3 were waited for; matrix products, arithmetic and copies ran while one was open for 0% of the time, Pallas kernels for 1%

profile of v2, /device:TPU:1, one launch (start us, length us, event | category | flops | bytes accessed | tf_op | source)
XLA Modules:
  0.0 76.4 jit_solution(8273153611625054759)
XLA Ops:
  0.0 1.7 %copy-done = f32[36,36,4,128]{3,2,1,0:T(4,128)S(1)} copy-done((f32[36,36,4,128]{3,2,1,0:T(4,128)S(1)}, f32[36,36,4,128]{3,2,1,0:T(4,128)}, u32[]{:S(2)}) %copy-start) | copy-done | bytes 2654232
  1.8 0.7 copy-done.9
  2.5 0.0 copy-start.5
  2.5 0.0 copy-start.6
  2.5 1.8 %planes.1 = (f32[2,1304,128]{2,1,0:T(8,128)S(1)}, f32[2,1304,128]{2,1,0:T(8,128)S(1)}, f32[10,40,128]{2,1,0:T(8,128)S(1)}) custom-call(f32[5184,128]{1,0:T(8,128)S(1)} %bitcast.7, s32[4,128]{1,0:T(4,128)S(1)} %copy-done.9), custom_call_target="tpu_custom_call" | custom-call | flops 2000000 | bytes 4000000 | tf_op jit(solution)/shard_map/planes/pallas_call | solution.py:442
  4.3 4.9 %collective-permute-start = (f32[2,1304,128]{2,1,0:T(8,128)S(1)}, f32[2,1304,128]{2,1,0:T(8,128)S(1)}, u32[]{:S(2)}, u32[]{:S(2)}) collective-permute-start(f32[2,1304,128]{2,1,0:T(8,128)S(1)} %get-tuple-element.20.na), channel_id=1, source_target_pairs={{16,32},{32,16},{48,64},{64,48},{80,96},{96,80},{17,33},{33,17},{4... | collective-permute-start | bytes 4005896 | tf_op jit(solution)/shard_map/ppermute | solution.py:430
  9.2 0.1 collective-permute-start.1
  9.3 5.0 %collective-permute-start.3 = (f32[10,40,128]{2,1,0:T(8,128)S(1)}, f32[10,40,128]{2,1,0:T(8,128)S(1)}, u32[]{:S(2)}, u32[]{:S(2)}) collective-permute-start(f32[10,40,128]{2,1,0:T(8,128)S(1)} %get-tuple-element.22.edges), channel_id=1, source_target_pairs={{1,0},{2,1},{3,2},{4,3},{5,4},{6,5},{7,6},{8,7},{9,8},{10,9},{11,1... | collective-permute-start | bytes 614408 | tf_op jit(solution)/shard_map/ppermute | solution.py:433
  14.4 0.4 pieces.1
  14.8 19.3 %all_to_all.11 = f32[128,1,128]{2,1,0:T(1,128)S(1)} all-to-all(f32[128,1,128]{2,1,0:T(1,128)S(1)} %bitcast.9), channel_id=1, replica_groups=mesh['ty'=8,'tx'=16] {'ty','tx'}, dimensions={0} | all-to-all | bytes 131072 | tf_op jit(solution)/shard_map/all_to_all | solution.py:444
  34.1 0.0 collective-permute-done.3.right_in
  34.2 0.0 collective-permute-done.2.left_in
  34.2 0.0 copy-start.2
  34.2 0.0 copy-start.3
  34.2 2.6 %fields.1 = (f32[36,8,128]{2,1,0:T(8,128)S(1)}, f32[36,8,128]{2,1,0:T(8,128)S(1)}, f32[36,8,128]{2,1,0:T(8,128)S(1)}, f32[36,8,128]{2,1,0:T(8,128)S(1)}, f32[8,1...) custom-call(f32[128,128]{1,0:T(8,128)S(1)} %bitcast.8, ...), custom_call_target="tpu_custom_call" | custom-call | flops 2000000 | bytes 4000000 | tf_op jit(solution)/shard_map/fields/pallas_call | solution.py:446
  36.9 10.1 %step_one.1 = (f32[2,1304,128]{2,1,0:T(8,128)S(1)}, f32[2,1304,128]{2,1,0:T(8,128)S(1)}, f32[10,40,128]{2,1,0:T(8,128)S(1)}) custom-call(f32[2,1304,128]{2,1,0:T(8,128)S(1)} %get-tuple-element.20.na, f32[2,1304,128]{2,1,0:T(8,128)S(1)} %get-tuple-element.21.nb, f32[2,1304,128]{2,1,0:T(8,128)S(1)} %collective-permute-done.z_in, ...), custom_call_target="tpu_custom_call" | custom-call | flops 2000000 | bytes 4000000 | tf_op jit(solution)/shard_map/step_one/pallas_call | solution.py:451
  47.0 3.3 %collective-permute-start.4 = (f32[2,1304,128]{2,1,0:T(8,128)S(1)}, f32[2,1304,128]{2,1,0:T(8,128)S(1)}, u32[]{:S(2)}, u32[]{:S(2)}) collective-permute-start(f32[2,1304,128]{2,1,0:T(8,128)S(1)} %get-tuple-element.32.na), channel_id=1, source_target_pairs={{16,32},{32,16},{48,64},{64,48},{80,96},{96,80},{17,33},{33,17},{4... | collective-permute-start | bytes 4005896 | tf_op jit(solution)/shard_map/ppermute | solution.py:430
  50.3 0.1 collective-permute-start.5
  50.4 1.1 %collective-permute-start.7 = (f32[10,40,128]{2,1,0:T(8,128)S(1)}, f32[10,40,128]{2,1,0:T(8,128)S(1)}, u32[]{:S(2)}, u32[]{:S(2)}) collective-permute-start(f32[10,40,128]{2,1,0:T(8,128)S(1)} %get-tuple-element.34.edges), channel_id=1, source_target_pairs={{1,0},{2,1},{3,2},{4,3},{5,4},{6,5},{7,6},{8,7},{9,8},{10,9},{11,1... | collective-permute-start | bytes 614408 | tf_op jit(solution)/shard_map/ppermute | solution.py:433
  51.5 0.5 collective-permute-start.6
  52.0 4.7 %collective-permute-done.7.right_in = f32[10,40,128]{2,1,0:T(8,128)S(1)} collective-permute-done((f32[10,40,128]{2,1,0:T(8,128)S(1)}, f32[10,40,128]{2,1,0:T(8,128)S(1)}, u32[]{:S(2)}, u32[]{:S(2)}) %collective-permute-start.7) | collective-permute-done | bytes 204832 | tf_op jit(solution)/shard_map/ppermute | solution.py:433
  56.7 4.0 %collective-permute-done.6.left_in = f32[10,40,128]{2,1,0:T(8,128)S(1)} collective-permute-done((f32[10,40,128]{2,1,0:T(8,128)S(1)}, f32[10,40,128]{2,1,0:T(8,128)S(1)}, u32[]{:S(2)}, u32[]{:S(2)}) %collective-permute-start.6) | collective-permute-done | bytes 204832 | tf_op jit(solution)/shard_map/ppermute | solution.py:432
  60.7 5.5 %collective-permute-done.4.z_in = f32[2,1304,128]{2,1,0:T(8,128)S(1)} collective-permute-done((f32[2,1304,128]{2,1,0:T(8,128)S(1)}, f32[2,1304,128]{2,1,0:T(8,128)S(1)}, u32[]{:S(2)}, u32[]{:S(2)}) %collective-permute-start.4) | collective-permute-done | bytes 1335328 | tf_op jit(solution)/shard_map/ppermute | solution.py:430
  66.2 10.2 %step_two.1 = f32[5184,128]{1,0:T(8,128)} custom-call(f32[2,1304,128]{2,1,0:T(8,128)S(1)} %get-tuple-element.32.na, f32[2,1304,128]{2,1,0:T(8,128)S(1)} %get-tuple-element.33.nb, f32[2,1304,128]{2,1,0:T(8,128)S(1)} %collective-permute-done.4.z_in, f32[2,1304,128]{2,1,0:T(8,128)S(1)} %collective-permute-done.5.chip_in, ...), custom_call_target="tpu_custom_call" | custom-call | flops 2000000 | bytes 4000000 | tf_op jit(solution)/shard_map/step_two/pallas_call | solution.py:455
  (20 shorter events, 0.0 us)
Async XLA Ops:
  0.0 1.7 %copy-start = (f32[36,36,4,128]{3,2,1,0:T(4,128)S(1)}, f32[36,36,4,128]{3,2,1,0:T(4,128)}, u32[]{:S(2)}) copy-start(f32[36,36,4,128]{3,2,1,0:T(4,128)} %param.11) | copy-start | bytes 7962628
  1.8 0.7 copy-start.9
  2.4 11.9 %copy-start.1 = (s32[128,128]{1,0:T(8,128)S(1)}, s32[128,128]{1,0:T(8,128)}, u32[]{:S(2)}) copy-start(s32[128,128]{1,0:T(8,128)} %count.3) | copy-start | bytes 196612
  2.4 11.9 %copy-start.4 = (s32[128,128]{1,0:T(8,128)S(1)}, s32[128,128]{1,0:T(8,128)}, u32[]{:S(2)}) copy-start(s32[128,128]{1,0:T(8,128)} %offset.1) | copy-start | bytes 196612
  2.4 11.9 %copy-start.7 = (f32[2,1024]{1,0:T(2,128)S(1)}, f32[2,1024]{1,0:T(2,128)}, u32[]{:S(2)}) copy-start(f32[2,1024]{1,0:T(2,128)} %currents.1) | copy-start | bytes 24580
  2.4 11.9 %copy-start.8 = (f32[2,1024]{1,0:T(2,128)S(1)}, f32[2,1024]{1,0:T(2,128)}, u32[]{:S(2)}) copy-start(f32[2,1024]{1,0:T(2,128)} %slopes.1) | copy-start | bytes 24580
  2.4 11.9 %copy-start.10 = (f32[1024]{0:T(1024)S(1)}, f32[1024]{0:T(1024)}, u32[]{:S(2)}) copy-start(f32[1024]{0:T(1024)} %param.14) | copy-start | bytes 12292
  2.5 31.7 %copy-start.5 = (f32[36,128]{1,0:T(8,128)S(1)}, f32[36,128]{1,0:T(8,128)}, u32[]{:S(2)}) copy-start(f32[36,128]{1,0:T(8,128)} %constant.8.clone.sigma_rows) | copy-start | bytes 55300
  2.5 31.7 %copy-start.6 = (f32[16,128]{1,0:T(8,128)S(1)}, f32[16,128]{1,0:T(8,128)}, u32[]{:S(2)}) copy-start(f32[16,128]{1,0:T(8,128)} %constant.9.clone.sigma_packed) | copy-start | bytes 24580
  4.3 29.9 %collective-permute-start = (f32[2,1304,128]{2,1,0:T(8,128)S(1)}, f32[2,1304,128]{2,1,0:T(8,128)S(1)}, u32[]{:S(2)}, u32[]{:S(2)}) collective-permute-start(f32[2,1304,128]{2,1,0:T(8,128)S(1)} %get-tuple-element.20.na), channel_id=1, source_target_pairs={{16,32},{32,16},{48,64},{64,48},{80,96},{96,80},{17,33},{33,17},{4... | collective-permute-start | bytes 4005896 | tf_op jit(solution)/shard_map/ppermute | solution.py:430
  9.2 24.9 %collective-permute-start.1 = (f32[2,1304,128]{2,1,0:T(8,128)S(1)}, f32[2,1304,128]{2,1,0:T(8,128)S(1)}, u32[]{:S(2)}, u32[]{:S(2)}) collective-permute-start(f32[2,1304,128]{2,1,0:T(8,128)S(1)} %get-tuple-element.21.nb), channel_id=1, source_target_pairs={{0,16},{16,0},{32,48},{48,32},{64,80},{80,64},{96,112},{112,96},{1... | collective-permute-start | bytes 4005896 | tf_op jit(solution)/shard_map/ppermute | solution.py:431
  9.3 24.8 %collective-permute-start.3 = (f32[10,40,128]{2,1,0:T(8,128)S(1)}, f32[10,40,128]{2,1,0:T(8,128)S(1)}, u32[]{:S(2)}, u32[]{:S(2)}) collective-permute-start(f32[10,40,128]{2,1,0:T(8,128)S(1)} %get-tuple-element.22.edges), channel_id=1, source_target_pairs={{1,0},{2,1},{3,2},{4,3},{5,4},{6,5},{7,6},{8,7},{9,8},{10,9},{11,1... | collective-permute-start | bytes 614408 | tf_op jit(solution)/shard_map/ppermute | solution.py:433
  14.3 19.8 %collective-permute-start.2 = (f32[10,40,128]{2,1,0:T(8,128)S(1)}, f32[10,40,128]{2,1,0:T(8,128)S(1)}, u32[]{:S(2)}, u32[]{:S(2)}) collective-permute-start(f32[10,40,128]{2,1,0:T(8,128)S(1)} %get-tuple-element.22.edges), channel_id=1, source_target_pairs={{0,1},{1,2},{2,3},{3,4},{4,5},{5,6},{6,7},{7,8},{8,9},{9,10},{10,1... | collective-permute-start | bytes 614408 | tf_op jit(solution)/shard_map/ppermute | solution.py:432
  34.2 2.7 %copy-start.2 = (f32[48,128]{1,0:T(8,128)S(1)}, f32[48,128]{1,0:T(8,128)}, u32[]{:S(2)}) copy-start(f32[48,128]{1,0:T(8,128)} %constant.11.clone.sine) | copy-start | bytes 73732
  34.2 2.7 %copy-start.3 = (f32[48,128]{1,0:T(8,128)S(1)}, f32[48,128]{1,0:T(8,128)}, u32[]{:S(2)}) copy-start(f32[48,128]{1,0:T(8,128)} %constant.10.clone.cosine) | copy-start | bytes 73732
  47.0 19.2 %collective-permute-start.4 = (f32[2,1304,128]{2,1,0:T(8,128)S(1)}, f32[2,1304,128]{2,1,0:T(8,128)S(1)}, u32[]{:S(2)}, u32[]{:S(2)}) collective-permute-start(f32[2,1304,128]{2,1,0:T(8,128)S(1)} %get-tuple-element.32.na), channel_id=1, source_target_pairs={{16,32},{32,16},{48,64},{64,48},{80,96},{96,80},{17,33},{33,17},{4... | collective-permute-start | bytes 4005896 | tf_op jit(solution)/shard_map/ppermute | solution.py:430
  50.3 15.9 %collective-permute-start.5 = (f32[2,1304,128]{2,1,0:T(8,128)S(1)}, f32[2,1304,128]{2,1,0:T(8,128)S(1)}, u32[]{:S(2)}, u32[]{:S(2)}) collective-permute-start(f32[2,1304,128]{2,1,0:T(8,128)S(1)} %get-tuple-element.33.nb), channel_id=1, source_target_pairs={{0,16},{16,0},{32,48},{48,32},{64,80},{80,64},{96,112},{112,96},{1... | collective-permute-start | bytes 4005896 | tf_op jit(solution)/shard_map/ppermute | solution.py:431
  50.4 6.3 %collective-permute-start.7 = (f32[10,40,128]{2,1,0:T(8,128)S(1)}, f32[10,40,128]{2,1,0:T(8,128)S(1)}, u32[]{:S(2)}, u32[]{:S(2)}) collective-permute-start(f32[10,40,128]{2,1,0:T(8,128)S(1)} %get-tuple-element.34.edges), channel_id=1, source_target_pairs={{1,0},{2,1},{3,2},{4,3},{5,4},{6,5},{7,6},{8,7},{9,8},{10,9},{11,1... | collective-permute-start | bytes 614408 | tf_op jit(solution)/shard_map/ppermute | solution.py:433
  51.5 9.2 %collective-permute-start.6 = (f32[10,40,128]{2,1,0:T(8,128)S(1)}, f32[10,40,128]{2,1,0:T(8,128)S(1)}, u32[]{:S(2)}, u32[]{:S(2)}) collective-permute-start(f32[10,40,128]{2,1,0:T(8,128)S(1)} %get-tuple-element.34.edges), channel_id=1, source_target_pairs={{0,1},{1,2},{2,3},{3,4},{4,5},{5,6},{6,7},{7,8},{8,9},{9,10},{10,1... | collective-permute-start | bytes 614408 | tf_op jit(solution)/shard_map/ppermute | solution.py:432

commit v3 on v2

--- a/solution.py
+++ b/solution.py
@@ -8,6 +8,7 @@
 from jax.experimental import pallas as pl
 from jax.experimental.pallas import tpu as pltpu
 from jax.sharding import PartitionSpec as P
+
 
 NF, ND = 36, 36
 BINS = NF * ND
@@ -65,15 +66,15 @@
     return lax.rem(lax.axis_index("ty"), 2)
 
 
-def planes_kernel(spectra, sea, na, nb, edges):
+def planes_kernel(spectra, sea, na, nb, edges, to_east, to_west):
     flip = parity()
     mask = sea[...].astype(f32)
-    for ref in (na, nb):
-        for part in range(2):
-            ref[part, pl.ds(BINS, 8), :] = jnp.concatenate([mask, jnp.zeros((4, 128), f32)], 0)
-    edges[GROUPS, pl.ds(0, 8), :] = jnp.concatenate([mask, jnp.zeros((4, 128), f32)], 0)
-    for r in range(8, 40, 8):
-        edges[GROUPS, pl.ds(r, 8), :] = jnp.zeros((8, 128), f32)
+    tail = jnp.concatenate([mask, jnp.zeros((4, 128), f32)], 0)
+    for part in range(2):
+        na[part, pl.ds(BINS, 8), :] = tail
+        nb[part, pl.ds(BINS, 8), :] = tail
+    to_east[0, pl.ds(40, 8), :] = tail
+    to_west[0, pl.ds(40, 8), :] = tail
     row_mask = [jnp.broadcast_to(jnp.where(flip == 1, mask[3 - j : 4 - j], mask[j : j + 1]), (8, 128)) for j in range(4)]
     source = [jnp.where(flip == 1, 3 - j, j) for j in range(4)]
 
@@ -88,6 +89,7 @@
 
     lax.fori_loop(0, GROUPS, group, 0)
     pack_planes(na, nb, edges)
+    pack_sends(edges, to_east, to_west)
 
 
 def pack_planes(na, nb, edges):
@@ -105,6 +107,36 @@
         return carry
 
     lax.fori_loop(0, GROUPS, group, 0)
+
+
+SHIFTS = (0, 2, 4, -2)
+
+
+def place_of(first, g):
+    return lanes() % 8 // 2 == (first + SHIFTS[g % 4]) % 8 // 2
+
+
+def pack_sends(edges, to_east, to_west):
+    for b in range(5):
+        here = pl.ds(8 * b, 8)
+        for first in range(0, GROUPS, 4):
+            east, west = jnp.zeros((8, 128), f32), jnp.zeros((8, 128), f32)
+            for g in range(first, min(first + 4, GROUPS)):
+                value = roll(edges[g, here, :], SHIFTS[g % 4])
+                east = jnp.where(place_of(2, g), value, east)
+                west = jnp.where(place_of(4, g), value, west)
+            to_east[first // 4, here, :] = east
+            to_west[first // 4, here, :] = west
+
+
+def unpack_sends(edges, left_in, right_in, halo):
+    c = lanes() % 8 // 2
+    for b in range(5):
+        here = pl.ds(8 * b, 8)
+        for g in range(GROUPS):
+            mine = edges[g, here, :]
+            halo[0, g, here, :] = jnp.where(c == 1, roll(left_in[g // 4, here, :], -SHIFTS[g % 4]), mine)
+            halo[1, g, here, :] = jnp.where(c == 2, roll(right_in[g // 4, here, :], -SHIFTS[g % 4]), mine)
 
 
 def pieces_kernel(currents, depth, slopes, offset, count, out, rows):
@@ -183,8 +215,8 @@
         sea[...].astype(f32),
         chip_in[0, pl.ds(BINS, 4), :],
         z_in[0, pl.ds(BINS, 4), :],
-        left_in[GROUPS, pl.ds(0, 4), :],
-        right_in[GROUPS, pl.ds(0, 4), :],
+        left_in[0, pl.ds(40, 4), :],
+        right_in[0, pl.ds(40, 4), :],
     ]
     stacked = jnp.concatenate(masks + [jnp.zeros((4, 128), f32)], 0)
     upto = (sub128 <= lane128).astype(f32).astype(bf16)
@@ -294,31 +326,35 @@
     return flux(speed, value - roll(value, 1) * third, roll(value, -1) - roll(value, -2) * third)
 
 
-def step_kernel(
-    last, na, nb, z_in, chip_in, edges, left_in, right_in,
-    cgx, cgy, tx, ty, ux, vy, water, edge_cg, edge_u, cosine, sine, *rest,
-):
-    if last:
-        out, edge_flux, fix, east, moved, turn, swirl = rest
+def step_kernel(high, make_fix, pack, last, halo, na, nb, *refs):
+    refs = list(refs)
+    take = lambda n: [refs.pop(0) for _ in range(n)]
+    if make_fix:
+        edges, left_in, right_in = take(3)
     else:
-        out_a, out_b, out_edges, edge_flux, fix, east, moved, turn, swirl = rest
+        (fix,) = take(1)
+    cgx, cgy, tx, ty, ux, vy, water, edge_cg, edge_u, cosine, sine = take(11)
+    other = take(1)[0] if pack or last else None
+    out = take(1)[0]
+    if make_fix:
+        (fix,) = take(1)
+    if pack:
+        out_edges, to_east, to_west = take(3)
+    edge_halo, edge_flux, east, moved, turn, swirl, buffer, done = refs
     flip = parity()
     lane = lanes()
-    source = [jnp.where(flip == 1, 3 - j, j) for j in range(4)]
     low = lane % 8 < 4
+    first = 2 if high else 0
+    own = nb if high else na
 
     def edge_group(g, carry):
         for b, start in enumerate(STARTS):
-            mine = edges[g, pl.ds(8 * b, 8), :]
-            left = jnp.where(low, left_in[g, pl.ds(8 * b, 8), :], mine)
-            right = jnp.where(low, mine, right_in[g, pl.ds(8 * b, 8), :])
             c = cosine[pl.ds(start, 8), :]
-            for side, value in enumerate((left, right)):
+            for side in range(2):
                 speed = c * edge_cg[side, pl.ds(g, 1), :] + edge_u[side]
-                edge_flux[side, g, pl.ds(8 * b, 8), :] = through_east(value, speed)
-        return carry
-
-    lax.fori_loop(0, GROUPS, edge_group, 0)
+                here = pl.ds(8 * b, 8)
+                edge_flux[side, g, here, :] = through_east(edge_halo[side, g, here, :], speed)
+        return carry
 
     def x_group(g, carry):
         for q in range(4):
@@ -326,12 +362,10 @@
             for start in STARTS:
                 here = pl.ds(f * ND + start, 8)
                 c = cosine[pl.ds(start, 8), :]
-                for j in range(4):
-                    value = (na if j < 2 else nb)[j % 2, here, :]
-                    east[j, here, :] = through_east(value, c * cgx[f, pl.ds(j, 1), :] + ux[pl.ds(j, 1), :])
-        return carry
-
-    lax.fori_loop(0, GROUPS, x_group, 0)
+                for j in range(2):
+                    speed = c * cgx[f, pl.ds(first + j, 1), :] + ux[pl.ds(first + j, 1), :]
+                    east[j, here, :] = through_east(own[j, here, :], speed)
+        return carry
 
     def fix_group(g, carry):
         for b in range(5):
@@ -340,7 +374,12 @@
             fix[g, here, :] = jnp.where(low, right - roll(right, 1), left - roll(left, 1))
         return carry
 
-    lax.fori_loop(0, GROUPS, fix_group, 0)
+    if make_fix:
+        unpack_sends(edges, left_in, right_in, edge_halo)
+        lax.fori_loop(0, GROUPS, edge_group, 0)
+    x_group(0, 0)
+    if make_fix:
+        lax.fori_loop(0, GROUPS, fix_group, 0)
     at_edge = (lane < 2) | (lane >= 126)
 
     def one(g, q):
@@ -349,23 +388,25 @@
             base = f * ND + start
             c, s = cosine[pl.ds(start, 8), :], sine[pl.ds(start, 8), :]
             here = pl.ds(base, 8)
-            value = [
-                z_in[1, here, :], z_in[0, here, :], na[0, here, :], na[1, here, :],
-                nb[0, here, :], nb[1, here, :], chip_in[1, here, :], chip_in[0, here, :],
-            ]
+            value = [na[0, here, :], na[1, here, :], nb[0, here, :], nb[1, here, :]]
+            if high:
+                value = value + [halo[1, here, :], halo[0, here, :]]
+            else:
+                value = [halo[1, here, :], halo[0, here, :]] + value
             third = [v * (1.0 / 3.0) for v in value]
             across = []
-            for k in range(5):
-                speed = s * cgy[f, pl.ds(k, 1), :] + vy[pl.ds(k, 1), :]
+            for k in range(3):
+                speed = s * cgy[f, pl.ds(first + k, 1), :] + vy[pl.ds(first + k, 1), :]
                 across.append(flux(speed, value[k + 1] - third[k], value[k + 2] - third[k + 3]))
             edge = fix[g, pl.ds(8 * b, 8), :]
-            for j in range(4):
+            for j in range(2):
+                row = first + j
                 through = east[j, here, :]
-                change = jnp.where(at_edge, roll(edge, -(32 * q + 8 * j + 4)), through - roll(through, 1))
+                change = jnp.where(at_edge, roll(edge, -(32 * q + 8 * row + 4)), through - roll(through, 1))
                 moved[q, j, pl.ds(8 + start, 8), :] = value[j + 2] - change - (across[j + 1] - across[j])
-                half = s * tx[f, pl.ds(j, 1), :] - c * ty[f, pl.ds(j, 1), :]
+                half = s * tx[f, pl.ds(row, 1), :] - c * ty[f, pl.ds(row, 1), :]
                 turn[q, j, pl.ds(8 + start, 8), :] = jnp.clip(half, -0.5 * refraction_limit, 0.5 * refraction_limit)
-        for j in range(4):
+        for j in range(2):
             moved[q, j, pl.ds(8 + ND, 1), :] = moved[q, j, pl.ds(8, 1), :]
             turn[q, j, pl.ds(8 + ND, 1), :] = turn[q, j, pl.ds(8, 1), :]
             for start in STARTS:
@@ -375,86 +416,127 @@
                 )
             swirl[q, j, pl.ds(7, 1), :] = swirl[q, j, pl.ds(7 + ND, 1), :]
 
-    def finish(g, q, b):
-        start = STARTS[b]
+    def finish(g, q, start):
         base = (4 * g + q) * ND + start
-        for j in range(4):
+        for j in range(2):
             value = (
                 moved[q, j, pl.ds(8 + start, 8), :]
                 - swirl[q, j, pl.ds(8 + start, 8), :]
                 + swirl[q, j, pl.ds(7 + start, 8), :]
-            ) * water[pl.ds(j, 1), :]
+            ) * water[pl.ds(first + j, 1), :]
             if last:
-                out[pl.ds(4 * base + source[j], 8, stride=4), :] = value
+                buffer[pl.ds(4 * base + jnp.where(flip == 1, 3 - j, j), 8, stride=4), :] = value
+                buffer[pl.ds(4 * base + jnp.where(flip == 1, 1 - j, 2 + j), 8, stride=4), :] = other[j, pl.ds(base, 8), :]
             else:
-                (out_a if j < 2 else out_b)[j % 2, pl.ds(base, 8), :] = value
+                out[j, pl.ds(base, 8), :] = value
+
+    def result(g):
+        rows = pl.ds(pl.multiple_of(576 * g, 8), 576)
+        return pltpu.make_async_copy(buffer.at[rows, :], out.at[rows, :], done.at[g])
 
     def group(g, carry):
         for q in range(4):
             one(g, q)
         for q in range(4):
-            for b in range(5):
-                finish(g, q, b)
+            for start in STARTS:
+                finish(g, q, start)
+        if last:
+            result(g).start()
+        x_group(jnp.minimum(g + 1, GROUPS - 1), 0)
         return carry
 
     lax.fori_loop(0, GROUPS, group, 0)
-    if not last:
-        pack_planes(out_a, out_b, out_edges)
+    if last:
+        for g in range(GROUPS):
+            result(g).wait()
+    if pack:
+        pack_planes(other, out, out_edges)
+        pack_sends(out_edges, to_east, to_west)
 
 
 def shape(*dims, dtype=f32):
     return jax.ShapeDtypeStruct(dims, dtype)
 
 
-def call(kernel, out, name, scratch=(), limit=24, cost=2_000_000, moved=4_000_000):
+def call(kernel, out, scratch=(), limit=8, cost=2_000_000, moved=4_000_000, **specs):
     return pl.pallas_call(
         kernel,
         out_shape=out,
         scratch_shapes=list(scratch),
-        name=name,
         compiler_params=pltpu.CompilerParams(vmem_limit_bytes=limit << 20),
         cost_estimate=pl.CostEstimate(flops=cost, bytes_accessed=moved, transcendentals=0),
+        **specs,
     )
 
 
 PLANE = shape(2, ROWS, 128)
-EDGES = shape(GROUPS + 1, 40, 128)
-STEP_SCRATCH = [pltpu.VMEM((2, GROUPS, 40, 128), f32), pltpu.VMEM((GROUPS, 40, 128), f32), pltpu.VMEM((4, BINS, 128), f32)] + [pltpu.VMEM((4, 4, 56, 128), f32)] * 3
-
-
-def exchange(na, nb, edges):
-    z_pairs = [p for z in range(3) for p in ((2 * z + 1, 2 * z + 2), (2 * z + 2, 2 * z + 1))]
-    chip_pairs = [p for z in range(4) for p in ((2 * z, 2 * z + 1), (2 * z + 1, 2 * z))]
+EDGES = shape(GROUPS, 40, 128)
+SENDS = shape(3, 48, 128)
+
+
+def step(high, make_fix, pack, last, *operands):
+    out = [shape(4 * BINS, 128) if last else PLANE]
+    specs = {}
+    if make_fix:
+        out.append(shape(GROUPS, 40, 128))
+    if pack:
+        out += [EDGES, SENDS, SENDS]
+    if last:
+        specs["out_specs"] = [pl.BlockSpec(memory_space=pltpu.MemorySpace.HBM)]
+    scratch = [
+        pltpu.VMEM((2, GROUPS, 40, 128) if make_fix else (8, 128), f32),
+        pltpu.VMEM((2, GROUPS, 40, 128) if make_fix else (8, 128), f32),
+        pltpu.VMEM((2, BINS, 128), f32),
+        pltpu.VMEM((4, 2, 56, 128), f32),
+        pltpu.VMEM((4, 2, 56, 128), f32),
+        pltpu.VMEM((4, 2, 56, 128), f32),
+        pltpu.VMEM((4 * BINS, 128) if last else (8, 128), f32),
+        pltpu.SemaphoreType.DMA((GROUPS,)),
+    ]
+    return call(functools.partial(step_kernel, high, make_fix, pack, last), out, scratch, 8, **specs)(*operands)
+
+
+Z_PAIRS = [p for z in range(3) for p in ((2 * z + 1, 2 * z + 2), (2 * z + 2, 2 * z + 1))]
+CHIP_PAIRS = [p for z in range(4) for p in ((2 * z, 2 * z + 1), (2 * z + 1, 2 * z))]
+
+
+def swap_z(rows):
+    return lax.ppermute(rows, "ty", Z_PAIRS)
+
+
+def swap_chip(rows):
+    return lax.ppermute(rows, "ty", CHIP_PAIRS)
+
+
+def swap_x(to_east, to_west):
     east = [(i, (i + 1) % 16) for i in range(16)]
     west = [((i + 1) % 16, i) for i in range(16)]
-    z_in = lax.ppermute(na, "ty", z_pairs)
-    chip_in = lax.ppermute(nb, "ty", chip_pairs)
-    left_in = lax.ppermute(edges, "tx", east)
-    right_in = lax.ppermute(edges, "tx", west)
-    return z_in, chip_in, left_in, right_in
+    return lax.ppermute(to_east, "tx", east), lax.ppermute(to_west, "tx", west)
 
 
 def on_device(spectra, sea_mask, currents, sea_depth, slopes, piece_offset, piece_count):
     flat = spectra.reshape(4 * BINS, 128)
-    pieces = call(pieces_kernel, shape(128, 128), "pieces", [pltpu.VMEM((128, 128), f32)])(
+    pieces = call(pieces_kernel, shape(128, 128), [pltpu.VMEM((128, 128), f32)], 60)(
         currents, sea_depth.reshape(1, 1024), slopes, piece_offset, piece_count
     )
-    na, nb, edges = call(planes_kernel, (PLANE, PLANE, EDGES), "planes")(flat, sea_mask)
-    z_in, chip_in, left_in, right_in = exchange(na, nb, edges)
+    pieces, sea_mask = lax.optimization_barrier((pieces, sea_mask))
+    na, nb, edges, to_east, to_west = call(planes_kernel, (PLANE, PLANE, EDGES, SENDS, SENDS), limit=8)(flat, sea_mask)
+    z_in = swap_z(na)
+    chip_in = swap_chip(nb)
+    left_in, right_in = swap_x(to_east, to_west)
     arrived = lax.all_to_all(pieces, ("ty", "tx"), split_axis=0, concat_axis=0, tiled=True)
     per_frequency = shape(NF, 8, 128)
     speeds = call(
-        fields_kernel,
-        (per_frequency,) * 4 + (shape(8, 128),) * 3 + (shape(2, 16, 128), shape(2, 8, 128)),
-        "fields",
+        fields_kernel, (per_frequency,) * 4 + (shape(8, 128),) * 3 + (shape(2, 16, 128), shape(2, 8, 128)), limit=12
     )(arrived, piece_count, sea_mask, chip_in, z_in, left_in, right_in, SIGMA_ROWS, SIGMA_PACKED)
-    na, nb, own_edges = call(
-        functools.partial(step_kernel, False), (PLANE, PLANE, EDGES), "step_one", STEP_SCRATCH
-    )(na, nb, z_in, chip_in, edges, left_in, right_in, *speeds, COSINE, SINE)
-    z_in, chip_in, left_in, right_in = exchange(na, nb, own_edges)
-    out = call(functools.partial(step_kernel, True), shape(4 * BINS, 128), "step_two", STEP_SCRATCH)(
-        na, nb, z_in, chip_in, own_edges, left_in, right_in, *speeds, COSINE, SINE
-    )
+    common = (*speeds, COSINE, SINE)
+    new_a, fix = step(False, True, False, False, z_in, na, nb, edges, left_in, right_in, *common)
+    z_in = swap_z(new_a)
+    new_b, edges, to_east, to_west = step(True, False, True, False, chip_in, na, nb, fix, *common, new_a)
+    chip_in = swap_chip(new_b)
+    left_in, right_in = swap_x(to_east, to_west)
+    end_b, fix = step(True, True, False, False, chip_in, new_a, new_b, edges, left_in, right_in, *common)
+    (out,) = step(False, False, False, True, z_in, new_a, new_b, fix, *common, end_b)
     return out.reshape(spectra.shape)
 
 

time: 76.6 us -> 70.8 us (0.924)
  waiting for transfers between devices: 14.2 us -> 6.58 us
  starting transfers between devices: 15 us -> 18.4 us
  blocking collectives: 19.3 us -> 16.4 us
  Pallas kernels: 25.3 us -> 26.7 us
    ppermute x8, waiting for transfers between devices: 14.2 us -> 6.58 us  [the longest x2 4.83 us: swap_z(): return lax.ppermute(rows, 'ty', Z_PAIRS)]
    ppermute x8, starting transfers between devices: 15 us -> 18.4 us  [the longest x2 8.15 us: swap_x(): lax.ppermute(to_west, 'tx', west)]
    all_to_all x1, blocking collectives: 19.3 us -> 16.4 us  [on_device(): lax.all_to_all(pieces, ('ty', 'tx'), split_axis=0, concat_axis=0, tiled=T...]
    pallas_call x4 -> x6, Pallas kernels: 22.6 us -> 24 us  [the longest x4 20.1 us: step(): call(functools.partial(step_kernel, high, make_fix, pack, last), out, scr...]
    unnamed x22 -> x16, local copies, waits for them, and re-layouts: 2.48 us -> 2.46 us
  transfers between devices with their start and end apart: 8 -> 8, of which waited for: 3 -> 2; matrix products, arithmetic and copies ran while one was open for 0% -> 0% of each run, Pallas kernels for 1% -> 8%
where the time goes in v3:
time: 70.8 us; the launch traced here: 70.6 us
  Pallas kernels  26.7 us (38%)
  starting transfers between devices  18.4 us (26%)
  blocking collectives  16.4 us (23%)
  waiting for transfers between devices  6.58 us (9%)
  local copies, waits for them, and re-layouts  2.46 us (3%)
    pallas_call x4, Pallas kernels, step(): call(functools.partial(step_kernel, high, make_fix, pack, last), out, scr...  20.1 us
    all_to_all x1, blocking collectives, on_device(): lax.all_to_all(pieces, ('ty', 'tx'), split_axis=0, concat_axis=0, tiled=T...  16.4 us
    ppermute x2, starting transfers between devices, swap_x(): lax.ppermute(to_west, 'tx', west)  8.15 us
    ppermute x2, starting transfers between devices, swap_z(): return lax.ppermute(rows, 'ty', Z_PAIRS)  7.28 us
    ppermute x2, waiting for transfers between devices, swap_z(): return lax.ppermute(rows, 'ty', Z_PAIRS)  4.83 us
    pallas_call x1, Pallas kernels, on_device(): call(fields_kernel, (per_frequency,) * 4 + (shape(8, 128),) * 3 + (shape(...  2.65 us
    unnamed x16, local copies, waits for them, and re-layouts  2.46 us
    pallas_call x1, Pallas kernels, on_device(): call(pieces_kernel, shape(128, 128), [pltpu.VMEM((128, 128), f32)], 60)  1.99 us
  transfers between devices with their start and end apart: 8, of which 2 were waited for; matrix products, arithmetic and copies ran while one was open for 0% of the time, Pallas kernels for 8%

profile of v3, /device:TPU:1, one launch (start us, length us, event | category | flops | bytes accessed | tf_op | source)
XLA Modules:
  0.0 70.6 jit_solution(1363109064489138697)
XLA Ops:
  0.0 2.0 %shard_map.109 = f32[128,128]{1,0:T(8,128)} custom-call(f32[2,1024]{1,0:T(2,128)} %currents.1, f32[1,1024]{1,0:T(1,128)} %bitcast.10, f32[2,1024]{1,0:T(2,128)} %slopes.1, s32[128,128]{1,0:T(8,128)} %offset.1, s32[128,128]{1,0:T(8,128)} %count.3), custom_call_target="tpu_custom_call" | custom-call | flops 2000000 | bytes 4000000 | tf_op jit(solution)/shard_map/pallas_call | solution.py:519
  2.0 1.7 %copy-done = f32[36,36,4,128]{3,2,1,0:T(4,128)S(1)} copy-done((f32[36,36,4,128]{3,2,1,0:T(4,128)S(1)}, f32[36,36,4,128]{3,2,1,0:T(4,128)}, u32[]{:S(2)}) %copy-start) | copy-done | bytes 2654232
  3.7 0.7 copy-done.6
  4.4 1.9 %shard_map.110 = (f32[2,1304,128]{2,1,0:T(8,128)S(1)}, f32[2,1304,128]{2,1,0:T(8,128)S(1)}, f32[9,40,128]{2,1,0:T(8,128)S(1)}, f32[3,48,128]{2,1,0:T(8,128)S(1)}, f32[3,48,128]{2,1,0:T(8,128)S(1)}) custom-call(f32[5184,128]{1,0:T(8,128)S(1)} %bitcast.7, s32[4,128]{1,0:T(4,128)S(1)} %copy-done.6), custom_call_target="tpu_custom_call" | custom-call | flops 2000000 | bytes 4000000 | tf_op jit(solution)/shard_map/pallas_call | solution.py:523
  6.4 4.9 %collective-permute-start = (f32[2,1304,128]{2,1,0:T(8,128)S(1)}, f32[2,1304,128]{2,1,0:T(8,128)S(1)}, u32[]{:S(2)}, u32[]{:S(2)}) collective-permute-start(f32[2,1304,128]{2,1,0:T(8,128)S(1)} %get-tuple-element.30.na), channel_id=1, source_target_pairs={{16,32},{32,16},{48,64},{64,48},{80,96},{96,80},{17,33},{33,17},{4... | collective-permute-start | bytes 4005896 | tf_op jit(solution)/shard_map/ppermute | solution.py:504
  11.3 0.1 collective-permute-start.3
  11.4 1.4 %collective-permute-start.1 = (f32[3,48,128]{2,1,0:T(8,128)S(1)}, f32[3,48,128]{2,1,0:T(8,128)S(1)}, u32[]{:S(2)}, u32[]{:S(2)}) collective-permute-start(f32[3,48,128]{2,1,0:T(8,128)S(1)} %get-tuple-element.33), channel_id=1, source_target_pairs={{0,1},{1,2},{2,3},{3,4},{4,5},{5,6},{6,7},{7,8},{8,9},{9,10},{10,1... | collective-permute-start | bytes 221192 | tf_op jit(solution)/shard_map/ppermute | solution.py:514
  12.7 3.7 %collective-permute-start.2 = (f32[3,48,128]{2,1,0:T(8,128)S(1)}, f32[3,48,128]{2,1,0:T(8,128)S(1)}, u32[]{:S(2)}, u32[]{:S(2)}) collective-permute-start(f32[3,48,128]{2,1,0:T(8,128)S(1)} %get-tuple-element.34), channel_id=1, source_target_pairs={{1,0},{2,1},{3,2},{4,3},{5,4},{6,5},{7,6},{8,7},{9,8},{10,9},{11,1... | collective-permute-start | bytes 221192 | tf_op jit(solution)/shard_map/ppermute | solution.py:514
  16.5 16.4 %all_to_all.11 = f32[128,1,128]{2,1,0:T(1,128)S(1)} all-to-all(f32[128,1,128]{2,1,0:T(1,128)S(1)} %bitcast.9), channel_id=1, replica_groups=mesh['ty'=8,'tx'=16] {'ty','tx'}, dimensions={0} | all-to-all | bytes 131072 | tf_op jit(solution)/shard_map/all_to_all | solution.py:527
  32.8 0.0 collective-permute-done.1.left_in.refs_1_
  32.9 0.0 collective-permute-done.2.right_in.refs_2_
  32.9 0.0 copy-start.1
  32.9 0.0 copy-start.2
  32.9 2.7 %shard_map.111 = (f32[36,8,128]{2,1,0:T(8,128)S(1)}, f32[36,8,128]{2,1,0:T(8,128)S(1)}, f32[36,8,128]{2,1,0:T(8,128)S(1)}, f32[36,8,128]{2,1,0:T(8,128)S(1)}, f3...) custom-call(f32[128,128]{1,0:T(8,128)S(1)} %bitcast.8, ...), custom_call_target="tpu_custom_call" | custom-call | flops 2000000 | bytes 4000000 | tf_op jit(solution)/shard_map/pallas_call | solution.py:529
  35.6 5.4 %shard_map.112 = (f32[2,1304,128]{2,1,0:T(8,128)S(1)}, f32[9,40,128]{2,1,0:T(8,128)S(1)}) custom-call(f32[2,1304,128]{2,1,0:T(8,128)S(1)} %collective-permute-done.z_in.halo, f32[2,1304,128]{2,1,0:T(8,128)S(1)} %get-tuple-element.30.na, f32[2,1304,128]{2,1,0:T(8,128)S(1)} %get-tuple-element.31.nb, f32[9,40,128]{2,1,0:T(8,128)S(1)} %get-tuple-element.32.refs_0_, ...), custom_call_target="tpu_custom_call" | custom-call | flops 2000000 | bytes 4000000 | tf_op jit(solution)/shard_map/pallas_call | solution.py:496
  41.0 5.1 %shard_map.113 = (f32[2,1304,128]{2,1,0:T(8,128)S(1)}, f32[9,40,128]{2,1,0:T(8,128)S(1)}, f32[3,48,128]{2,1,0:T(8,128)S(1)}, f32[3,48,128]{2,1,0:T(8,128)S(1)}) custom-call(f32[2,1304,128]{2,1,0:T(8,128)S(1)} %collective-permute-done.3.chip_in.halo, f32[2,1304,128]{2,1,0:T(8,128)S(1)} %get-tuple-element.30.na, f32[2,1304,128]{2,1,0:T(8,128)S(1)} %get-tuple-element.31.nb, ...), custom_call_target="tpu_custom_call" | custom-call | flops 2000000 | bytes 4000000 | tf_op jit(solution)/shard_map/pallas_call | solution.py:496
  46.1 1.1 %collective-permute-start.5 = (f32[2,1304,128]{2,1,0:T(8,128)S(1)}, f32[2,1304,128]{2,1,0:T(8,128)S(1)}, u32[]{:S(2)}, u32[]{:S(2)}) collective-permute-start(f32[2,1304,128]{2,1,0:T(8,128)S(1)} %get-tuple-element.47.nb), channel_id=1, source_target_pairs={{0,16},{16,0},{32,48},{48,32},{64,80},{80,64},{96,112},{112,96},{1... | collective-permute-start | bytes 4005896 | tf_op jit(solution)/shard_map/ppermute | solution.py:508
  47.2 2.4 %collective-permute-start.4 = (f32[2,1304,128]{2,1,0:T(8,128)S(1)}, f32[2,1304,128]{2,1,0:T(8,128)S(1)}, u32[]{:S(2)}, u32[]{:S(2)}) collective-permute-start(f32[2,1304,128]{2,1,0:T(8,128)S(1)} %get-tuple-element.45.refs_12_.na), channel_id=1, source_target_pairs={{16,32},{32,16},{48,64},{64,48},{80,96},{96,80},{17,33},{33,17},{4... | collective-permute-start | bytes 4005896 | tf_op jit(solution)/shard_map/ppermute | solution.py:504
  49.5 0.4 collective-permute-start.6
  49.9 4.4 %collective-permute-start.7 = (f32[3,48,128]{2,1,0:T(8,128)S(1)}, f32[3,48,128]{2,1,0:T(8,128)S(1)}, u32[]{:S(2)}, u32[]{:S(2)}) collective-permute-start(f32[3,48,128]{2,1,0:T(8,128)S(1)} %get-tuple-element.50), channel_id=1, source_target_pairs={{1,0},{2,1},{3,2},{4,3},{5,4},{6,5},{7,6},{8,7},{9,8},{10,9},{11,1... | collective-permute-start | bytes 221192 | tf_op jit(solution)/shard_map/ppermute | solution.py:514
  54.4 1.7 %collective-permute-done.6.refs_1_ = f32[3,48,128]{2,1,0:T(8,128)S(1)} collective-permute-done((f32[3,48,128]{2,1,0:T(8,128)S(1)}, f32[3,48,128]{2,1,0:T(8,128)S(1)}, u32[]{:S(2)}, u32[]{:S(2)}) %collective-permute-start.6) | collective-permute-done | bytes 73760 | tf_op jit(solution)/shard_map/ppermute | solution.py:514
  56.1 5.4 %shard_map.114 = (f32[2,1304,128]{2,1,0:T(8,128)S(1)}, f32[9,40,128]{2,1,0:T(8,128)S(1)}) custom-call(f32[2,1304,128]{2,1,0:T(8,128)S(1)} %collective-permute-done.5.halo, f32[2,1304,128]{2,1,0:T(8,128)S(1)} %get-tuple-element.45.refs_12_.na, f32[2,1304,128]{2,1,0:T(8,128)S(1)} %get-tuple-element.47.nb, f32[9,40,128]{2,1,0:T(8,128)S(1)} %get-tuple-element.48.refs_0_, ...), custom_call_target="tpu_custom_call" | custom-call | flops 2000000 | bytes 4000000 | tf_op jit(solution)/shard_map/pallas_call | solution.py:496
  61.5 4.8 %collective-permute-done.4.halo = f32[2,1304,128]{2,1,0:T(8,128)S(1)} collective-permute-done((f32[2,1304,128]{2,1,0:T(8,128)S(1)}, f32[2,1304,128]{2,1,0:T(8,128)S(1)}, u32[]{:S(2)}, u32[]{:S(2)}) %collective-permute-start.4) | collective-permute-done | bytes 1335328 | tf_op jit(solution)/shard_map/ppermute | solution.py:504
  66.3 4.3 %shard_map.115 = f32[5184,128]{1,0:T(8,128)} custom-call(f32[2,1304,128]{2,1,0:T(8,128)S(1)} %collective-permute-done.4.halo, f32[2,1304,128]{2,1,0:T(8,128)S(1)} %get-tuple-element.45.refs_12_.na, f32[2,1304,128]{2,1,0:T(8,128)S(1)} %get-tuple-element.47.nb, f32[9,40,128]{2,1,0:T(8,128)S(1)} %get-tuple-element.51.refs_0_, ...), custom_call_target="tpu_custom_call" | custom-call | flops 2000000 | bytes 4000000 | tf_op jit(solution)/shard_map/pallas_call | solution.py:496
  (16 shorter events, 0.0 us)
Async XLA Ops:
  2.0 1.7 %copy-start = (f32[36,36,4,128]{3,2,1,0:T(4,128)S(1)}, f32[36,36,4,128]{3,2,1,0:T(4,128)}, u32[]{:S(2)}) copy-start(f32[36,36,4,128]{3,2,1,0:T(4,128)} %param.11) | copy-start | bytes 7962628
  3.7 0.7 copy-start.6
  4.4 12.0 %copy-start.7 = (f32[128,128]{1,0:T(8,128)S(1)}, f32[128,128]{1,0:T(8,128)}, u32[]{:S(2)}) copy-start(f32[128,128]{1,0:T(8,128)} %shard_map.109) | copy-start | bytes 196612
  4.4 28.4 %copy-start.3 = (s32[128,128]{1,0:T(8,128)S(1)}, s32[128,128]{1,0:T(8,128)}, u32[]{:S(2)}) copy-start(s32[128,128]{1,0:T(8,128)} %count.3) | copy-start | bytes 196612
  4.4 28.5 %copy-start.4 = (f32[36,128]{1,0:T(8,128)S(1)}, f32[36,128]{1,0:T(8,128)}, u32[]{:S(2)}) copy-start(f32[36,128]{1,0:T(8,128)} %constant.8.clone.sigma_rows) | copy-start | bytes 55300
  4.4 28.5 %copy-start.5 = (f32[16,128]{1,0:T(8,128)S(1)}, f32[16,128]{1,0:T(8,128)}, u32[]{:S(2)}) copy-start(f32[16,128]{1,0:T(8,128)} %constant.9.clone.sigma_packed) | copy-start | bytes 24580
  6.4 26.5 %collective-permute-start = (f32[2,1304,128]{2,1,0:T(8,128)S(1)}, f32[2,1304,128]{2,1,0:T(8,128)S(1)}, u32[]{:S(2)}, u32[]{:S(2)}) collective-permute-start(f32[2,1304,128]{2,1,0:T(8,128)S(1)} %get-tuple-element.30.na), channel_id=1, source_target_pairs={{16,32},{32,16},{48,64},{64,48},{80,96},{96,80},{17,33},{33,17},{4... | collective-permute-start | bytes 4005896 | tf_op jit(solution)/shard_map/ppermute | solution.py:504
  11.3 21.6 %collective-permute-start.3 = (f32[2,1304,128]{2,1,0:T(8,128)S(1)}, f32[2,1304,128]{2,1,0:T(8,128)S(1)}, u32[]{:S(2)}, u32[]{:S(2)}) collective-permute-start(f32[2,1304,128]{2,1,0:T(8,128)S(1)} %get-tuple-element.31.nb), channel_id=1, source_target_pairs={{0,16},{16,0},{32,48},{48,32},{64,80},{80,64},{96,112},{112,96},{1... | collective-permute-start | bytes 4005896 | tf_op jit(solution)/shard_map/ppermute | solution.py:508
  11.4 21.5 %collective-permute-start.1 = (f32[3,48,128]{2,1,0:T(8,128)S(1)}, f32[3,48,128]{2,1,0:T(8,128)S(1)}, u32[]{:S(2)}, u32[]{:S(2)}) collective-permute-start(f32[3,48,128]{2,1,0:T(8,128)S(1)} %get-tuple-element.33), channel_id=1, source_target_pairs={{0,1},{1,2},{2,3},{3,4},{4,5},{5,6},{6,7},{7,8},{8,9},{9,10},{10,1... | collective-permute-start | bytes 221192 | tf_op jit(solution)/shard_map/ppermute | solution.py:514
  12.7 20.1 %collective-permute-start.2 = (f32[3,48,128]{2,1,0:T(8,128)S(1)}, f32[3,48,128]{2,1,0:T(8,128)S(1)}, u32[]{:S(2)}, u32[]{:S(2)}) collective-permute-start(f32[3,48,128]{2,1,0:T(8,128)S(1)} %get-tuple-element.34), channel_id=1, source_target_pairs={{1,0},{2,1},{3,2},{4,3},{5,4},{6,5},{7,6},{8,7},{9,8},{10,9},{11,1... | collective-permute-start | bytes 221192 | tf_op jit(solution)/shard_map/ppermute | solution.py:514
  32.9 2.7 %copy-start.1 = (f32[48,128]{1,0:T(8,128)S(1)}, f32[48,128]{1,0:T(8,128)}, u32[]{:S(2)}) copy-start(f32[48,128]{1,0:T(8,128)} %constant.11.clone.refs_13_.refs_11_) | copy-start | bytes 73732
  32.9 2.7 %copy-start.2 = (f32[48,128]{1,0:T(8,128)S(1)}, f32[48,128]{1,0:T(8,128)}, u32[]{:S(2)}) copy-start(f32[48,128]{1,0:T(8,128)} %constant.10.clone.refs_12_.refs_10_) | copy-start | bytes 73732
  46.1 10.0 %collective-permute-start.5 = (f32[2,1304,128]{2,1,0:T(8,128)S(1)}, f32[2,1304,128]{2,1,0:T(8,128)S(1)}, u32[]{:S(2)}, u32[]{:S(2)}) collective-permute-start(f32[2,1304,128]{2,1,0:T(8,128)S(1)} %get-tuple-element.47.nb), channel_id=1, source_target_pairs={{0,16},{16,0},{32,48},{48,32},{64,80},{80,64},{96,112},{112,96},{1... | collective-permute-start | bytes 4005896 | tf_op jit(solution)/shard_map/ppermute | solution.py:508
  47.2 19.2 %collective-permute-start.4 = (f32[2,1304,128]{2,1,0:T(8,128)S(1)}, f32[2,1304,128]{2,1,0:T(8,128)S(1)}, u32[]{:S(2)}, u32[]{:S(2)}) collective-permute-start(f32[2,1304,128]{2,1,0:T(8,128)S(1)} %get-tuple-element.45.refs_12_.na), channel_id=1, source_target_pairs={{16,32},{32,16},{48,64},{64,48},{80,96},{96,80},{17,33},{33,17},{4... | collective-permute-start | bytes 4005896 | tf_op jit(solution)/shard_map/ppermute | solution.py:504
  49.5 6.6 %collective-permute-start.6 = (f32[3,48,128]{2,1,0:T(8,128)S(1)}, f32[3,48,128]{2,1,0:T(8,128)S(1)}, u32[]{:S(2)}, u32[]{:S(2)}) collective-permute-start(f32[3,48,128]{2,1,0:T(8,128)S(1)} %get-tuple-element.49), channel_id=1, source_target_pairs={{0,1},{1,2},{2,3},{3,4},{4,5},{5,6},{6,7},{7,8},{8,9},{9,10},{10,1... | collective-permute-start | bytes 221192 | tf_op jit(solution)/shard_map/ppermute | solution.py:514
  49.9 6.2 %collective-permute-start.7 = (f32[3,48,128]{2,1,0:T(8,128)S(1)}, f32[3,48,128]{2,1,0:T(8,128)S(1)}, u32[]{:S(2)}, u32[]{:S(2)}) collective-permute-start(f32[3,48,128]{2,1,0:T(8,128)S(1)} %get-tuple-element.50), channel_id=1, source_target_pairs={{1,0},{2,1},{3,2},{4,3},{5,4},{6,5},{7,6},{8,7},{9,8},{10,9},{11,1... | collective-permute-start | bytes 221192 | tf_op jit(solution)/shard_map/ppermute | solution.py:514

commit v4 on v3

--- a/solution.py
+++ b/solution.py
@@ -66,30 +66,61 @@
     return lax.rem(lax.axis_index("ty"), 2)
 
 
-def planes_kernel(spectra, sea, na, nb, edges, to_east, to_west):
+def prepare_kernel(
+    source_ref, sea, currents, depth, slopes, offset, count,
+    na_out, nb_out, edges, to_east, to_west, pieces,
+    rows, spectra, na, nb, arrived, sent,
+):
+    def fetch(g):
+        part = pl.ds(pl.multiple_of(576 * g, 8), 576)
+        return pltpu.make_async_copy(source_ref.at[part, :], spectra.at[part, :], arrived.at[g])
+
+    def send(half, g):
+        part = pl.ds(pl.multiple_of(144 * g, 8), 144)
+        held, out = ((na, na_out), (nb, nb_out))[half]
+        return pltpu.make_async_copy(held.at[:, part, :], out.at[:, part, :], sent.at[half, g])
+
+    def send_tail(half):
+        held, out = ((na, na_out), (nb, nb_out))[half]
+        return pltpu.make_async_copy(
+            held.at[:, pl.ds(BINS, 8), :], out.at[:, pl.ds(BINS, 8), :], sent.at[half, GROUPS]
+        )
+
+    for g in range(GROUPS):
+        fetch(g).start()
+    pieces_kernel(currents, depth, slopes, offset, count, pieces, rows)
     flip = parity()
     mask = sea[...].astype(f32)
     tail = jnp.concatenate([mask, jnp.zeros((4, 128), f32)], 0)
     for part in range(2):
         na[part, pl.ds(BINS, 8), :] = tail
         nb[part, pl.ds(BINS, 8), :] = tail
+    send_tail(0).start()
+    send_tail(1).start()
     to_east[0, pl.ds(40, 8), :] = tail
     to_west[0, pl.ds(40, 8), :] = tail
     row_mask = [jnp.broadcast_to(jnp.where(flip == 1, mask[3 - j : 4 - j], mask[j : j + 1]), (8, 128)) for j in range(4)]
     source = [jnp.where(flip == 1, 3 - j, j) for j in range(4)]
 
     def group(g, carry):
+        fetch(g).wait()
         for k in range(18):
             base = 144 * g + 8 * k
             for j in range(4):
                 (na if j < 2 else nb)[j % 2, pl.ds(base, 8), :] = (
                     spectra[pl.ds(4 * base + source[j], 8, stride=4), :] * row_mask[j]
                 )
+        send(0, g).start()
+        send(1, g).start()
         return carry
 
     lax.fori_loop(0, GROUPS, group, 0)
     pack_planes(na, nb, edges)
     pack_sends(edges, to_east, to_west)
+    for half in range(2):
+        send_tail(half).wait()
+        for g in range(GROUPS):
+            send(half, g).wait()
 
 
 def pack_planes(na, nb, edges):
@@ -178,10 +209,10 @@
     lane = lanes()
     total = jnp.zeros((8, 128), f32)
     for j, row in enumerate(rows):
-        moved = roll(jnp.broadcast_to(row, (8, 128)), 8 * j + 4)
-        total = jnp.where((lane >= 8 * j) & (lane < 8 * j + 8), moved, total)
-    total = total + roll(total, 32)
-    return total + roll(total, 64)
+        wide = jnp.broadcast_to(row, (8, 128))
+        for at in range(8 * j, 128, 32):
+            total = jnp.where((lane >= at) & (lane < at + 8), roll(wide, at + 4), total)
+    return total
 
 
 def faces(x, mask, axis):
@@ -516,11 +547,22 @@
 
 def on_device(spectra, sea_mask, currents, sea_depth, slopes, piece_offset, piece_count):
     flat = spectra.reshape(4 * BINS, 128)
-    pieces = call(pieces_kernel, shape(128, 128), [pltpu.VMEM((128, 128), f32)], 60)(
-        currents, sea_depth.reshape(1, 1024), slopes, piece_offset, piece_count
-    )
-    pieces, sea_mask = lax.optimization_barrier((pieces, sea_mask))
-    na, nb, edges, to_east, to_west = call(planes_kernel, (PLANE, PLANE, EDGES, SENDS, SENDS), limit=8)(flat, sea_mask)
+    hbm, vmem = (pl.BlockSpec(memory_space=kind) for kind in (pltpu.MemorySpace.HBM, pltpu.MemorySpace.VMEM))
+    na, nb, edges, to_east, to_west, pieces = call(
+        prepare_kernel,
+        (PLANE, PLANE, EDGES, SENDS, SENDS, shape(128, 128)),
+        [
+            pltpu.VMEM((128, 128), f32),
+            pltpu.VMEM((4 * BINS, 128), f32),
+            pltpu.VMEM(PLANE.shape, f32),
+            pltpu.VMEM(PLANE.shape, f32),
+            pltpu.SemaphoreType.DMA((GROUPS,)),
+            pltpu.SemaphoreType.DMA((2, GROUPS + 1)),
+        ],
+        60,
+        in_specs=[hbm] + [vmem] * 6,
+        out_specs=[hbm] * 2 + [vmem] * 4,
+    )(flat, sea_mask, currents, sea_depth.reshape(1, 1024), slopes, piece_offset, piece_count)
     z_in = swap_z(na)
     chip_in = swap_chip(nb)
     left_in, right_in = swap_x(to_east, to_west)

time: 70.8 us -> 70 us (0.989)
  local copies, waits for them, and re-layouts: 2.46 us -> 0.04 us
  Pallas kernels: 26.7 us -> 28 us
    unnamed x16 -> x18, local copies, waits for them, and re-layouts: 2.46 us -> 0.04 us
    pallas_call x2 -> x1, Pallas kernels: 3.9 us -> 5.44 us  [on_device(): call(prepare_kernel, (PLANE, PLANE, EDGES, SENDS, SENDS, shape(128, 128))...]
where the time goes in v4:
time: 70 us; the launch traced here: 69.8 us
  Pallas kernels  28 us (40%)
  starting transfers between devices  18.4 us (26%)
  blocking collectives  16.6 us (24%)
  waiting for transfers between devices  6.56 us (9%)
    pallas_call x4, Pallas kernels, step(): call(functools.partial(step_kernel, high, make_fix, pack, last), out, scr...  20.1 us
    all_to_all x1, blocking collectives, on_device(): lax.all_to_all(pieces, ('ty', 'tx'), split_axis=0, concat_axis=0, tiled=T...  16.6 us
    ppermute x2, starting transfers between devices, swap_x(): lax.ppermute(to_west, 'tx', west)  8.16 us
    ppermute x2, starting transfers between devices, swap_z(): return lax.ppermute(rows, 'ty', Z_PAIRS)  7.29 us
    pallas_call x1, Pallas kernels, on_device(): call(prepare_kernel, (PLANE, PLANE, EDGES, SENDS, SENDS, shape(128, 128))...  5.44 us
    ppermute x2, waiting for transfers between devices, swap_z(): return lax.ppermute(rows, 'ty', Z_PAIRS)  4.81 us
    pallas_call x1, Pallas kernels, on_device(): call(fields_kernel, (per_frequency,) * 4 + (shape(8, 128),) * 3 + (shape(...  2.47 us
    ppermute x2, starting transfers between devices, swap_x(): lax.ppermute(to_east, 'tx', east)  1.77 us
  transfers between devices with their start and end apart: 8, of which 2 were waited for; matrix products, arithmetic and copies ran while one was open for 0% of the time, Pallas kernels for 8%

profile of v4, /device:TPU:1, one launch (start us, length us, event | category | flops | bytes accessed | tf_op | source)
XLA Modules:
  0.0 69.8 jit_solution(8701550378587809163)
XLA Ops:
  0.0 5.4 %shard_map.109 = (f32[2,1304,128]{2,1,0:T(8,128)}, f32[2,1304,128]{2,1,0:T(8,128)}, f32[9,40,128]{2,1,0:T(8,128)}, f32[3,48,128]{2,1,0:T(8,128)}, f32[3,48,128]{2,1,0:T(8,128)}, /*index=5*/f32[128,128]{1,0:T(8,128)}) custom-call(f32[5184,128]{1,0:T(8,128)} %bitcast.8, s32[4,128]{1,0:T(4,128)} %sea.3, f32[2,1024]{1,0:T(2,128)} %currents.1, ...), custom_call_target="tpu_custom_call" | custom-call | flops 2000000 | bytes 4000000 | tf_op jit(solution)/shard_map/pallas_call | solution.py:551
  5.5 4.9 %collective-permute-start = (f32[2,1304,128]{2,1,0:T(8,128)}, f32[2,1304,128]{2,1,0:T(8,128)S(1)}, u32[]{:S(2)}, u32[]{:S(2)}) collective-permute-start(f32[2,1304,128]{2,1,0:T(8,128)} %get-tuple-element.28.na), channel_id=1, source_target_pairs={{16,32},{32,16},{48,64},{64,48},{80,96},{96,80},{17,33},{33,17},{4... | collective-permute-start | bytes 4005896 | tf_op jit(solution)/shard_map/ppermute | solution.py:535
  10.4 0.1 collective-permute-start.3
  10.5 1.4 %collective-permute-start.1 = (f32[3,48,128]{2,1,0:T(8,128)}, f32[3,48,128]{2,1,0:T(8,128)S(1)}, u32[]{:S(2)}, u32[]{:S(2)}) collective-permute-start(f32[3,48,128]{2,1,0:T(8,128)} %get-tuple-element.31), channel_id=1, source_target_pairs={{0,1},{1,2},{2,3},{3,4},{4,5},{5,6},{6,7},{7,8},{8,9},{9,10},{10,1... | collective-permute-start | bytes 221192 | tf_op jit(solution)/shard_map/ppermute | solution.py:545
  11.9 3.7 %collective-permute-start.2 = (f32[3,48,128]{2,1,0:T(8,128)}, f32[3,48,128]{2,1,0:T(8,128)S(1)}, u32[]{:S(2)}, u32[]{:S(2)}) collective-permute-start(f32[3,48,128]{2,1,0:T(8,128)} %get-tuple-element.32), channel_id=1, source_target_pairs={{1,0},{2,1},{3,2},{4,3},{5,4},{6,5},{7,6},{8,7},{9,8},{10,9},{11,1... | collective-permute-start | bytes 221192 | tf_op jit(solution)/shard_map/ppermute | solution.py:545
  15.6 16.6 %all_to_all.11 = f32[128,1,128]{2,1,0:T(1,128)S(1)} all-to-all(f32[128,1,128]{2,1,0:T(1,128)} %bitcast.9), channel_id=1, replica_groups=mesh['ty'=8,'tx'=16] {'ty','tx'}, dimensions={0} | all-to-all | bytes 131072 | tf_op jit(solution)/shard_map/all_to_all | solution.py:569
  32.2 0.0 collective-permute-done.1.left_in.refs_1_
  32.2 0.0 collective-permute-done.2.right_in.refs_2_
  32.2 0.0 collective-permute-done.z_in.halo
  32.2 0.0 copy-start
  32.2 0.0 copy-start.2
  32.3 0.0 copy-start.3
  32.3 2.5 %shard_map.110 = (f32[36,8,128]{2,1,0:T(8,128)S(1)}, f32[36,8,128]{2,1,0:T(8,128)S(1)}, f32[36,8,128]{2,1,0:T(8,128)S(1)}, f32[36,8,128]{2,1,0:T(8,128)S(1)}, f3...) custom-call(f32[128,128]{1,0:T(8,128)S(1)} %bitcast.7, ...), custom_call_target="tpu_custom_call" | custom-call | flops 2000000 | bytes 4000000 | tf_op jit(solution)/shard_map/pallas_call | solution.py:571
  34.8 5.4 %shard_map.111 = (f32[2,1304,128]{2,1,0:T(8,128)S(1)}, f32[9,40,128]{2,1,0:T(8,128)S(1)}) custom-call(f32[2,1304,128]{2,1,0:T(8,128)S(1)} %collective-permute-done.z_in.halo, f32[2,1304,128]{2,1,0:T(8,128)S(1)} %copy-done, f32[2,1304,128]{2,1,0:T(8,128)S(1)} %copy-done.1, f32[9,40,128]{2,1,0:T(8,128)S(1)} %copy-done.5, ...), custom_call_target="tpu_custom_call" | custom-call | flops 2000000 | bytes 4000000 | tf_op jit(solution)/shard_map/pallas_call | solution.py:527
  40.2 5.1 %shard_map.112 = (f32[2,1304,128]{2,1,0:T(8,128)S(1)}, f32[9,40,128]{2,1,0:T(8,128)S(1)}, f32[3,48,128]{2,1,0:T(8,128)S(1)}, f32[3,48,128]{2,1,0:T(8,128)S(1)}) custom-call(f32[2,1304,128]{2,1,0:T(8,128)S(1)} %collective-permute-done.3.chip_in.halo, f32[2,1304,128]{2,1,0:T(8,128)S(1)} %copy-done, f32[2,1304,128]{2,1,0:T(8,128)S(1)} %copy-done.1, ...), custom_call_target="tpu_custom_call" | custom-call | flops 2000000 | bytes 4000000 | tf_op jit(solution)/shard_map/pallas_call | solution.py:527
  45.3 1.1 %collective-permute-start.5 = (f32[2,1304,128]{2,1,0:T(8,128)S(1)}, f32[2,1304,128]{2,1,0:T(8,128)S(1)}, u32[]{:S(2)}, u32[]{:S(2)}) collective-permute-start(f32[2,1304,128]{2,1,0:T(8,128)S(1)} %get-tuple-element.45.nb), channel_id=1, source_target_pairs={{0,16},{16,0},{32,48},{48,32},{64,80},{80,64},{96,112},{112,96},{1... | collective-permute-start | bytes 4005896 | tf_op jit(solution)/shard_map/ppermute | solution.py:539
  46.4 2.4 %collective-permute-start.4 = (f32[2,1304,128]{2,1,0:T(8,128)S(1)}, f32[2,1304,128]{2,1,0:T(8,128)S(1)}, u32[]{:S(2)}, u32[]{:S(2)}) collective-permute-start(f32[2,1304,128]{2,1,0:T(8,128)S(1)} %get-tuple-element.43.refs_12_.na), channel_id=1, source_target_pairs={{16,32},{32,16},{48,64},{64,48},{80,96},{96,80},{17,33},{33,17},{4... | collective-permute-start | bytes 4005896 | tf_op jit(solution)/shard_map/ppermute | solution.py:535
  48.7 0.4 collective-permute-start.6
  49.1 4.4 %collective-permute-start.7 = (f32[3,48,128]{2,1,0:T(8,128)S(1)}, f32[3,48,128]{2,1,0:T(8,128)S(1)}, u32[]{:S(2)}, u32[]{:S(2)}) collective-permute-start(f32[3,48,128]{2,1,0:T(8,128)S(1)} %get-tuple-element.48), channel_id=1, source_target_pairs={{1,0},{2,1},{3,2},{4,3},{5,4},{6,5},{7,6},{8,7},{9,8},{10,9},{11,1... | collective-permute-start | bytes 221192 | tf_op jit(solution)/shard_map/ppermute | solution.py:545
  53.6 1.7 %collective-permute-done.6.refs_1_ = f32[3,48,128]{2,1,0:T(8,128)S(1)} collective-permute-done((f32[3,48,128]{2,1,0:T(8,128)S(1)}, f32[3,48,128]{2,1,0:T(8,128)S(1)}, u32[]{:S(2)}, u32[]{:S(2)}) %collective-permute-start.6) | collective-permute-done | bytes 73760 | tf_op jit(solution)/shard_map/ppermute | solution.py:545
  55.3 0.0 collective-permute-done.7.refs_2_
  55.3 5.4 %shard_map.113 = (f32[2,1304,128]{2,1,0:T(8,128)S(1)}, f32[9,40,128]{2,1,0:T(8,128)S(1)}) custom-call(f32[2,1304,128]{2,1,0:T(8,128)S(1)} %collective-permute-done.5.halo, f32[2,1304,128]{2,1,0:T(8,128)S(1)} %get-tuple-element.43.refs_12_.na, f32[2,1304,128]{2,1,0:T(8,128)S(1)} %get-tuple-element.45.nb, f32[9,40,128]{2,1,0:T(8,128)S(1)} %get-tuple-element.46.refs_0_, ...), custom_call_target="tpu_custom_call" | custom-call | flops 2000000 | bytes 4000000 | tf_op jit(solution)/shard_map/pallas_call | solution.py:527
  60.7 4.8 %collective-permute-done.4.halo = f32[2,1304,128]{2,1,0:T(8,128)S(1)} collective-permute-done((f32[2,1304,128]{2,1,0:T(8,128)S(1)}, f32[2,1304,128]{2,1,0:T(8,128)S(1)}, u32[]{:S(2)}, u32[]{:S(2)}) %collective-permute-start.4) | collective-permute-done | bytes 1335328 | tf_op jit(solution)/shard_map/ppermute | solution.py:535
  65.5 4.3 %shard_map.114 = f32[5184,128]{1,0:T(8,128)} custom-call(f32[2,1304,128]{2,1,0:T(8,128)S(1)} %collective-permute-done.4.halo, f32[2,1304,128]{2,1,0:T(8,128)S(1)} %get-tuple-element.43.refs_12_.na, f32[2,1304,128]{2,1,0:T(8,128)S(1)} %get-tuple-element.45.nb, f32[9,40,128]{2,1,0:T(8,128)S(1)} %get-tuple-element.49.refs_0_, ...), custom_call_target="tpu_custom_call" | custom-call | flops 2000000 | bytes 4000000 | tf_op jit(solution)/shard_map/pallas_call | solution.py:527
  (17 shorter events, 0.0 us)
Async XLA Ops:
  0.0 32.2 %copy-start.4 = (s32[128,128]{1,0:T(8,128)S(1)}, s32[128,128]{1,0:T(8,128)}, u32[]{:S(2)}) copy-start(s32[128,128]{1,0:T(8,128)} %count.3) | copy-start | bytes 196612
  0.0 32.2 %copy-start.6 = (f32[36,128]{1,0:T(8,128)S(1)}, f32[36,128]{1,0:T(8,128)}, u32[]{:S(2)}) copy-start(f32[36,128]{1,0:T(8,128)} %constant.8.clone.sigma_rows) | copy-start | bytes 55300
  0.0 32.2 %copy-start.7 = (f32[16,128]{1,0:T(8,128)S(1)}, f32[16,128]{1,0:T(8,128)}, u32[]{:S(2)}) copy-start(f32[16,128]{1,0:T(8,128)} %constant.9.clone.sigma_packed) | copy-start | bytes 24580
  0.0 32.2 %copy-start.8 = (s32[4,128]{1,0:T(4,128)S(1)}, s32[4,128]{1,0:T(4,128)}, u32[]{:S(2)}) copy-start(s32[4,128]{1,0:T(4,128)} %sea.3) | copy-start | bytes 6148
  5.5 26.7 %collective-permute-start = (f32[2,1304,128]{2,1,0:T(8,128)}, f32[2,1304,128]{2,1,0:T(8,128)S(1)}, u32[]{:S(2)}, u32[]{:S(2)}) collective-permute-start(f32[2,1304,128]{2,1,0:T(8,128)} %get-tuple-element.28.na), channel_id=1, source_target_pairs={{16,32},{32,16},{48,64},{64,48},{80,96},{96,80},{17,33},{33,17},{4... | collective-permute-start | bytes 4005896 | tf_op jit(solution)/shard_map/ppermute | solution.py:535
  10.4 21.8 %collective-permute-start.3 = (f32[2,1304,128]{2,1,0:T(8,128)}, f32[2,1304,128]{2,1,0:T(8,128)S(1)}, u32[]{:S(2)}, u32[]{:S(2)}) collective-permute-start(f32[2,1304,128]{2,1,0:T(8,128)} %get-tuple-element.29.nb), channel_id=1, source_target_pairs={{0,16},{16,0},{32,48},{48,32},{64,80},{80,64},{96,112},{112,96},{1... | collective-permute-start | bytes 4005896 | tf_op jit(solution)/shard_map/ppermute | solution.py:539
  10.5 21.7 %collective-permute-start.1 = (f32[3,48,128]{2,1,0:T(8,128)}, f32[3,48,128]{2,1,0:T(8,128)S(1)}, u32[]{:S(2)}, u32[]{:S(2)}) collective-permute-start(f32[3,48,128]{2,1,0:T(8,128)} %get-tuple-element.31), channel_id=1, source_target_pairs={{0,1},{1,2},{2,3},{3,4},{4,5},{5,6},{6,7},{7,8},{8,9},{9,10},{10,1... | collective-permute-start | bytes 221192 | tf_op jit(solution)/shard_map/ppermute | solution.py:545
  11.9 20.3 %collective-permute-start.2 = (f32[3,48,128]{2,1,0:T(8,128)}, f32[3,48,128]{2,1,0:T(8,128)S(1)}, u32[]{:S(2)}, u32[]{:S(2)}) collective-permute-start(f32[3,48,128]{2,1,0:T(8,128)} %get-tuple-element.32), channel_id=1, source_target_pairs={{1,0},{2,1},{3,2},{4,3},{5,4},{6,5},{7,6},{8,7},{9,8},{10,9},{11,1... | collective-permute-start | bytes 221192 | tf_op jit(solution)/shard_map/ppermute | solution.py:545
  32.2 2.5 %copy-start = (f32[2,1304,128]{2,1,0:T(8,128)S(1)}, f32[2,1304,128]{2,1,0:T(8,128)}, u32[]{:S(2)}) copy-start(f32[2,1304,128]{2,1,0:T(8,128)} %get-tuple-element.28.na) | copy-start | bytes 4005892
  32.2 2.5 %copy-start.1 = (f32[2,1304,128]{2,1,0:T(8,128)S(1)}, f32[2,1304,128]{2,1,0:T(8,128)}, u32[]{:S(2)}) copy-start(f32[2,1304,128]{2,1,0:T(8,128)} %get-tuple-element.29.nb) | copy-start | bytes 4005892
  32.2 2.5 %copy-start.2 = (f32[48,128]{1,0:T(8,128)S(1)}, f32[48,128]{1,0:T(8,128)}, u32[]{:S(2)}) copy-start(f32[48,128]{1,0:T(8,128)} %constant.11.clone.refs_13_.refs_11_) | copy-start | bytes 73732
  32.3 2.5 %copy-start.3 = (f32[48,128]{1,0:T(8,128)S(1)}, f32[48,128]{1,0:T(8,128)}, u32[]{:S(2)}) copy-start(f32[48,128]{1,0:T(8,128)} %constant.10.clone.refs_12_.refs_10_) | copy-start | bytes 73732
  32.3 2.5 %copy-start.5 = (f32[9,40,128]{2,1,0:T(8,128)S(1)}, f32[9,40,128]{2,1,0:T(8,128)}, u32[]{:S(2)}) copy-start(f32[9,40,128]{2,1,0:T(8,128)} %get-tuple-element.30.refs_0_) | copy-start | bytes 552964
  45.3 10.0 %collective-permute-start.5 = (f32[2,1304,128]{2,1,0:T(8,128)S(1)}, f32[2,1304,128]{2,1,0:T(8,128)S(1)}, u32[]{:S(2)}, u32[]{:S(2)}) collective-permute-start(f32[2,1304,128]{2,1,0:T(8,128)S(1)} %get-tuple-element.45.nb), channel_id=1, source_target_pairs={{0,16},{16,0},{32,48},{48,32},{64,80},{80,64},{96,112},{112,96},{1... | collective-permute-start | bytes 4005896 | tf_op jit(solution)/shard_map/ppermute | solution.py:539
  46.4 19.2 %collective-permute-start.4 = (f32[2,1304,128]{2,1,0:T(8,128)S(1)}, f32[2,1304,128]{2,1,0:T(8,128)S(1)}, u32[]{:S(2)}, u32[]{:S(2)}) collective-permute-start(f32[2,1304,128]{2,1,0:T(8,128)S(1)} %get-tuple-element.43.refs_12_.na), channel_id=1, source_target_pairs={{16,32},{32,16},{48,64},{64,48},{80,96},{96,80},{17,33},{33,17},{4... | collective-permute-start | bytes 4005896 | tf_op jit(solution)/shard_map/ppermute | solution.py:535
  48.7 6.6 %collective-permute-start.6 = (f32[3,48,128]{2,1,0:T(8,128)S(1)}, f32[3,48,128]{2,1,0:T(8,128)S(1)}, u32[]{:S(2)}, u32[]{:S(2)}) collective-permute-start(f32[3,48,128]{2,1,0:T(8,128)S(1)} %get-tuple-element.47), channel_id=1, source_target_pairs={{0,1},{1,2},{2,3},{3,4},{4,5},{5,6},{6,7},{7,8},{8,9},{9,10},{10,1... | collective-permute-start | bytes 221192 | tf_op jit(solution)/shard_map/ppermute | solution.py:545
  49.1 6.2 %collective-permute-start.7 = (f32[3,48,128]{2,1,0:T(8,128)S(1)}, f32[3,48,128]{2,1,0:T(8,128)S(1)}, u32[]{:S(2)}, u32[]{:S(2)}) collective-permute-start(f32[3,48,128]{2,1,0:T(8,128)S(1)} %get-tuple-element.48), channel_id=1, source_target_pairs={{1,0},{2,1},{3,2},{4,3},{5,4},{6,5},{7,6},{8,7},{9,8},{10,9},{11,1... | collective-permute-start | bytes 221192 | tf_op jit(solution)/shard_map/ppermute | solution.py:545

commit v5 on v4

--- a/solution.py
+++ b/solution.py
@@ -31,6 +31,15 @@
 HEADING = np.arange(48) % ND * (2.0 * math.pi / ND)
 COSINE = np.broadcast_to(np.cos(HEADING)[:, None], (48, 128)).astype(np.float32)
 SINE = np.broadcast_to(np.sin(HEADING)[:, None], (48, 128)).astype(np.float32)
+AT = np.arange(128)
+
+
+def shift_matrix(ahead):
+    return (AT[:, None] == (AT[None, :] + ahead) % 128).astype(np.float32)
+
+
+STENCIL = np.concatenate([3.0 * shift_matrix(0) - shift_matrix(-1), 3.0 * shift_matrix(1) - shift_matrix(2)], 1)
+STENCIL = np.concatenate([STENCIL, STENCIL], 0).astype(jnp.bfloat16)
 SIGMA = (2.0 * math.pi * first_frequency * frequency_ratio ** np.arange(64)).astype(np.float32)
 SIGMA_ROWS = np.broadcast_to(SIGMA[:NF, None], (NF, 128)).astype(np.float32)
 SIGMA_PACKED = np.where(
@@ -112,10 +121,11 @@
                 )
         send(0, g).start()
         send(1, g).start()
+        pack_group(na, nb, edges, jnp.maximum(g - 1, 0))
         return carry
 
     lax.fori_loop(0, GROUPS, group, 0)
-    pack_planes(na, nb, edges)
+    pack_group(na, nb, edges, GROUPS - 1)
     pack_sends(edges, to_east, to_west)
     for half in range(2):
         send_tail(half).wait()
@@ -123,21 +133,17 @@
             send(half, g).wait()
 
 
-def pack_planes(na, nb, edges):
+def pack_group(na, nb, edges, g):
     lane = lanes()
-
-    def group(g, carry):
-        for b, start in enumerate(STARTS):
-            packed = jnp.zeros((8, 128), f32)
-            for q in range(4):
-                for j in range(4):
-                    value = (na if j < 2 else nb)[j % 2, pl.ds((4 * g + q) * ND + start, 8), :]
-                    at = 32 * q + 8 * j
-                    packed = jnp.where((lane >= at) & (lane < at + 8), roll(value, at + 4), packed)
-            edges[g, pl.ds(8 * b, 8), :] = packed
-        return carry
-
-    lax.fori_loop(0, GROUPS, group, 0)
+    for b, start in enumerate(STARTS):
+        packed = None
+        for q in reversed(range(4)):
+            for j in reversed(range(4)):
+                value = (na if j < 2 else nb)[j % 2, pl.ds((4 * g + q) * ND + start, 8), :]
+                at = 32 * q + 8 * j
+                value = roll(value, at + 4)
+                packed = value if packed is None else jnp.where(lane < at + 8, value, packed)
+        edges[g, pl.ds(8 * b, 8), :] = packed
 
 
 SHIFTS = (0, 2, 4, -2)
@@ -217,7 +223,7 @@
 
 def faces(x, mask, axis):
     ahead = roll(x, -1, axis)
-    value = (9.0 * (x + ahead) - roll(x, 1, axis) - roll(x, -2, axis)) * (1.5 / 16.0)
+    value = (9.0 * (x + ahead) - roll(x, 1, axis) - roll(x, -2, axis)) * (0.5 / 16.0)
     return value * (mask * roll(mask, -1, axis))
 
 
@@ -353,24 +359,28 @@
 
 
 def through_east(value, speed):
-    third = 1.0 / 3.0
-    return flux(speed, value - roll(value, 1) * third, roll(value, -1) - roll(value, -2) * third)
-
-
-def step_kernel(high, make_fix, pack, last, halo, na, nb, *refs):
+    triple = 3.0 * value
+    return flux(speed, triple - roll(value, 1), roll(triple, -1) - roll(value, -2))
+
+
+def step_kernel(high, make_fix, pack, last, again, halo, na, nb, *refs):
     refs = list(refs)
     take = lambda n: [refs.pop(0) for _ in range(n)]
     if make_fix:
         edges, left_in, right_in = take(3)
     else:
         (fix,) = take(1)
-    cgx, cgy, tx, ty, ux, vy, water, edge_cg, edge_u, cosine, sine = take(11)
+    cgx, cgy, tx, ty, ux, vy, water, edge_cg, edge_u, cosine, sine, stencil = take(12)
     other = take(1)[0] if pack or last else None
+    if again:
+        east_speed, north_speed, turn_speed = take(3)
     out = take(1)[0]
     if make_fix:
         (fix,) = take(1)
     if pack:
         out_edges, to_east, to_west = take(3)
+    if not again:
+        east_speed, north_speed, turn_speed = take(3)
     edge_halo, edge_flux, east, moved, turn, swirl, buffer, done = refs
     flip = parity()
     lane = lanes()
@@ -388,14 +398,22 @@
         return carry
 
     def x_group(g, carry):
-        for q in range(4):
+        places = [(q, start, j) for q in range(4) for start in STARTS for j in range(2)]
+        value = jnp.concatenate([own[j, pl.ds((4 * g + q) * ND + start, 8), :] for q, start, j in places], 0)
+        upper = value.astype(bf16)
+        lower = (value - upper.astype(f32)).astype(bf16)
+        sides = dot(jnp.concatenate([upper, lower], 1), stencil[...])
+        for r, (q, start, j) in enumerate(places):
             f = 4 * g + q
-            for start in STARTS:
-                here = pl.ds(f * ND + start, 8)
+            here = pl.ds(f * ND + start, 8)
+            if again:
+                speed = east_speed[j, here, :]
+            else:
                 c = cosine[pl.ds(start, 8), :]
-                for j in range(2):
-                    speed = c * cgx[f, pl.ds(first + j, 1), :] + ux[pl.ds(first + j, 1), :]
-                    east[j, here, :] = through_east(own[j, here, :], speed)
+                speed = c * cgx[f, pl.ds(first + j, 1), :] + ux[pl.ds(first + j, 1), :]
+                east_speed[j, here, :] = speed
+            both = sides[8 * r : 8 * r + 8]
+            east[j, here, :] = flux(speed, both[:, :128], both[:, 128:])
         return carry
 
     def fix_group(g, carry):
@@ -424,24 +442,36 @@
                 value = value + [halo[1, here, :], halo[0, here, :]]
             else:
                 value = [halo[1, here, :], halo[0, here, :]] + value
-            third = [v * (1.0 / 3.0) for v in value]
+            triple = [3.0 * v for v in value]
             across = []
             for k in range(3):
-                speed = s * cgy[f, pl.ds(first + k, 1), :] + vy[pl.ds(first + k, 1), :]
-                across.append(flux(speed, value[k + 1] - third[k], value[k + 2] - third[k + 3]))
+                if again:
+                    speed = north_speed[k, here, :]
+                else:
+                    speed = s * cgy[f, pl.ds(first + k, 1), :] + vy[pl.ds(first + k, 1), :]
+                    north_speed[k, here, :] = speed
+                across.append(flux(speed, triple[k + 1] - value[k], triple[k + 2] - value[k + 3]))
             edge = fix[g, pl.ds(8 * b, 8), :]
             for j in range(2):
                 row = first + j
                 through = east[j, here, :]
                 change = jnp.where(at_edge, roll(edge, -(32 * q + 8 * row + 4)), through - roll(through, 1))
                 moved[q, j, pl.ds(8 + start, 8), :] = value[j + 2] - change - (across[j + 1] - across[j])
+                if again:
+                    continue
                 half = s * tx[f, pl.ds(row, 1), :] - c * ty[f, pl.ds(row, 1), :]
                 turn[q, j, pl.ds(8 + start, 8), :] = jnp.clip(half, -0.5 * refraction_limit, 0.5 * refraction_limit)
         for j in range(2):
             moved[q, j, pl.ds(8 + ND, 1), :] = moved[q, j, pl.ds(8, 1), :]
-            turn[q, j, pl.ds(8 + ND, 1), :] = turn[q, j, pl.ds(8, 1), :]
+            if not again:
+                turn[q, j, pl.ds(8 + ND, 1), :] = turn[q, j, pl.ds(8, 1), :]
             for start in STARTS:
-                speed = turn[q, j, pl.ds(8 + start, 8), :] + turn[q, j, pl.ds(9 + start, 8), :]
+                here = pl.ds((4 * g + q) * ND + start, 8)
+                if again:
+                    speed = turn_speed[j, here, :]
+                else:
+                    speed = turn[q, j, pl.ds(8 + start, 8), :] + turn[q, j, pl.ds(9 + start, 8), :]
+                    turn_speed[j, here, :] = speed
                 swirl[q, j, pl.ds(8 + start, 8), :] = flux(
                     speed, moved[q, j, pl.ds(8 + start, 8), :], moved[q, j, pl.ds(9 + start, 8), :]
                 )
@@ -474,6 +504,8 @@
         if last:
             result(g).start()
         x_group(jnp.minimum(g + 1, GROUPS - 1), 0)
+        if pack:
+            pack_group(other, out, out_edges, jnp.maximum(g - 1, 0))
         return carry
 
     lax.fori_loop(0, GROUPS, group, 0)
@@ -481,7 +513,7 @@
         for g in range(GROUPS):
             result(g).wait()
     if pack:
-        pack_planes(other, out, out_edges)
+        pack_group(other, out, out_edges, GROUPS - 1)
         pack_sends(out_edges, to_east, to_west)
 
 
@@ -505,13 +537,15 @@
 SENDS = shape(3, 48, 128)
 
 
-def step(high, make_fix, pack, last, *operands):
+def step(high, make_fix, pack, last, again, *operands):
     out = [shape(4 * BINS, 128) if last else PLANE]
     specs = {}
     if make_fix:
         out.append(shape(GROUPS, 40, 128))
     if pack:
         out += [EDGES, SENDS, SENDS]
+    if not again:
+        out += [shape(2, BINS, 128), shape(3, BINS, 128), shape(2, BINS, 128)]
     if last:
         specs["out_specs"] = [pl.BlockSpec(memory_space=pltpu.MemorySpace.HBM)]
     scratch = [
@@ -524,7 +558,7 @@
         pltpu.VMEM((4 * BINS, 128) if last else (8, 128), f32),
         pltpu.SemaphoreType.DMA((GROUPS,)),
     ]
-    return call(functools.partial(step_kernel, high, make_fix, pack, last), out, scratch, 8, **specs)(*operands)
+    return call(functools.partial(step_kernel, high, make_fix, pack, last, again), out, scratch, 8, **specs)(*operands)
 
 
 Z_PAIRS = [p for z in range(3) for p in ((2 * z + 1, 2 * z + 2), (2 * z + 2, 2 * z + 1))]
@@ -571,14 +605,16 @@
     speeds = call(
         fields_kernel, (per_frequency,) * 4 + (shape(8, 128),) * 3 + (shape(2, 16, 128), shape(2, 8, 128)), limit=12
     )(arrived, piece_count, sea_mask, chip_in, z_in, left_in, right_in, SIGMA_ROWS, SIGMA_PACKED)
-    common = (*speeds, COSINE, SINE)
-    new_a, fix = step(False, True, False, False, z_in, na, nb, edges, left_in, right_in, *common)
+    common = (*speeds, COSINE, SINE, STENCIL)
+    new_a, fix, *low_speeds = step(False, True, False, False, False, z_in, na, nb, edges, left_in, right_in, *common)
     z_in = swap_z(new_a)
-    new_b, edges, to_east, to_west = step(True, False, True, False, chip_in, na, nb, fix, *common, new_a)
+    new_b, edges, to_east, to_west, *high_speeds = step(True, False, True, False, False, chip_in, na, nb, fix, *common, new_a)
     chip_in = swap_chip(new_b)
     left_in, right_in = swap_x(to_east, to_west)
-    end_b, fix = step(True, True, False, False, chip_in, new_a, new_b, edges, left_in, right_in, *common)
-    (out,) = step(False, False, False, True, z_in, new_a, new_b, fix, *common, end_b)
+    end_b, fix = step(
+        True, True, False, False, True, chip_in, new_a, new_b, edges, left_in, right_in, *common, *high_speeds
+    )
+    (out,) = step(False, False, False, True, True, z_in, new_a, new_b, fix, *common, end_b, *low_speeds)
     return out.reshape(spectra.shape)
 
 

time: 70 us -> 68.3 us (0.976)
  Pallas kernels: 28 us -> 25.3 us
  waiting for transfers between devices: 6.56 us -> 7.48 us
    pallas_call x4, Pallas kernels: 20.1 us -> 17.4 us  [step(): call(functools.partial(step_kernel, high, make_fix, pack, last, again), o...]
    ppermute x2, waiting for transfers between devices: 4.81 us -> 5.73 us  [swap_z(): return lax.ppermute(rows, 'ty', Z_PAIRS)]
  transfers between devices with their start and end apart: 8 -> 8, of which waited for: 2 -> 2; matrix products, arithmetic and copies ran while one was open for 0% -> 0% of each run, Pallas kernels for 8% -> 7%
where the time goes in v5:
time: 68.3 us; the launch traced here: 68 us
  Pallas kernels  25.3 us (37%)
  starting transfers between devices  18.4 us (27%)
  blocking collectives  16.6 us (24%)
  waiting for transfers between devices  7.48 us (11%)
    pallas_call x4, Pallas kernels, step(): call(functools.partial(step_kernel, high, make_fix, pack, last, again), o...  17.4 us
    all_to_all x1, blocking collectives, on_device(): lax.all_to_all(pieces, ('ty', 'tx'), split_axis=0, concat_axis=0, tiled=T...  16.6 us
    ppermute x2, starting transfers between devices, swap_x(): lax.ppermute(to_west, 'tx', west)  8.18 us
    ppermute x2, starting transfers between devices, swap_z(): return lax.ppermute(rows, 'ty', Z_PAIRS)  7.28 us
    ppermute x2, waiting for transfers between devices, swap_z(): return lax.ppermute(rows, 'ty', Z_PAIRS)  5.73 us
    pallas_call x1, Pallas kernels, on_device(): call(prepare_kernel, (PLANE, PLANE, EDGES, SENDS, SENDS, shape(128, 128))...  5.44 us
    pallas_call x1, Pallas kernels, on_device(): call(fields_kernel, (per_frequency,) * 4 + (shape(8, 128),) * 3 + (shape(...  2.47 us
    ppermute x2, starting transfers between devices, swap_x(): lax.ppermute(to_east, 'tx', east)  1.75 us
  transfers between devices with their start and end apart: 8, of which 2 were waited for; matrix products, arithmetic and copies ran while one was open for 0% of the time, Pallas kernels for 7%

profile of v5, /device:TPU:1, one launch (start us, length us, event | category | flops | bytes accessed | tf_op | source)
XLA Modules:
  0.0 68.0 jit_solution(3201093344165629154)
XLA Ops:
  0.0 5.4 %shard_map.118 = (f32[2,1304,128]{2,1,0:T(8,128)}, f32[2,1304,128]{2,1,0:T(8,128)}, f32[9,40,128]{2,1,0:T(8,128)}, f32[3,48,128]{2,1,0:T(8,128)}, f32[3,48,128]{2,1,0:T(8,128)}, /*index=5*/f32[128,128]{1,0:T(8,128)}) custom-call(f32[5184,128]{1,0:T(8,128)} %bitcast.8, s32[4,128]{1,0:T(4,128)} %sea.3, f32[2,1024]{1,0:T(2,128)} %currents.1, ...), custom_call_target="tpu_custom_call" | custom-call | flops 2000000 | bytes 4000000 | tf_op jit(solution)/shard_map/pallas_call | solution.py:585
  5.5 4.9 %collective-permute-start = (f32[2,1304,128]{2,1,0:T(8,128)}, f32[2,1304,128]{2,1,0:T(8,128)S(1)}, u32[]{:S(2)}, u32[]{:S(2)}) collective-permute-start(f32[2,1304,128]{2,1,0:T(8,128)} %get-tuple-element.34.na), channel_id=1, source_target_pairs={{16,32},{32,16},{48,64},{64,48},{80,96},{96,80},{17,33},{33,17},{4... | collective-permute-start | bytes 4005896 | tf_op jit(solution)/shard_map/ppermute | solution.py:569
  10.4 0.1 collective-permute-start.3
  10.5 1.4 %collective-permute-start.1 = (f32[3,48,128]{2,1,0:T(8,128)}, f32[3,48,128]{2,1,0:T(8,128)S(1)}, u32[]{:S(2)}, u32[]{:S(2)}) collective-permute-start(f32[3,48,128]{2,1,0:T(8,128)} %get-tuple-element.37), channel_id=1, source_target_pairs={{0,1},{1,2},{2,3},{3,4},{4,5},{5,6},{6,7},{7,8},{8,9},{9,10},{10,1... | collective-permute-start | bytes 221192 | tf_op jit(solution)/shard_map/ppermute | solution.py:579
  11.9 3.7 %collective-permute-start.2 = (f32[3,48,128]{2,1,0:T(8,128)}, f32[3,48,128]{2,1,0:T(8,128)S(1)}, u32[]{:S(2)}, u32[]{:S(2)}) collective-permute-start(f32[3,48,128]{2,1,0:T(8,128)} %get-tuple-element.38), channel_id=1, source_target_pairs={{1,0},{2,1},{3,2},{4,3},{5,4},{6,5},{7,6},{8,7},{9,8},{10,9},{11,1... | collective-permute-start | bytes 221192 | tf_op jit(solution)/shard_map/ppermute | solution.py:579
  15.6 16.6 %all_to_all.11 = f32[128,1,128]{2,1,0:T(1,128)S(1)} all-to-all(f32[128,1,128]{2,1,0:T(1,128)} %bitcast.9), channel_id=1, replica_groups=mesh['ty'=8,'tx'=16] {'ty','tx'}, dimensions={0} | all-to-all | bytes 131072 | tf_op jit(solution)/shard_map/all_to_all | solution.py:603
  32.2 0.0 collective-permute-done.1.left_in.refs_1_
  32.2 0.0 collective-permute-done.2.right_in.refs_2_
  32.2 0.0 collective-permute-done.z_in.halo
  32.2 0.0 copy-start
  32.2 0.0 copy-start.2
  32.3 0.0 copy-start.3
  32.3 0.0 copy-start.4
  32.3 2.5 %shard_map.119 = (f32[36,8,128]{2,1,0:T(8,128)S(1)}, f32[36,8,128]{2,1,0:T(8,128)S(1)}, f32[36,8,128]{2,1,0:T(8,128)S(1)}, f32[36,8,128]{2,1,0:T(8,128)S(1)}, f3...) custom-call(f32[128,128]{1,0:T(8,128)S(1)} %bitcast.7, ...), custom_call_target="tpu_custom_call" | custom-call | flops 2000000 | bytes 4000000 | tf_op jit(solution)/shard_map/pallas_call | solution.py:605
  34.8 5.1 %shard_map.120 = (f32[2,1304,128]{2,1,0:T(8,128)S(1)}, f32[9,40,128]{2,1,0:T(8,128)S(1)}, f32[2,1296,128]{2,1,0:T(8,128)S(1)}, f32[3,1296,128]{2,1,0:T(8,128)S(1)}, f32[2,1296,128]{2,1,0:T(8,128)S(1)}) custom-call(f32[2,1304,128]{2,1,0:T(8,128)S(1)} %collective-permute-done.z_in.halo, f32[2,1304,128]{2,1,0:T(8,128)S(1)} %copy-done, ...), custom_call_target="tpu_custom_call" | custom-call | flops 2000000 | bytes 4000000 | tf_op jit(solution)/shard_map/pallas_call | solution.py:561
  39.9 4.4 %shard_map.121 = (f32[2,1304,128]{2,1,0:T(8,128)S(1)}, f32[9,40,128]{2,1,0:T(8,128)S(1)}, f32[3,48,128]{2,1,0:T(8,128)S(1)}, f32[3,48,128]{2,1,0:T(8,128)S(1)}, ...) custom-call(f32[2,1304,128]{2,1,0:T(8,128)S(1)} %collective-permute-done.3.chip_in.halo, ...), custom_call_target="tpu_custom_call" | custom-call | flops 2000000 | bytes 4000000 | tf_op jit(solution)/shard_map/pallas_call | solution.py:561
  44.3 1.1 %collective-permute-start.5 = (f32[2,1304,128]{2,1,0:T(8,128)S(1)}, f32[2,1304,128]{2,1,0:T(8,128)S(1)}, u32[]{:S(2)}, u32[]{:S(2)}) collective-permute-start(f32[2,1304,128]{2,1,0:T(8,128)S(1)} %get-tuple-element.51.nb), channel_id=1, source_target_pairs={{0,16},{16,0},{32,48},{48,32},{64,80},{80,64},{96,112},{112,96},{1... | collective-permute-start | bytes 4005896 | tf_op jit(solution)/shard_map/ppermute | solution.py:573
  45.4 2.4 %collective-permute-start.4 = (f32[2,1304,128]{2,1,0:T(8,128)S(1)}, f32[2,1304,128]{2,1,0:T(8,128)S(1)}, u32[]{:S(2)}, u32[]{:S(2)}) collective-permute-start(f32[2,1304,128]{2,1,0:T(8,128)S(1)} %get-tuple-element.49.refs_13_.na), channel_id=1, source_target_pairs={{16,32},{32,16},{48,64},{64,48},{80,96},{96,80},{17,33},{33,17},{4... | collective-permute-start | bytes 4005896 | tf_op jit(solution)/shard_map/ppermute | solution.py:569
  47.7 0.4 collective-permute-start.6
  48.1 4.5 %collective-permute-start.7 = (f32[3,48,128]{2,1,0:T(8,128)S(1)}, f32[3,48,128]{2,1,0:T(8,128)S(1)}, u32[]{:S(2)}, u32[]{:S(2)}) collective-permute-start(f32[3,48,128]{2,1,0:T(8,128)S(1)} %get-tuple-element.54), channel_id=1, source_target_pairs={{1,0},{2,1},{3,2},{4,3},{5,4},{6,5},{7,6},{8,7},{9,8},{10,9},{11,1... | collective-permute-start | bytes 221192 | tf_op jit(solution)/shard_map/ppermute | solution.py:579
  52.6 1.7 %collective-permute-done.6.refs_1_ = f32[3,48,128]{2,1,0:T(8,128)S(1)} collective-permute-done((f32[3,48,128]{2,1,0:T(8,128)S(1)}, f32[3,48,128]{2,1,0:T(8,128)S(1)}, u32[]{:S(2)}, u32[]{:S(2)}) %collective-permute-start.6) | collective-permute-done | bytes 73760 | tf_op jit(solution)/shard_map/ppermute | solution.py:579
  54.3 4.5 %shard_map.122 = (f32[2,1304,128]{2,1,0:T(8,128)S(1)}, f32[9,40,128]{2,1,0:T(8,128)S(1)}) custom-call(f32[2,1304,128]{2,1,0:T(8,128)S(1)} %collective-permute-done.5.halo, f32[2,1304,128]{2,1,0:T(8,128)S(1)} %get-tuple-element.49.refs_13_.na, f32[2,1304,128]{2,1,0:T(8,128)S(1)} %get-tuple-element.51.nb, f32[9,40,128]{2,1,0:T(8,128)S(1)} %get-tuple-element.52.refs_0_, ...), custom_call_target="tpu_custom_call" | custom-call | flops 2000000 | bytes 4000000 | tf_op jit(solution)/shard_map/pallas_call | solution.py:561
  58.8 5.7 %collective-permute-done.4.halo = f32[2,1304,128]{2,1,0:T(8,128)S(1)} collective-permute-done((f32[2,1304,128]{2,1,0:T(8,128)S(1)}, f32[2,1304,128]{2,1,0:T(8,128)S(1)}, u32[]{:S(2)}, u32[]{:S(2)}) %collective-permute-start.4) | collective-permute-done | bytes 1335328 | tf_op jit(solution)/shard_map/ppermute | solution.py:569
  64.5 3.5 %shard_map.123 = f32[5184,128]{1,0:T(8,128)} custom-call(f32[2,1304,128]{2,1,0:T(8,128)S(1)} %collective-permute-done.4.halo, f32[2,1304,128]{2,1,0:T(8,128)S(1)} %get-tuple-element.49.refs_13_.na, f32[2,1304,128]{2,1,0:T(8,128)S(1)} %get-tuple-element.51.nb, f32[9,40,128]{2,1,0:T(8,128)S(1)} %get-tuple-element.58.refs_0_, ...), custom_call_target="tpu_custom_call" | custom-call | flops 2000000 | bytes 4000000 | tf_op jit(solution)/shard_map/pallas_call | solution.py:561
  (19 shorter events, 0.0 us)
Async XLA Ops:
  0.0 32.2 %copy-start.5 = (s32[128,128]{1,0:T(8,128)S(1)}, s32[128,128]{1,0:T(8,128)}, u32[]{:S(2)}) copy-start(s32[128,128]{1,0:T(8,128)} %count.3) | copy-start | bytes 196612
  0.0 32.2 %copy-start.7 = (f32[36,128]{1,0:T(8,128)S(1)}, f32[36,128]{1,0:T(8,128)}, u32[]{:S(2)}) copy-start(f32[36,128]{1,0:T(8,128)} %constant.10.clone.sigma_rows) | copy-start | bytes 55300
  0.0 32.2 %copy-start.8 = (f32[16,128]{1,0:T(8,128)S(1)}, f32[16,128]{1,0:T(8,128)}, u32[]{:S(2)}) copy-start(f32[16,128]{1,0:T(8,128)} %constant.11.clone.sigma_packed) | copy-start | bytes 24580
  0.0 32.2 %copy-start.9 = (s32[4,128]{1,0:T(4,128)S(1)}, s32[4,128]{1,0:T(4,128)}, u32[]{:S(2)}) copy-start(s32[4,128]{1,0:T(4,128)} %sea.3) | copy-start | bytes 6148
  5.5 26.7 %collective-permute-start = (f32[2,1304,128]{2,1,0:T(8,128)}, f32[2,1304,128]{2,1,0:T(8,128)S(1)}, u32[]{:S(2)}, u32[]{:S(2)}) collective-permute-start(f32[2,1304,128]{2,1,0:T(8,128)} %get-tuple-element.34.na), channel_id=1, source_target_pairs={{16,32},{32,16},{48,64},{64,48},{80,96},{96,80},{17,33},{33,17},{4... | collective-permute-start | bytes 4005896 | tf_op jit(solution)/shard_map/ppermute | solution.py:569
  10.4 21.8 %collective-permute-start.3 = (f32[2,1304,128]{2,1,0:T(8,128)}, f32[2,1304,128]{2,1,0:T(8,128)S(1)}, u32[]{:S(2)}, u32[]{:S(2)}) collective-permute-start(f32[2,1304,128]{2,1,0:T(8,128)} %get-tuple-element.35.nb), channel_id=1, source_target_pairs={{0,16},{16,0},{32,48},{48,32},{64,80},{80,64},{96,112},{112,96},{1... | collective-permute-start | bytes 4005896 | tf_op jit(solution)/shard_map/ppermute | solution.py:573
  10.5 21.7 %collective-permute-start.1 = (f32[3,48,128]{2,1,0:T(8,128)}, f32[3,48,128]{2,1,0:T(8,128)S(1)}, u32[]{:S(2)}, u32[]{:S(2)}) collective-permute-start(f32[3,48,128]{2,1,0:T(8,128)} %get-tuple-element.37), channel_id=1, source_target_pairs={{0,1},{1,2},{2,3},{3,4},{4,5},{5,6},{6,7},{7,8},{8,9},{9,10},{10,1... | collective-permute-start | bytes 221192 | tf_op jit(solution)/shard_map/ppermute | solution.py:579
  11.9 20.3 %collective-permute-start.2 = (f32[3,48,128]{2,1,0:T(8,128)}, f32[3,48,128]{2,1,0:T(8,128)S(1)}, u32[]{:S(2)}, u32[]{:S(2)}) collective-permute-start(f32[3,48,128]{2,1,0:T(8,128)} %get-tuple-element.38), channel_id=1, source_target_pairs={{1,0},{2,1},{3,2},{4,3},{5,4},{6,5},{7,6},{8,7},{9,8},{10,9},{11,1... | collective-permute-start | bytes 221192 | tf_op jit(solution)/shard_map/ppermute | solution.py:579
  15.6 19.2 %copy-start.6 = (f32[9,40,128]{2,1,0:T(8,128)S(1)}, f32[9,40,128]{2,1,0:T(8,128)}, u32[]{:S(2)}) copy-start(f32[9,40,128]{2,1,0:T(8,128)} %get-tuple-element.36.refs_0_) | copy-start | bytes 552964
  32.2 2.5 %copy-start = (f32[2,1304,128]{2,1,0:T(8,128)S(1)}, f32[2,1304,128]{2,1,0:T(8,128)}, u32[]{:S(2)}) copy-start(f32[2,1304,128]{2,1,0:T(8,128)} %get-tuple-element.34.na) | copy-start | bytes 4005892
  32.2 2.5 %copy-start.1 = (f32[2,1304,128]{2,1,0:T(8,128)S(1)}, f32[2,1304,128]{2,1,0:T(8,128)}, u32[]{:S(2)}) copy-start(f32[2,1304,128]{2,1,0:T(8,128)} %get-tuple-element.35.nb) | copy-start | bytes 4005892
  32.2 2.5 %copy-start.2 = (bf16[256,256]{1,0:T(8,128)(2,1)S(1)}, bf16[256,256]{1,0:T(8,128)(2,1)}, u32[]{:S(2)}) copy-start(bf16[256,256]{1,0:T(8,128)(2,1)} %constant.14.clone.refs_14_.refs_12_) | copy-start | bytes 393220
  32.3 2.5 %copy-start.3 = (f32[48,128]{1,0:T(8,128)S(1)}, f32[48,128]{1,0:T(8,128)}, u32[]{:S(2)}) copy-start(f32[48,128]{1,0:T(8,128)} %constant.12.clone.refs_12_.refs_10_) | copy-start | bytes 73732
  32.3 2.5 %copy-start.4 = (f32[48,128]{1,0:T(8,128)S(1)}, f32[48,128]{1,0:T(8,128)}, u32[]{:S(2)}) copy-start(f32[48,128]{1,0:T(8,128)} %constant.13.clone.refs_13_.refs_11_) | copy-start | bytes 73732
  44.3 10.0 %collective-permute-start.5 = (f32[2,1304,128]{2,1,0:T(8,128)S(1)}, f32[2,1304,128]{2,1,0:T(8,128)S(1)}, u32[]{:S(2)}, u32[]{:S(2)}) collective-permute-start(f32[2,1304,128]{2,1,0:T(8,128)S(1)} %get-tuple-element.51.nb), channel_id=1, source_target_pairs={{0,16},{16,0},{32,48},{48,32},{64,80},{80,64},{96,112},{112,96},{1... | collective-permute-start | bytes 4005896 | tf_op jit(solution)/shard_map/ppermute | solution.py:573
  45.4 19.2 %collective-permute-start.4 = (f32[2,1304,128]{2,1,0:T(8,128)S(1)}, f32[2,1304,128]{2,1,0:T(8,128)S(1)}, u32[]{:S(2)}, u32[]{:S(2)}) collective-permute-start(f32[2,1304,128]{2,1,0:T(8,128)S(1)} %get-tuple-element.49.refs_13_.na), channel_id=1, source_target_pairs={{16,32},{32,16},{48,64},{64,48},{80,96},{96,80},{17,33},{33,17},{4... | collective-permute-start | bytes 4005896 | tf_op jit(solution)/shard_map/ppermute | solution.py:569
  47.7 6.6 %collective-permute-start.6 = (f32[3,48,128]{2,1,0:T(8,128)S(1)}, f32[3,48,128]{2,1,0:T(8,128)S(1)}, u32[]{:S(2)}, u32[]{:S(2)}) collective-permute-start(f32[3,48,128]{2,1,0:T(8,128)S(1)} %get-tuple-element.53), channel_id=1, source_target_pairs={{0,1},{1,2},{2,3},{3,4},{4,5},{5,6},{6,7},{7,8},{8,9},{9,10},{10,1... | collective-permute-start | bytes 221192 | tf_op jit(solution)/shard_map/ppermute | solution.py:579
  48.1 6.2 %collective-permute-start.7 = (f32[3,48,128]{2,1,0:T(8,128)S(1)}, f32[3,48,128]{2,1,0:T(8,128)S(1)}, u32[]{:S(2)}, u32[]{:S(2)}) collective-permute-start(f32[3,48,128]{2,1,0:T(8,128)S(1)} %get-tuple-element.54), channel_id=1, source_target_pairs={{1,0},{2,1},{3,2},{4,3},{5,4},{6,5},{7,6},{8,7},{9,8},{10,9},{11,1... | collective-permute-start | bytes 221192 | tf_op jit(solution)/shard_map/ppermute | solution.py:579

commit v6 on v5

--- a/solution.py
+++ b/solution.py
@@ -335,7 +335,7 @@
         ty[f] = turning * turn_y
         return carry
 
-    lax.fori_loop(0, NF, one, 0, unroll=4)
+    lax.fori_loop(0, NF, one, 0, unroll=12)
 
     low = lanes() % 8 < 4
     own_mask_edge = pack_edges(own_mask)
@@ -425,10 +425,10 @@
 
     if make_fix:
         unpack_sends(edges, left_in, right_in, edge_halo)
-        lax.fori_loop(0, GROUPS, edge_group, 0)
+        lax.fori_loop(0, GROUPS, edge_group, 0, unroll=3)
     x_group(0, 0)
     if make_fix:
-        lax.fori_loop(0, GROUPS, fix_group, 0)
+        lax.fori_loop(0, GROUPS, fix_group, 0, unroll=9)
     at_edge = (lane < 2) | (lane >= 126)
 
     def one(g, q):
@@ -555,7 +555,7 @@
         pltpu.VMEM((4, 2, 56, 128), f32),
         pltpu.VMEM((4, 2, 56, 128), f32),
         pltpu.VMEM((4, 2, 56, 128), f32),
-        pltpu.VMEM((4 * BINS, 128) if last else (8, 128), f32),
+        pltpu.VMEM((4 * BINS + 32, 128) if last else (8, 128), f32),
         pltpu.SemaphoreType.DMA((GROUPS,)),
     ]
     return call(functools.partial(step_kernel, high, make_fix, pack, last, again), out, scratch, 8, **specs)(*operands)
@@ -587,7 +587,7 @@
         (PLANE, PLANE, EDGES, SENDS, SENDS, shape(128, 128)),
         [
             pltpu.VMEM((128, 128), f32),
-            pltpu.VMEM((4 * BINS, 128), f32),
+            pltpu.VMEM((4 * BINS + 32, 128), f32),
             pltpu.VMEM(PLANE.shape, f32),
             pltpu.VMEM(PLANE.shape, f32),
             pltpu.SemaphoreType.DMA((GROUPS,)),

time: 68.3 us -> 66.4 us (0.972)
  Pallas kernels: 25.3 us -> 22.3 us
  waiting for transfers between devices: 7.48 us -> 8.66 us
    pallas_call x4, Pallas kernels: 17.4 us -> 15.1 us  [step(): call(functools.partial(step_kernel, high, make_fix, pack, last, again), o...]
    ppermute x2, waiting for transfers between devices: 5.73 us -> 6.91 us  [swap_z(): return lax.ppermute(rows, 'ty', Z_PAIRS)]
  transfers between devices with their start and end apart: 8 -> 8, of which waited for: 2 -> 2; matrix products, arithmetic and copies ran while one was open for 0% -> 0% of each run, Pallas kernels for 7% -> 5%
where the time goes in v6:
time: 66.4 us; the launch traced here: 66.2 us
  Pallas kernels  22.3 us (34%)
  starting transfers between devices  18.4 us (28%)
  blocking collectives  16.6 us (25%)
  waiting for transfers between devices  8.66 us (13%)
    all_to_all x1, blocking collectives, on_device(): lax.all_to_all(pieces, ('ty', 'tx'), split_axis=0, concat_axis=0, tiled=T...  16.6 us
    pallas_call x4, Pallas kernels, step(): call(functools.partial(step_kernel, high, make_fix, pack, last, again), o...  15.1 us
    ppermute x2, starting transfers between devices, swap_x(): lax.ppermute(to_west, 'tx', west)  8.17 us
    ppermute x2, starting transfers between devices, swap_z(): return lax.ppermute(rows, 'ty', Z_PAIRS)  7.28 us
    ppermute x2, waiting for transfers between devices, swap_z(): return lax.ppermute(rows, 'ty', Z_PAIRS)  6.91 us
    pallas_call x1, Pallas kernels, on_device(): call(prepare_kernel, (PLANE, PLANE, EDGES, SENDS, SENDS, shape(128, 128))...  5.44 us
    pallas_call x1, Pallas kernels, on_device(): call(fields_kernel, (per_frequency,) * 4 + (shape(8, 128),) * 3 + (shape(...  1.81 us
    ppermute x2, starting transfers between devices, swap_x(): lax.ppermute(to_east, 'tx', east)  1.76 us
  transfers between devices with their start and end apart: 8, of which 2 were waited for; matrix products, arithmetic and copies ran while one was open for 0% of the time, Pallas kernels for 5%

profile of v6, /device:TPU:1, one launch (start us, length us, event | category | flops | bytes accessed | tf_op | source)
XLA Modules:
  0.0 66.2 jit_solution(13081678702172805038)
XLA Ops:
  0.0 5.4 %shard_map.118 = (f32[2,1304,128]{2,1,0:T(8,128)}, f32[2,1304,128]{2,1,0:T(8,128)}, f32[9,40,128]{2,1,0:T(8,128)}, f32[3,48,128]{2,1,0:T(8,128)}, f32[3,48,128]{2,1,0:T(8,128)}, /*index=5*/f32[128,128]{1,0:T(8,128)}) custom-call(f32[5184,128]{1,0:T(8,128)} %bitcast.8, s32[4,128]{1,0:T(4,128)} %sea.3, f32[2,1024]{1,0:T(2,128)} %currents.1, ...), custom_call_target="tpu_custom_call" | custom-call | flops 2000000 | bytes 4000000 | tf_op jit(solution)/shard_map/pallas_call | solution.py:585
  5.5 4.9 %collective-permute-start = (f32[2,1304,128]{2,1,0:T(8,128)}, f32[2,1304,128]{2,1,0:T(8,128)S(1)}, u32[]{:S(2)}, u32[]{:S(2)}) collective-permute-start(f32[2,1304,128]{2,1,0:T(8,128)} %get-tuple-element.34.na), channel_id=1, source_target_pairs={{16,32},{32,16},{48,64},{64,48},{80,96},{96,80},{17,33},{33,17},{4... | collective-permute-start | bytes 4005896 | tf_op jit(solution)/shard_map/ppermute | solution.py:569
  10.4 0.1 collective-permute-start.3
  10.5 1.4 %collective-permute-start.1 = (f32[3,48,128]{2,1,0:T(8,128)}, f32[3,48,128]{2,1,0:T(8,128)S(1)}, u32[]{:S(2)}, u32[]{:S(2)}) collective-permute-start(f32[3,48,128]{2,1,0:T(8,128)} %get-tuple-element.37), channel_id=1, source_target_pairs={{0,1},{1,2},{2,3},{3,4},{4,5},{5,6},{6,7},{7,8},{8,9},{9,10},{10,1... | collective-permute-start | bytes 221192 | tf_op jit(solution)/shard_map/ppermute | solution.py:579
  11.9 3.7 %collective-permute-start.2 = (f32[3,48,128]{2,1,0:T(8,128)}, f32[3,48,128]{2,1,0:T(8,128)S(1)}, u32[]{:S(2)}, u32[]{:S(2)}) collective-permute-start(f32[3,48,128]{2,1,0:T(8,128)} %get-tuple-element.38), channel_id=1, source_target_pairs={{1,0},{2,1},{3,2},{4,3},{5,4},{6,5},{7,6},{8,7},{9,8},{10,9},{11,1... | collective-permute-start | bytes 221192 | tf_op jit(solution)/shard_map/ppermute | solution.py:579
  15.6 16.6 %all_to_all.11 = f32[128,1,128]{2,1,0:T(1,128)S(1)} all-to-all(f32[128,1,128]{2,1,0:T(1,128)} %bitcast.9), channel_id=1, replica_groups=mesh['ty'=8,'tx'=16] {'ty','tx'}, dimensions={0} | all-to-all | bytes 131072 | tf_op jit(solution)/shard_map/all_to_all | solution.py:603
  32.2 0.0 collective-permute-done.1.left_in.refs_1_
  32.2 0.0 collective-permute-done.2.right_in.refs_2_
  32.2 0.0 copy-start
  32.2 0.0 copy-start.2
  32.3 0.0 copy-start.3
  32.3 0.0 copy-start.4
  32.3 1.8 %shard_map.119 = (f32[36,8,128]{2,1,0:T(8,128)S(1)}, f32[36,8,128]{2,1,0:T(8,128)S(1)}, f32[36,8,128]{2,1,0:T(8,128)S(1)}, f32[36,8,128]{2,1,0:T(8,128)S(1)}, f3...) custom-call(f32[128,128]{1,0:T(8,128)S(1)} %bitcast.7, ...), custom_call_target="tpu_custom_call" | custom-call | flops 2000000 | bytes 4000000 | tf_op jit(solution)/shard_map/pallas_call | solution.py:605
  34.2 3.9 %shard_map.120 = (f32[2,1304,128]{2,1,0:T(8,128)S(1)}, f32[9,40,128]{2,1,0:T(8,128)S(1)}, f32[2,1296,128]{2,1,0:T(8,128)S(1)}, f32[3,1296,128]{2,1,0:T(8,128)S(1)}, f32[2,1296,128]{2,1,0:T(8,128)S(1)}) custom-call(f32[2,1304,128]{2,1,0:T(8,128)S(1)} %collective-permute-done.z_in.halo, f32[2,1304,128]{2,1,0:T(8,128)S(1)} %copy-done, ...), custom_call_target="tpu_custom_call" | custom-call | flops 2000000 | bytes 4000000 | tf_op jit(solution)/shard_map/pallas_call | solution.py:561
  38.1 4.4 %shard_map.121 = (f32[2,1304,128]{2,1,0:T(8,128)S(1)}, f32[9,40,128]{2,1,0:T(8,128)S(1)}, f32[3,48,128]{2,1,0:T(8,128)S(1)}, f32[3,48,128]{2,1,0:T(8,128)S(1)}, ...) custom-call(f32[2,1304,128]{2,1,0:T(8,128)S(1)} %collective-permute-done.3.chip_in.halo, ...), custom_call_target="tpu_custom_call" | custom-call | flops 2000000 | bytes 4000000 | tf_op jit(solution)/shard_map/pallas_call | solution.py:561
  42.5 1.1 %collective-permute-start.5 = (f32[2,1304,128]{2,1,0:T(8,128)S(1)}, f32[2,1304,128]{2,1,0:T(8,128)S(1)}, u32[]{:S(2)}, u32[]{:S(2)}) collective-permute-start(f32[2,1304,128]{2,1,0:T(8,128)S(1)} %get-tuple-element.51.nb), channel_id=1, source_target_pairs={{0,16},{16,0},{32,48},{48,32},{64,80},{80,64},{96,112},{112,96},{1... | collective-permute-start | bytes 4005896 | tf_op jit(solution)/shard_map/ppermute | solution.py:573
  43.6 2.4 %collective-permute-start.4 = (f32[2,1304,128]{2,1,0:T(8,128)S(1)}, f32[2,1304,128]{2,1,0:T(8,128)S(1)}, u32[]{:S(2)}, u32[]{:S(2)}) collective-permute-start(f32[2,1304,128]{2,1,0:T(8,128)S(1)} %get-tuple-element.49.refs_13_.na), channel_id=1, source_target_pairs={{16,32},{32,16},{48,64},{64,48},{80,96},{96,80},{17,33},{33,17},{4... | collective-permute-start | bytes 4005896 | tf_op jit(solution)/shard_map/ppermute | solution.py:569
  45.9 0.4 collective-permute-start.6
  46.3 4.5 %collective-permute-start.7 = (f32[3,48,128]{2,1,0:T(8,128)S(1)}, f32[3,48,128]{2,1,0:T(8,128)S(1)}, u32[]{:S(2)}, u32[]{:S(2)}) collective-permute-start(f32[3,48,128]{2,1,0:T(8,128)S(1)} %get-tuple-element.54), channel_id=1, source_target_pairs={{1,0},{2,1},{3,2},{4,3},{5,4},{6,5},{7,6},{8,7},{9,8},{10,9},{11,1... | collective-permute-start | bytes 221192 | tf_op jit(solution)/shard_map/ppermute | solution.py:579
  50.8 1.7 %collective-permute-done.6.refs_1_ = f32[3,48,128]{2,1,0:T(8,128)S(1)} collective-permute-done((f32[3,48,128]{2,1,0:T(8,128)S(1)}, f32[3,48,128]{2,1,0:T(8,128)S(1)}, u32[]{:S(2)}, u32[]{:S(2)}) %collective-permute-start.6) | collective-permute-done | bytes 73760 | tf_op jit(solution)/shard_map/ppermute | solution.py:579
  52.5 0.0 collective-permute-done.5.halo
  52.5 3.3 %shard_map.122 = (f32[2,1304,128]{2,1,0:T(8,128)S(1)}, f32[9,40,128]{2,1,0:T(8,128)S(1)}) custom-call(f32[2,1304,128]{2,1,0:T(8,128)S(1)} %collective-permute-done.5.halo, f32[2,1304,128]{2,1,0:T(8,128)S(1)} %get-tuple-element.49.refs_13_.na, f32[2,1304,128]{2,1,0:T(8,128)S(1)} %get-tuple-element.51.nb, f32[9,40,128]{2,1,0:T(8,128)S(1)} %get-tuple-element.52.refs_0_, ...), custom_call_target="tpu_custom_call" | custom-call | flops 2000000 | bytes 4000000 | tf_op jit(solution)/shard_map/pallas_call | solution.py:561
  55.8 6.9 %collective-permute-done.4.halo = f32[2,1304,128]{2,1,0:T(8,128)S(1)} collective-permute-done((f32[2,1304,128]{2,1,0:T(8,128)S(1)}, f32[2,1304,128]{2,1,0:T(8,128)S(1)}, u32[]{:S(2)}, u32[]{:S(2)}) %collective-permute-start.4) | collective-permute-done | bytes 1335328 | tf_op jit(solution)/shard_map/ppermute | solution.py:569
  62.7 3.5 %shard_map.123 = f32[5184,128]{1,0:T(8,128)} custom-call(f32[2,1304,128]{2,1,0:T(8,128)S(1)} %collective-permute-done.4.halo, f32[2,1304,128]{2,1,0:T(8,128)S(1)} %get-tuple-element.49.refs_13_.na, f32[2,1304,128]{2,1,0:T(8,128)S(1)} %get-tuple-element.51.nb, f32[9,40,128]{2,1,0:T(8,128)S(1)} %get-tuple-element.58.refs_0_, ...), custom_call_target="tpu_custom_call" | custom-call | flops 2000000 | bytes 4000000 | tf_op jit(solution)/shard_map/pallas_call | solution.py:561
  (19 shorter events, 0.0 us)
Async XLA Ops:
  0.0 32.2 %copy-start.5 = (s32[128,128]{1,0:T(8,128)S(1)}, s32[128,128]{1,0:T(8,128)}, u32[]{:S(2)}) copy-start(s32[128,128]{1,0:T(8,128)} %count.3) | copy-start | bytes 196612
  0.0 32.2 %copy-start.7 = (f32[36,128]{1,0:T(8,128)S(1)}, f32[36,128]{1,0:T(8,128)}, u32[]{:S(2)}) copy-start(f32[36,128]{1,0:T(8,128)} %constant.10.clone.sigma_rows) | copy-start | bytes 55300
  0.0 32.2 %copy-start.8 = (f32[16,128]{1,0:T(8,128)S(1)}, f32[16,128]{1,0:T(8,128)}, u32[]{:S(2)}) copy-start(f32[16,128]{1,0:T(8,128)} %constant.11.clone.sigma_packed) | copy-start | bytes 24580
  0.0 32.2 %copy-start.9 = (s32[4,128]{1,0:T(4,128)S(1)}, s32[4,128]{1,0:T(4,128)}, u32[]{:S(2)}) copy-start(s32[4,128]{1,0:T(4,128)} %sea.3) | copy-start | bytes 6148
  5.5 26.7 %collective-permute-start = (f32[2,1304,128]{2,1,0:T(8,128)}, f32[2,1304,128]{2,1,0:T(8,128)S(1)}, u32[]{:S(2)}, u32[]{:S(2)}) collective-permute-start(f32[2,1304,128]{2,1,0:T(8,128)} %get-tuple-element.34.na), channel_id=1, source_target_pairs={{16,32},{32,16},{48,64},{64,48},{80,96},{96,80},{17,33},{33,17},{4... | collective-permute-start | bytes 4005896 | tf_op jit(solution)/shard_map/ppermute | solution.py:569
  10.4 21.8 %collective-permute-start.3 = (f32[2,1304,128]{2,1,0:T(8,128)}, f32[2,1304,128]{2,1,0:T(8,128)S(1)}, u32[]{:S(2)}, u32[]{:S(2)}) collective-permute-start(f32[2,1304,128]{2,1,0:T(8,128)} %get-tuple-element.35.nb), channel_id=1, source_target_pairs={{0,16},{16,0},{32,48},{48,32},{64,80},{80,64},{96,112},{112,96},{1... | collective-permute-start | bytes 4005896 | tf_op jit(solution)/shard_map/ppermute | solution.py:573
  10.5 21.7 %collective-permute-start.1 = (f32[3,48,128]{2,1,0:T(8,128)}, f32[3,48,128]{2,1,0:T(8,128)S(1)}, u32[]{:S(2)}, u32[]{:S(2)}) collective-permute-start(f32[3,48,128]{2,1,0:T(8,128)} %get-tuple-element.37), channel_id=1, source_target_pairs={{0,1},{1,2},{2,3},{3,4},{4,5},{5,6},{6,7},{7,8},{8,9},{9,10},{10,1... | collective-permute-start | bytes 221192 | tf_op jit(solution)/shard_map/ppermute | solution.py:579
  11.9 20.3 %collective-permute-start.2 = (f32[3,48,128]{2,1,0:T(8,128)}, f32[3,48,128]{2,1,0:T(8,128)S(1)}, u32[]{:S(2)}, u32[]{:S(2)}) collective-permute-start(f32[3,48,128]{2,1,0:T(8,128)} %get-tuple-element.38), channel_id=1, source_target_pairs={{1,0},{2,1},{3,2},{4,3},{5,4},{6,5},{7,6},{8,7},{9,8},{10,9},{11,1... | collective-permute-start | bytes 221192 | tf_op jit(solution)/shard_map/ppermute | solution.py:579
  15.6 18.5 %copy-start.6 = (f32[9,40,128]{2,1,0:T(8,128)S(1)}, f32[9,40,128]{2,1,0:T(8,128)}, u32[]{:S(2)}) copy-start(f32[9,40,128]{2,1,0:T(8,128)} %get-tuple-element.36.refs_0_) | copy-start | bytes 552964
  32.2 1.9 %copy-start = (f32[2,1304,128]{2,1,0:T(8,128)S(1)}, f32[2,1304,128]{2,1,0:T(8,128)}, u32[]{:S(2)}) copy-start(f32[2,1304,128]{2,1,0:T(8,128)} %get-tuple-element.34.na) | copy-start | bytes 4005892
  32.2 1.9 %copy-start.1 = (f32[2,1304,128]{2,1,0:T(8,128)S(1)}, f32[2,1304,128]{2,1,0:T(8,128)}, u32[]{:S(2)}) copy-start(f32[2,1304,128]{2,1,0:T(8,128)} %get-tuple-element.35.nb) | copy-start | bytes 4005892
  32.2 1.9 %copy-start.2 = (bf16[256,256]{1,0:T(8,128)(2,1)S(1)}, bf16[256,256]{1,0:T(8,128)(2,1)}, u32[]{:S(2)}) copy-start(bf16[256,256]{1,0:T(8,128)(2,1)} %constant.14.clone.refs_14_.refs_12_) | copy-start | bytes 393220
  32.3 1.9 %copy-start.3 = (f32[48,128]{1,0:T(8,128)S(1)}, f32[48,128]{1,0:T(8,128)}, u32[]{:S(2)}) copy-start(f32[48,128]{1,0:T(8,128)} %constant.12.clone.refs_12_.refs_10_) | copy-start | bytes 73732
  32.3 1.9 %copy-start.4 = (f32[48,128]{1,0:T(8,128)S(1)}, f32[48,128]{1,0:T(8,128)}, u32[]{:S(2)}) copy-start(f32[48,128]{1,0:T(8,128)} %constant.13.clone.refs_13_.refs_11_) | copy-start | bytes 73732
  42.5 10.0 %collective-permute-start.5 = (f32[2,1304,128]{2,1,0:T(8,128)S(1)}, f32[2,1304,128]{2,1,0:T(8,128)S(1)}, u32[]{:S(2)}, u32[]{:S(2)}) collective-permute-start(f32[2,1304,128]{2,1,0:T(8,128)S(1)} %get-tuple-element.51.nb), channel_id=1, source_target_pairs={{0,16},{16,0},{32,48},{48,32},{64,80},{80,64},{96,112},{112,96},{1... | collective-permute-start | bytes 4005896 | tf_op jit(solution)/shard_map/ppermute | solution.py:573
  43.6 19.2 %collective-permute-start.4 = (f32[2,1304,128]{2,1,0:T(8,128)S(1)}, f32[2,1304,128]{2,1,0:T(8,128)S(1)}, u32[]{:S(2)}, u32[]{:S(2)}) collective-permute-start(f32[2,1304,128]{2,1,0:T(8,128)S(1)} %get-tuple-element.49.refs_13_.na), channel_id=1, source_target_pairs={{16,32},{32,16},{48,64},{64,48},{80,96},{96,80},{17,33},{33,17},{4... | collective-permute-start | bytes 4005896 | tf_op jit(solution)/shard_map/ppermute | solution.py:569
  45.9 6.6 %collective-permute-start.6 = (f32[3,48,128]{2,1,0:T(8,128)S(1)}, f32[3,48,128]{2,1,0:T(8,128)S(1)}, u32[]{:S(2)}, u32[]{:S(2)}) collective-permute-start(f32[3,48,128]{2,1,0:T(8,128)S(1)} %get-tuple-element.53), channel_id=1, source_target_pairs={{0,1},{1,2},{2,3},{3,4},{4,5},{5,6},{6,7},{7,8},{8,9},{9,10},{10,1... | collective-permute-start | bytes 221192 | tf_op jit(solution)/shard_map/ppermute | solution.py:579
  46.3 6.2 %collective-permute-start.7 = (f32[3,48,128]{2,1,0:T(8,128)S(1)}, f32[3,48,128]{2,1,0:T(8,128)S(1)}, u32[]{:S(2)}, u32[]{:S(2)}) collective-permute-start(f32[3,48,128]{2,1,0:T(8,128)S(1)} %get-tuple-element.54), channel_id=1, source_target_pairs={{1,0},{2,1},{3,2},{4,3},{5,4},{6,5},{7,6},{8,7},{9,8},{10,9},{11,1... | collective-permute-start | bytes 221192 | tf_op jit(solution)/shard_map/ppermute | solution.py:579
